TPU v7x, 32 devices: a whole 2x2x4 slice. The times are simulated.
32 devices in a mesh: slab: 8 (over z, y), cross: 4 (over x, core).
Axes of the slice: x: 2, y: 2, z: 4, core: 2. Of those that a mesh axis runs over, the one named last changes fastest.
Arguments:
- a_tiles: bfloat16 [64, 7, 128, 128], P(('slab', 'cross')), may hold values from -0.1875 to 0.1875
- a_cols: int32 [64, 7], P(('slab', 'cross')), may hold values from 0 to 17, as said below
- over_tiles: bfloat16 [128, 128, 128], P(('slab', 'cross')), may hold values from -0.1875 to 0.1875
- over_rows: int32 [128], P(('slab', 'cross')), may hold values from 0 to 1
- over_cols: int32 [128], P(('slab', 'cross')), may hold values from 0 to 17
- p_tiles: bfloat16 [64, 3, 128, 128], P(('slab', 'cross')), may hold values from -0.8984375 to 0.8984375
- p_cols: int32 [64, 3], P(('slab', 'cross')), may hold values from 0 to 5, as said below
Outputs:
- coarse: float32 [2048, 1792], P(('slab', 'cross'))
Inputs may be any that keep to these rules, and one draw needn't show every extreme that they name: `a_cols`: the 7 entries of a row are different. `p_cols`: the 3 entries of a row are different.
All inputs are finite; a program needn't handle non-finite values.
Results may differ from a plain program's by a relative error of at most 0.0063.
Values may be sent and summed in bfloat16 or wider, within the bound.
No kernel may reach another device: no remote copies, remote signals or barrier semaphores. Data moves between devices by JAX's collectives and lax.ppermute only.
A program may use at most 64 MiB of HBM per device.

v0:
```python
import jax
import jax.numpy as jnp
from jax import lax
from jax.sharding import PartitionSpec as P

CB = 2


def with_halo(block, sides, width):
    for axis, dim in sides:
        count = lax.axis_size(axis)
        forward = [(i, i + 1) for i in range(count - 1)]
        backward = [(target, source) for source, target in forward]
        low = lax.ppermute(
            lax.slice_in_dim(block, block.shape[dim] - width, None, axis=dim), axis, forward
        )
        high = lax.ppermute(lax.slice_in_dim(block, 0, width, axis=dim), axis, backward)
        block = jnp.concatenate([low, block, high], axis=dim)
    return block


def from_behind(value, axis, by):
    devices = lax.axis_size(axis)
    pairs = [(i, i + by) for i in range(devices) if 0 <= i + by < devices]
    return lax.ppermute(value, axis, pairs)


def place_rows(lower, middle, upper, width):
    total = jnp.zeros((middle.shape[0], 7 * width), jnp.float32)
    total = total.at[:, 0 : 5 * width].add(lower)
    total = total.at[:, width : 6 * width].add(middle)
    total = total.at[:, 2 * width : 7 * width].add(upper)
    return total


def body(a_tiles, a_cols, over_tiles, over_rows, over_cols, p_tiles, p_cols):
    blocks = a_tiles.shape[0]
    tile_size = a_tiles.shape[-1]
    width = CB * tile_size
    wide = 3 * width
    span = blocks * tile_size
    p_picks = (p_cols[:, :, None] == jnp.arange(3 * CB, dtype=jnp.int32)[None, None, :]).astype(
        jnp.bfloat16
    )
    dense_p = jnp.einsum("nmq,nmab->naqb", p_picks, p_tiles, preferred_element_type=jnp.float32)
    dense_p = dense_p.astype(jnp.bfloat16).reshape(span, wide)
    extended = with_halo(
        dense_p.reshape(1, 1, blocks, tile_size, wide), (("slab", 0), ("cross", 1)), 1
    )
    extended = extended.reshape(9 * blocks, tile_size, wide)
    product = jnp.zeros((blocks, tile_size, 5 * width), jnp.float32)
    for k_index in range(a_cols.shape[1]):
        rows = jnp.take(extended, a_cols[:, k_index], axis=0)
        piece = jnp.einsum(
            "nab,nbq->naq", a_tiles[:, k_index], rows, preferred_element_type=jnp.float32
        )
        offsets = a_cols[:, k_index] // (3 * blocks)
        for shift_index in range(3):
            mask = (offsets == shift_index).astype(jnp.float32)[:, None, None]
            product = product.at[:, :, shift_index * width : shift_index * width + wide].add(
                mask * piece
            )
    rows = jnp.take(extended, over_cols, axis=0)
    piece = jnp.einsum("oab,obq->oaq", over_tiles, rows, preferred_element_type=jnp.float32)
    row_pick = (over_rows[:, None] == jnp.arange(blocks, dtype=jnp.int32)[None, :]).astype(
        jnp.float32
    )
    offsets = over_cols // (3 * blocks)
    for shift_index in range(3):
        select = row_pick * (offsets == shift_index).astype(jnp.float32)[:, None]
        contrib = jnp.einsum("on,oaq->naq", select, piece)
        product = product.at[:, :, shift_index * width : shift_index * width + wide].add(contrib)
    product = product.astype(jnp.bfloat16).reshape(span, 5 * width)
    partial_value = lax.dot_general(
        dense_p, product, (((0,), (0,)), ((), ())), preferred_element_type=jnp.float32
    )
    partial_value = partial_value.reshape(3, width, 5 * width)
    shares = lax.psum_scatter(partial_value, "cross", scatter_dimension=1, tiled=True)
    upper = from_behind(shares[0], "slab", -1)
    lower = from_behind(shares[2], "slab", 1)
    return place_rows(lower, shares[1], upper, width)


def solution(mesh):
    return jax.shard_map(
        body,
        mesh=mesh,
        in_specs=(
            P(("slab", "cross"), None, None, None),
            P(("slab", "cross"), None),
            P(("slab", "cross"), None, None),
            P(("slab", "cross")),
            P(("slab", "cross")),
            P(("slab", "cross"), None, None, None),
            P(("slab", "cross"), None),
        ),
        out_specs=P(("slab", "cross"), None),
        check_vma=False,
    )
```

profile of v0, /device:TPU:0, one launch (start us, length us, event | category | flops | bytes accessed | tf_op | source)
XLA Modules:
  0.0 174.3 jit_solution(13369648834327118058)
XLA Ops:
  6.5 0.9 copy-done
  7.5 1.1 convolution_convert_fusion
  8.9 1.3 collective-permute-start.1
  10.2 5.5 %collective-permute-start = (bf16[1,1,2,128,768]{3,4,2,1,0:T(8,128)(2,1)S(1)}, bf16[1,1,2,128,768]{3,4,2,1,0:T(8,128)(2,1)S(1)}, u32[]{:S(2)}, u32[]{:S(2)}) collective-permute-start(bf16[1,1,2,128,768]{3,4,2,1,0:T(8,128)(2,1)S(1)} %bitcast.146), channel_id=1, source_target_pairs={{0,4},{4,8},{8,12},{12,16},{16,20},{20,24},{24,28},{1,5},{5,9},{9,... | collective-permute-start | bytes 1179656 | tf_op jit(solution)/shard_map/ppermute | solution.py:14
  18.3 4.7 %collective-permute-done.1 = bf16[1,1,2,128,768]{3,4,2,1,0:T(8,128)(2,1)S(1)} collective-permute-done((bf16[1,1,2,128,768]{3,4,2,1,0:T(8,128)(2,1)S(1)}, bf16[1,1,2,128,768]{3,4,2,1,0:T(8,128)(2,1)S(1)}, u32[]{:S(2)}, u32[]{:S(2)}) %collective-permute-start.1) | collective-permute-done | bytes 393248 | tf_op jit(solution)/shard_map/ppermute | solution.py:17
  22.9 8.6 %collective-permute-done = bf16[1,1,2,128,768]{3,4,2,1,0:T(8,128)(2,1)S(1)} collective-permute-done((bf16[1,1,2,128,768]{3,4,2,1,0:T(8,128)(2,1)S(1)}, bf16[1,1,2,128,768]{3,4,2,1,0:T(8,128)(2,1)S(1)}, u32[]{:S(2)}, u32[]{:S(2)}) %collective-permute-start) | collective-permute-done | bytes 393248 | tf_op jit(solution)/shard_map/ppermute | solution.py:14
  31.7 1.3 collective-permute-start.3
  33.0 3.1 %collective-permute-start.2 = (bf16[3,1,2,128,768]{3,4,2,1,0:T(8,128)(2,1)S(1)}, bf16[3,1,2,128,768]{3,4,2,1,0:T(8,128)(2,1)S(1)}, u32[]{:S(2)}, u32[]{:S(2)}) collective-permute-start(bf16[3,1,2,128,768]{3,4,2,1,0:T(8,128)(2,1)S(1)} %pad_maximum_fusion.1), channel_id=1, source_target_pairs={{0,1},{1,2},{2,3},{4,5},{5,6},{6,7},{8,9},{9,10},{10,11},{12,13},{... | collective-permute-start | bytes 3538952 | tf_op jit(solution)/shard_map/ppermute | solution.py:14
  38.5 2.0 %pad_maximum_fusion = bf16[3,3,2,128,768]{3,4,2,1,0:T(8,128)(2,1)} fusion(bf16[3,1,2,128,768]{3,4,2,1,0:T(8,128)(2,1)S(1)} %collective-permute-done.3, bf16[1,1,2,128,768]{3,4,2,1,0:T(8,128)(2,1)S(1)} %collective-permute-done.1, bf16[1,1,2,128,768]{3,4,2,1,0:T(8,128)(2,1)S(1)} %bitcast.148, bf16[1,1,2,128,768]{3,4,2,1,0:T(8,128)(2,1)S(1)} %collective-permute-done, ...), kind=kLoop, calls=%fused_computation.8 | loop fusion | flops 7077888 | bytes 7077888 | tf_op jit(solution)/shard_map/concatenate | solution.py:18
  40.4 6.0 %copy.26 = bf16[3,3,2,128,768]{4,3,2,1,0:T(8,128)(2,1)} copy(bf16[3,3,2,128,768]{3,4,2,1,0:T(8,128)(2,1)} %pad_maximum_fusion) | data formatting | bytes 7077888 | tf_op jit(solution)/shard_map/concatenate | solution.py:18
  46.5 2.6 %gather_fusion.7 = bf16[2,128,768]{2,1,0:T(8,128)(2,1)S(1)} fusion(bf16[18,128,768]{2,1,0:T(8,128)(2,1)} %bitcast.135, s32[1024]{0:T(1024)S(1)} %pad_clamp_fusion.1), kind=kCustom, calls=%fused_computation.6.clone | custom fusion | bytes 786440 | tf_op jit(solution)/shard_map/jit(_take)/gather | solution.py:53
  49.0 2.6 %gather_fusion.6 = bf16[2,128,768]{2,1,0:T(8,128)(2,1)S(1)} fusion(bf16[18,128,768]{2,1,0:T(8,128)(2,1)} %bitcast.136, s32[1024]{0:T(1024)S(1)} %pad_clamp_fusion.2), kind=kCustom, calls=%fused_computation.5.clone | custom fusion | bytes 786440 | tf_op jit(solution)/shard_map/jit(_take)/gather | solution.py:53
  51.6 2.6 %gather_fusion.5 = bf16[2,128,768]{2,1,0:T(8,128)(2,1)S(1)} fusion(bf16[18,128,768]{2,1,0:T(8,128)(2,1)} %bitcast.137, s32[1024]{0:T(1024)S(1)} %pad_clamp_fusion.3), kind=kCustom, calls=%fused_computation.4.clone | custom fusion | bytes 786440 | tf_op jit(solution)/shard_map/jit(_take)/gather | solution.py:53
  54.2 3.3 %gather_fusion.4 = bf16[2,128,768]{2,1,0:T(8,128)(2,1)} fusion(bf16[18,128,768]{2,1,0:T(8,128)(2,1)} %bitcast.138, s32[1024]{0:T(1024)S(1)} %pad_clamp_fusion.4), kind=kCustom, calls=%fused_computation.3.clone | custom fusion | bytes 786440 | tf_op jit(solution)/shard_map/jit(_take)/gather | solution.py:53
  57.5 3.3 %gather_fusion.3 = bf16[2,128,768]{2,1,0:T(8,128)(2,1)} fusion(bf16[18,128,768]{2,1,0:T(8,128)(2,1)} %bitcast.139, s32[1024]{0:T(1024)S(1)} %pad_clamp_fusion.5), kind=kCustom, calls=%fused_computation.2.clone | custom fusion | bytes 786440 | tf_op jit(solution)/shard_map/jit(_take)/gather | solution.py:53
  60.9 3.3 %gather_fusion.2 = bf16[2,128,768]{2,1,0:T(8,128)(2,1)} fusion(bf16[18,128,768]{2,1,0:T(8,128)(2,1)} %bitcast.140, s32[1024]{0:T(1024)S(1)} %pad_clamp_fusion.6), kind=kCustom, calls=%fused_computation.1.clone | custom fusion | bytes 786440 | tf_op jit(solution)/shard_map/jit(_take)/gather | solution.py:53
  64.2 3.4 %gather_fusion.1 = bf16[2,128,768]{2,1,0:T(8,128)(2,1)} fusion(bf16[18,128,768]{2,1,0:T(8,128)(2,1)} %bitcast.141, s32[1024]{0:T(1024)S(1)} %pad_clamp_fusion.7), kind=kCustom, calls=%fused_computation.clone | custom fusion | bytes 786440 | tf_op jit(solution)/shard_map/jit(_take)/gather | solution.py:53
  67.5 2.6 %gather_fusion = bf16[4,128,768]{2,1,0:T(8,128)(2,1)S(1)} fusion(bf16[18,128,768]{2,1,0:T(8,128)(2,1)} %bitcast.142, s32[1024]{0:T(1024)S(1)} %pad_clamp_fusion), kind=kCustom, calls=%fused_computation.7 | custom fusion | bytes 1572880 | tf_op jit(solution)/shard_map/jit(_take)/gather | solution.py:63
  74.6 0.8 copy-done.4
  76.4 0.8 copy-done.3
  78.0 0.8 copy-done.2
  84.6 2.6 %fusion.103 = f32[3,256,1280]{2,1,0:T(8,128)} fusion(bf16[3,256,256]{2,1,0:T(8,128)(2,1)S(1)} %bitcast.150, bf16[256,1280,1]{1,0,2:T(8,128)(2,1)S(1)} %bitcast.149), kind=kOutput, calls=%fused_computation.213 | convolution fusion | flops 503316480 | bytes 4980736 | tf_op jit(solution)/shard_map/dot_general | solution.py:74
  87.2 56.9 %reduce-scatter.2.cloned.1.call-done = f32[3,64,1280]{2,1,0:T(8,128)} async-done(((f32[3,256,1280]{2,1,0:T(8,128)}), f32[3,64,1280]{2,1,0:T(8,128)}) %reduce-scatter.2.cloned.1.call-update) | async-done | bytes 983056 | tf_op jit(solution)/shard_map/reduce_scatter | solution.py:78
  144.1 1.1 slice_bitcast_fusion
  145.2 3.4 %collective-permute-start.4 = (f32[64,1280]{1,0:T(8,128)S(1)}, f32[64,1280]{1,0:T(8,128)S(1)}, u32[]{:S(2)}, u32[]{:S(2)}) collective-permute-start(f32[64,1280]{1,0:T(8,128)S(1)} %get-tuple-element.354), channel_id=1, source_target_pairs={{0,4},{4,8},{8,12},{12,16},{16,20},{20,24},{24,28},{1,5},{5,9},{9,... | collective-permute-start | bytes 983048 | tf_op jit(solution)/shard_map/ppermute | solution.py:25
  149.3 0.7 compare_reduce_fusion
  150.0 1.3 collective-permute-start.5
  151.3 11.2 %collective-permute-done.4 = f32[64,1280]{1,0:T(8,128)S(1)} collective-permute-done((f32[64,1280]{1,0:T(8,128)S(1)}, f32[64,1280]{1,0:T(8,128)S(1)}, u32[]{:S(2)}, u32[]{:S(2)}) %collective-permute-start.4) | collective-permute-done | bytes 327712 | tf_op jit(solution)/shard_map/ppermute | solution.py:25
  162.4 0.7 broadcast_select_fusion
  163.1 1.8 %fusion.47 = f32[64,1792]{1,0:T(8,128)S(1)} fusion(f32[64,1792]{1,0:T(8,128)S(1)} %scatter-add.130, f32[3,64,1280]{2,1,0:T(8,128)} %reduce-scatter.2.cloned.1.call-done, pred[]{:T(512)} %compare_reduce_fusion), kind=kLoop, calls=%fused_computation.85 | loop fusion | flops 163840 | bytes 983041 | tf_op jit(solution)/shard_map/scatter-add | solution.py:31
  164.9 0.7 copy-done.1
  165.7 1.7 fusion.48
  (113 shorter events, 17.6 us)
Async XLA Ops:
  6.5 0.9 copy-start
  6.5 9.3 %copy-start.23 = (s32[4]{0:T(128)S(1)}, s32[4]{0:T(128)}, u32[]{:S(2)}) copy-start(s32[4]{0:T(128)} %param.67) | copy-start | bytes 52
  6.5 9.3 %copy-start.8 = (s32[2,7]{1,0:T(2,128)S(1)}, s32[2,7]{1,0:T(2,128)}, u32[]{:S(2)}) copy-start(s32[2,7]{1,0:T(2,128)} %param.64) | copy-start | bytes 172
  6.5 137.6 %reduce-scatter.2.cloned.1.call-start = ((), (), s32[]{:S(2)}) async-start(), calls=%async_computation.1 | async-start | bytes 4915200 | tf_op jit(solution)/shard_map/reduce_scatter | solution.py:78
  8.9 14.0 %collective-permute-start.1 = (bf16[1,1,2,128,768]{3,4,2,1,0:T(8,128)(2,1)S(1)}, bf16[1,1,2,128,768]{3,4,2,1,0:T(8,128)(2,1)S(1)}, u32[]{:S(2)}, u32[]{:S(2)}) collective-permute-start(bf16[1,1,2,128,768]{3,4,2,1,0:T(8,128)(2,1)S(1)} %bitcast.145), channel_id=1, source_target_pairs={{4,0},{8,4},{12,8},{16,12},{20,16},{24,20},{28,24},{5,1},{9,5},{13... | collective-permute-start | bytes 1179656 | tf_op jit(solution)/shard_map/ppermute | solution.py:17
  10.2 21.3 %collective-permute-start = (bf16[1,1,2,128,768]{3,4,2,1,0:T(8,128)(2,1)S(1)}, bf16[1,1,2,128,768]{3,4,2,1,0:T(8,128)(2,1)S(1)}, u32[]{:S(2)}, u32[]{:S(2)}) collective-permute-start(bf16[1,1,2,128,768]{3,4,2,1,0:T(8,128)(2,1)S(1)} %bitcast.146), channel_id=1, source_target_pairs={{0,4},{4,8},{8,12},{12,16},{16,20},{20,24},{24,28},{1,5},{5,9},{9,... | collective-permute-start | bytes 1179656 | tf_op jit(solution)/shard_map/ppermute | solution.py:14
  31.7 6.8 %collective-permute-start.3 = (bf16[3,1,2,128,768]{3,4,2,1,0:T(8,128)(2,1)S(1)}, bf16[3,1,2,128,768]{3,4,2,1,0:T(8,128)(2,1)S(1)}, u32[]{:S(2)}, u32[]{:S(2)}) collective-permute-start(bf16[3,1,2,128,768]{3,4,2,1,0:T(8,128)(2,1)S(1)} %pad_maximum_fusion.1), channel_id=1, source_target_pairs={{1,0},{2,1},{3,2},{5,4},{6,5},{7,6},{9,8},{10,9},{11,10},{13,12},{... | collective-permute-start | bytes 3538952 | tf_op jit(solution)/shard_map/ppermute | solution.py:17
  33.0 5.5 %collective-permute-start.2 = (bf16[3,1,2,128,768]{3,4,2,1,0:T(8,128)(2,1)S(1)}, bf16[3,1,2,128,768]{3,4,2,1,0:T(8,128)(2,1)S(1)}, u32[]{:S(2)}, u32[]{:S(2)}) collective-permute-start(bf16[3,1,2,128,768]{3,4,2,1,0:T(8,128)(2,1)S(1)} %pad_maximum_fusion.1), channel_id=1, source_target_pairs={{0,1},{1,2},{2,3},{4,5},{5,6},{6,7},{8,9},{9,10},{10,11},{12,13},{... | collective-permute-start | bytes 3538952 | tf_op jit(solution)/shard_map/ppermute | solution.py:14
  64.2 6.0 %copy-start.7 = (bf16[4,128,128]{2,1,0:T(8,128)(2,1)S(1)}, bf16[4,128,128]{2,1,0:T(8,128)(2,1)}, u32[]{:S(2)}) copy-start(bf16[4,128,128]{2,1,0:T(8,128)(2,1)} %param.65) | copy-start | bytes 393220
  70.2 1.1 copy-start.9
  70.7 1.2 copy-start.17
  71.3 1.2 copy-start.16
  71.9 1.2 copy-start.5
  71.9 1.2 copy-start.6
  72.5 0.9 copy-start.15
  73.5 0.6 copy-start.12
  74.4 1.0 copy-start.4
  74.4 1.0 copy-start.21
  75.4 0.7 copy-start.19
  76.2 1.0 copy-start.3
  77.8 1.0 copy-start.2
  77.8 1.0 copy-start.22
  78.8 0.6 copy-start.20
  79.6 0.7 copy-start.13
  80.3 0.6 copy-start.11
  81.0 0.7 copy-start.18
  81.7 0.6 copy-start.14
  82.5 0.7 copy-start.10
  145.2 17.2 %collective-permute-start.4 = (f32[64,1280]{1,0:T(8,128)S(1)}, f32[64,1280]{1,0:T(8,128)S(1)}, u32[]{:S(2)}, u32[]{:S(2)}) collective-permute-start(f32[64,1280]{1,0:T(8,128)S(1)} %get-tuple-element.354), channel_id=1, source_target_pairs={{0,4},{4,8},{8,12},{12,16},{16,20},{20,24},{24,28},{1,5},{5,9},{9,... | collective-permute-start | bytes 983048 | tf_op jit(solution)/shard_map/ppermute | solution.py:25
  150.0 14.9 %collective-permute-start.5 = (f32[64,1280]{1,0:T(8,128)S(1)}, f32[64,1280]{1,0:T(8,128)S(1)}, u32[]{:S(2)}, u32[]{:S(2)}) collective-permute-start(f32[64,1280]{1,0:T(8,128)S(1)} %get-tuple-element.353), channel_id=1, source_target_pairs={{4,0},{8,4},{12,8},{16,12},{20,16},{24,20},{28,24},{5,1},{9,5},{13... | collective-permute-start | bytes 983048 | tf_op jit(solution)/shard_map/ppermute | solution.py:25
  164.9 0.8 copy-start.1
Sparse Core Ops, SparseCore 0:
  87.3 56.7 reduce-scatter.1
where the time goes:
time: 175 us; the launch traced here: 174 us
  waiting for transfers between devices  81.4 us (47%)
  local copies, waits for them, and re-layouts  39.2 us (22%)
  starting transfers between devices  15.9 us (9%)
  other arithmetic  15.2 us (9%)
  between operations  14 us (8%)
  matrix products  8.48 us (5%)
    reduce_scatter x1, waiting for transfers between devices, body(): lax.psum_scatter(partial_value, 'cross', scatter_dimension=1, tiled=True)  56.9 us
    gather x7, local copies, waits for them, and re-layouts, body(): rows = jnp.take(extended, a_cols[:, k_index], axis=0)  21.1 us
    ppermute x2, waiting for transfers between devices, from_behind(): return lax.ppermute(value, axis, pairs)  11.2 us
    ppermute x2, starting transfers between devices, with_halo(): lax.ppermute(lax.slice_in_dim(block, block.shape[dim] - width, None, axis...  8.65 us
    ppermute x2, waiting for transfers between devices, with_halo(): lax.ppermute(lax.slice_in_dim(block, block.shape[dim] - width, None, axis...  8.6 us
    unnamed x49, local copies, waits for them, and re-layouts  6.88 us
    concatenate x1, local copies, waits for them, and re-layouts, with_halo(): block = jnp.concatenate([low, block, high], axis=dim)  6.03 us
    ppermute x2, starting transfers between devices, from_behind(): return lax.ppermute(value, axis, pairs)  4.67 us
  transfers between devices with their start and end apart: 7, of which 4 were waited for; matrix products, arithmetic and copies ran while one was open for 5% of the time, Pallas kernels for 0%

commit v1 on v0

v1 whole, which is shorter than its diff:
```python
import jax
import jax.numpy as jnp
from jax import lax
from jax.experimental import pallas as pl
from jax.experimental.pallas import tpu as pltpu
from jax.sharding import PartitionSpec as P

CB = 2
AXES = ("slab", "cross")
PAD = 16


def exchange(value, slabs, parts, move):
    pairs = []
    for s in range(slabs):
        for c in range(parts):
            t, d = move(s, c)
            pairs.append((s * parts + c, t * parts + d))
    return lax.ppermute(value, AXES, pairs)


def moves(slabs, parts):
    def odd(s):
        return (s - 1) % slabs if s % 2 == 0 else (s + 1) % slabs

    def across(c):
        d = c - 1 if c % 2 == 0 else c + 1
        return d if 0 <= d < parts else c

    return {
        "even": lambda s, c: (s ^ 1, c),
        "odd": lambda s, c: (odd(s), c),
        "pair": lambda s, c: (s, c ^ 1),
        "across": lambda s, c: (s, across(c)),
        "other": lambda s, c: (s, c ^ 2),
    }


def prepare_kernel(place, own, mate, own_cols, mate_cols, out):
    blocks, kp, tile = own.shape[0], own_cols.shape[1], own.shape[-1]
    half = tile // 2
    lower = place[0] == 0
    out[...] = jnp.zeros_like(out)
    for d, (source, cols) in enumerate(((own, own_cols), (mate, mate_cols))):
        for n in range(blocks):
            for m in range(kp):
                piece = source[n, m * tile : (m + 1) * tile, :]
                piece = jnp.where(lower, piece[:, :half], piece[:, half:])
                at = (d * blocks + n) * tile
                out[place[1 + cols[n, m]], :, at : at + tile] = piece.T


def product_kernel(info, a_cols, over_rows, over_cols, *refs):
    sources = refs[:9]
    a_tiles, over_tiles, out, ext, acc, cols_v, cols_s, sem = refs[9:]
    blocks, taps, tile = a_tiles.shape[0], a_tiles.shape[1], a_tiles.shape[-1]
    kp = ext.shape[-1] // tile
    for i, source in enumerate(sources):
        slot = info[2 * i]
        valid = info[2 * i + 1] == 1
        for n in range(blocks):
            row = source[n, kp * tile : kp * tile + PAD, :].astype(jnp.float32)
            cols_v[slot * blocks + n] = row[:8].astype(jnp.int32)
    copy = pltpu.make_async_copy(cols_v, cols_s, sem)
    copy.start()
    for i, source in enumerate(sources):
        slot = info[2 * i]
        valid = info[2 * i + 1] == 1
        for n in range(blocks):
            for m in range(kp):
                piece = source[n, m * tile : (m + 1) * tile, :]
                piece = jnp.where(valid, piece, jnp.zeros_like(piece))
                ext[slot * blocks + n, :, m * tile : (m + 1) * tile] = piece
    acc[...] = jnp.zeros_like(acc)
    copy.wait()

    def add(n, col, matrix):
        piece = jnp.dot(matrix, ext[col], preferred_element_type=jnp.float32)
        shift = (col // (3 * blocks)) * CB
        for m in range(kp):
            j = shift + cols_s[col, 0, m]
            acc[n, j] += piece[:, m * tile : (m + 1) * tile]

    for n in range(blocks):
        for k in range(taps):
            add(n, a_cols[n, k], a_tiles[n, k])
    for o in range(over_tiles.shape[0]):
        add(over_rows[o], over_cols[o], over_tiles[o])
    for n in range(blocks):
        for j in range(acc.shape[1]):
            out[n * tile : (n + 1) * tile, j * tile : (j + 1) * tile] = acc[n, j].astype(
                jnp.bfloat16
            )


def partial_kernel(left, own, mate, *outs):
    count, half = left.shape[0], left.shape[1]
    rows = own.shape[0]
    for i in range(count):
        block = left[i]
        total = jnp.dot(block[:, :rows], own[...], preferred_element_type=jnp.float32)
        total += jnp.dot(block[:, rows:], mate[...], preferred_element_type=jnp.float32)
        outs[i][...] = total.astype(outs[i].dtype)


def final_kernel(info, own, across, even, odd, out):
    width = (out.shape[1] - own.shape[1]) // 2
    span = own.shape[1]
    first = info[0] == 1
    odd_value = jnp.where(info[1] == 1, odd[...].astype(jnp.float32), 0.0)
    even_value = even[...].astype(jnp.float32)
    lower = jnp.where(first, odd_value, even_value)
    upper = jnp.where(first, even_value, odd_value)
    middle = own[...] + across[...].astype(jnp.float32)
    out[...] = jnp.zeros_like(out)
    out[:, :span] = lower
    out[:, width : width + span] += middle
    out[:, 2 * width : 2 * width + span] += upper


def vmem(count):
    return [pl.BlockSpec(memory_space=pltpu.VMEM)] * count


def smem(count):
    return [pl.BlockSpec(memory_space=pltpu.SMEM)] * count


def fast_body(slabs, parts, a_tiles, a_cols, over_tiles, over_rows, over_cols, p_tiles, p_cols):
    blocks, kp, tile = p_tiles.shape[0], p_tiles.shape[1], p_tiles.shape[-1]
    width = CB * tile
    span = blocks * tile
    half = tile // 2
    step = moves(slabs, parts)

    def send(value, name):
        return exchange(value, slabs, parts, step[name])

    slab = lax.axis_index("slab")
    part = lax.axis_index("cross")
    s_even = (slab % 2 == 0).astype(jnp.int32)
    c_even = (part % 2 == 0).astype(jnp.int32)
    odd_ok = jnp.where(s_even == 1, slab > 0, slab < slabs - 1).astype(jnp.int32)
    across_ok = jnp.where(c_even == 1, part > 0, part < parts - 1).astype(jnp.int32)
    r_even, r_odd = 2 * s_even, 2 - 2 * s_even
    u_pair, u_across = 2 * c_even, 2 - 2 * c_even

    cols = jnp.broadcast_to(
        jnp.pad(p_cols, ((0, 0), (0, tile - kp)))[:, None, :], (blocks, PAD, tile)
    ).astype(jnp.bfloat16)
    own = jnp.concatenate([p_tiles.reshape(blocks, kp * tile, tile), cols], axis=1)
    even = send(own, "even")
    odd = send(own, "odd")
    mate = send(own, "pair")
    own_x = send(own, "across")
    mate_cols = mate[:, kp * tile, :kp].astype(jnp.int32)
    even_p, odd_p = send(even, "pair"), send(odd, "pair")
    even_x, odd_x = send(even, "across"), send(odd, "across")

    side = part // 2
    q = jnp.arange(3 * CB, dtype=jnp.int32)
    block, owner = q // CB, q % CB
    here = owner == side
    place = jnp.where(
        block == 1,
        jnp.where(here, 5, 2),
        jnp.where((block == 2) == (s_even == 1), jnp.where(here, 4, 1), jnp.where(here, 3, 0)),
    )
    place = jnp.concatenate([(part % 2)[None], place]).astype(jnp.int32)
    left = pl.pallas_call(
        prepare_kernel,
        out_shape=jax.ShapeDtypeStruct((3 * CB, half, 2 * span), jnp.bfloat16),
        in_specs=smem(1) + vmem(2) + smem(2),
        out_specs=vmem(1)[0],
        cost_estimate=pl.CostEstimate(flops=0, bytes_accessed=1 << 20, transcendentals=0),
    )(place, own, mate, p_cols, mate_cols)

    one = jnp.int32(1)
    info = []
    for r, ok in ((one, one), (r_even, one), (r_odd, odd_ok)):
        for u, good in ((one, one), (u_pair, one), (u_across, across_ok)):
            info += [3 * r + u, ok * good]
    info = jnp.stack(info).astype(jnp.int32)
    product = pl.pallas_call(
        product_kernel,
        out_shape=jax.ShapeDtypeStruct((span, 5 * width), jnp.bfloat16),
        in_specs=smem(4) + vmem(11),
        out_specs=vmem(1)[0],
        scratch_shapes=[
            pltpu.VMEM((9 * blocks, tile, kp * tile), jnp.bfloat16),
            pltpu.VMEM((blocks, 5 * CB, tile, tile), jnp.float32),
            pltpu.VMEM((9 * blocks, 8, tile), jnp.int32),
            pltpu.SMEM((9 * blocks, 8, tile), jnp.int32),
            pltpu.SemaphoreType.DMA,
        ],
        cost_estimate=pl.CostEstimate(flops=1 << 29, bytes_accessed=1 << 22, transcendentals=0),
    )(
        info, a_cols, over_rows, over_cols,
        own, mate, own_x, even, even_p, even_x, odd, odd_p, odd_x,
        a_tiles, over_tiles,
    )
    product_mate = send(product, "pair")

    kinds = [jnp.bfloat16] * 3 + [jnp.float32] * 3
    x_odd, x_even, x_own, b_odd, b_even, b_own = pl.pallas_call(
        partial_kernel,
        out_shape=[jax.ShapeDtypeStruct((half, 5 * width), kind) for kind in kinds],
        in_specs=vmem(3),
        out_specs=vmem(6),
        cost_estimate=pl.CostEstimate(flops=1 << 29, bytes_accessed=1 << 22, transcendentals=0),
    )(left, product, product_mate)
    g_odd = send(x_odd, "other")
    g_even = send(x_even, "other")
    g_own = send(x_own, "other")
    s_odd = send((b_odd + g_odd.astype(jnp.float32)).astype(jnp.bfloat16), "odd")
    s_even_ = send((b_even + g_even.astype(jnp.float32)).astype(jnp.bfloat16), "even")
    return pl.pallas_call(
        final_kernel,
        out_shape=jax.ShapeDtypeStruct((half, 7 * width), jnp.float32),
        in_specs=smem(1) + vmem(4),
        out_specs=vmem(1)[0],
    )(jnp.stack([s_even, odd_ok]), b_own, g_own, s_even_, s_odd)


SPECS = (
    P(AXES, None, None, None),
    P(AXES, None),
    P(AXES, None, None),
    P(AXES),
    P(AXES),
    P(AXES, None, None, None),
    P(AXES, None),
)


def solution(mesh):
    slabs, parts = mesh.shape["slab"], mesh.shape["cross"]

    def body(*args):
        return fast_body(slabs, parts, *args)

    return jax.shard_map(
        body, mesh=mesh, in_specs=SPECS, out_specs=P(AXES, None), check_vma=False
    )
```

time: 175 us -> 65 us (0.37)
  waiting for transfers between devices: 81.4 us -> 15.7 us
  local copies, waits for them, and re-layouts: 39.2 us -> 3.23 us
  between operations: 14 us -> 0.16 us
  Pallas kernels: 0 us -> 13.6 us
  starting transfers between devices: 15.9 us -> 26.8 us
  other arithmetic: 15.2 us -> 5.18 us
  matrix products: 8.48 us -> 0 us
    reduce_scatter x1 -> x0, waiting for transfers between devices: 56.9 us -> none  [body(): lax.psum_scatter(partial_value, 'cross', scatter_dimension=1, tiled=True)]
    gather x8 -> x0, local copies, waits for them, and re-layouts: 23.7 us -> none  [the longest x7 21.1 us: body(): rows = jnp.take(extended, a_cols[:, k_index], axis=0)]
    pallas_call x0 -> x4, Pallas kernels: none -> 13.6 us  [the longest x1 5.43 us: fast_body(): pl.pallas_call(product_kernel, out_shape=jax.ShapeDtypeStruct((span, 5 *...]
    ppermute x6 -> x14, starting transfers between devices: 15.9 us -> 26.8 us  [exchange(): return lax.ppermute(value, AXES, pairs)]
    ppermute x6 -> x14, waiting for transfers between devices: 24.4 us -> 15.7 us  [exchange(): return lax.ppermute(value, AXES, pairs)]
    dot_general x13 -> x0, matrix products: 8.48 us -> none  [the longest x7 2.63 us: body(): jnp.einsum('nab,nbq->naq', a_tiles[:, k_index], rows, preferred_element_t...]
    scatter-add x19 -> x0, other arithmetic: 6.77 us -> none  [the longest x17 3.27 us: body(): product.at[:, :, shift_index * width:shift_index * width + wide]]
    concatenate x1 -> x0, local copies, waits for them, and re-layouts: 6.03 us -> none  [with_halo(): block = jnp.concatenate([low, block, high], axis=dim)]
  transfers between devices with their start and end apart: 7 -> 14, of which waited for: 4 -> 6; matrix products, arithmetic and copies ran while one was open for 5% -> 6% of each run, Pallas kernels for 0% -> 4%
where the time goes in v1:
time: 65 us; the launch traced here: 64.6 us
  starting transfers between devices  26.8 us (41%)
  waiting for transfers between devices  15.7 us (24%)
  Pallas kernels  13.6 us (21%)
  other arithmetic  5.18 us (8%)
  local copies, waits for them, and re-layouts  3.23 us (5%)
    ppermute x14, starting transfers between devices, exchange(): return lax.ppermute(value, AXES, pairs)  26.8 us
    ppermute x14, waiting for transfers between devices, exchange(): return lax.ppermute(value, AXES, pairs)  15.7 us
    pallas_call x1, Pallas kernels, fast_body(): pl.pallas_call(product_kernel, out_shape=jax.ShapeDtypeStruct((span, 5 *...  5.43 us
    pallas_call x1, Pallas kernels, fast_body(): pl.pallas_call(partial_kernel, out_shape=[jax.ShapeDtypeStruct((half, 5 *...  3.61 us
    unnamed x28, local copies, waits for them, and re-layouts  2.63 us
    pallas_call x1, Pallas kernels, fast_body(): pl.pallas_call(prepare_kernel, out_shape=jax.ShapeDtypeStruct((3 * CB, ha...  2.45 us
    pallas_call x1, Pallas kernels, fast_body(): pl.pallas_call(final_kernel, out_shape=jax.ShapeDtypeStruct((half, 7 * wi...  2.11 us
  transfers between devices with their start and end apart: 14, of which 6 were waited for; matrix products, arithmetic and copies ran while one was open for 6% of the time, Pallas kernels for 4%

profile of v1, /device:TPU:0, one launch (start us, length us, event | category | flops | bytes accessed | tf_op | source)
XLA Modules:
  0.0 64.6 jit_solution(13350039792835449134)
XLA Ops:
  0.0 0.7 %convert.6 = bf16[2,3]{1,0:T(2,128)(2,1)S(1)} convert(s32[2,3]{1,0:T(2,128)} %own_cols.1) | non-fusion elementwise | flops 6 | bytes 36 | tf_op jit(solution)/shard_map/convert.2
  0.7 0.9 %pad_maximum_fusion.own.refs_0_ = bf16[2,400,128]{2,1,0:T(8,128)(2,1)S(1)} fusion(bf16[2,16,128]{2,1,0:T(8,128)(2,1)S(1)} %broadcast_in_dim.27, bf16[2,384,128]{2,1,0:T(8,128)(2,1)} %bitcast.15), kind=kLoop, calls=%fused_computation.2 | loop fusion | flops 409600 | bytes 409600 | tf_op jit(solution)/shard_map/concatenate | solution.py:151
  1.7 6.1 %collective-permute-start.5 = (bf16[2,400,128]{2,1,0:T(8,128)(2,1)S(1)}, bf16[2,400,128]{2,1,0:T(8,128)(2,1)S(1)}, u32[]{:S(2)}, u32[]{:S(2)}) collective-permute-start(bf16[2,400,128]{2,1,0:T(8,128)(2,1)S(1)} %pad_maximum_fusion.own.refs_0_), channel_id=1, source_target_pairs={{0,28},{1,29},{2,30},{3,31},{4,8},{5,9},{6,10},{7,11},{8,4},{9,5},... | collective-permute-start | bytes 614408 | tf_op jit(solution)/shard_map/ppermute | solution.py:19
  7.8 0.7 %collective-permute-start.1 = (bf16[2,400,128]{2,1,0:T(8,128)(2,1)S(1)}, bf16[2,400,128]{2,1,0:T(8,128)(2,1)S(1)}, u32[]{:S(2)}, u32[]{:S(2)}) collective-permute-start(bf16[2,400,128]{2,1,0:T(8,128)(2,1)S(1)} %pad_maximum_fusion.own.refs_0_), channel_id=1, source_target_pairs={{0,0},{1,2},{2,1},{3,3},{4,4},{5,6},{6,5},{7,7},{8,8},{9,10},{10,9... | collective-permute-start | bytes 614408 | tf_op jit(solution)/shard_map/ppermute | solution.py:19
  8.4 2.9 %collective-permute-start = (bf16[2,400,128]{2,1,0:T(8,128)(2,1)S(1)}, bf16[2,400,128]{2,1,0:T(8,128)(2,1)S(1)}, u32[]{:S(2)}, u32[]{:S(2)}) collective-permute-start(bf16[2,400,128]{2,1,0:T(8,128)(2,1)S(1)} %pad_maximum_fusion.own.refs_0_), channel_id=1, source_target_pairs={{0,1},{1,0},{2,3},{3,2},{4,5},{5,4},{6,7},{7,6},{8,9},{9,8},{10,11... | collective-permute-start | bytes 614408 | tf_op jit(solution)/shard_map/ppermute | solution.py:19
  11.3 1.6 %collective-permute-done.5.refs_6_ = bf16[2,400,128]{2,1,0:T(8,128)(2,1)S(1)} collective-permute-done((bf16[2,400,128]{2,1,0:T(8,128)(2,1)S(1)}, bf16[2,400,128]{2,1,0:T(8,128)(2,1)S(1)}, u32[]{:S(2)}, u32[]{:S(2)}) %collective-permute-start.5) | collective-permute-done | bytes 204832 | tf_op jit(solution)/shard_map/ppermute | solution.py:19
  12.9 0.7 %collective-permute-start.7 = (bf16[2,400,128]{2,1,0:T(8,128)(2,1)S(1)}, bf16[2,400,128]{2,1,0:T(8,128)(2,1)S(1)}, u32[]{:S(2)}, u32[]{:S(2)}) collective-permute-start(bf16[2,400,128]{2,1,0:T(8,128)(2,1)S(1)} %collective-permute-done.5.refs_6_), channel_id=1, source_target_pairs={{0,0},{1,2},{2,1},{3,3},{4,4},{5,6},{6,5},{7,7},{8,8},{9,10},{10,9... | collective-permute-start | bytes 614408 | tf_op jit(solution)/shard_map/ppermute | solution.py:19
  13.6 2.9 %collective-permute-start.6 = (bf16[2,400,128]{2,1,0:T(8,128)(2,1)S(1)}, bf16[2,400,128]{2,1,0:T(8,128)(2,1)S(1)}, u32[]{:S(2)}, u32[]{:S(2)}) collective-permute-start(bf16[2,400,128]{2,1,0:T(8,128)(2,1)S(1)} %collective-permute-done.5.refs_6_), channel_id=1, source_target_pairs={{0,1},{1,0},{2,3},{3,2},{4,5},{5,4},{6,7},{7,6},{8,9},{9,8},{10,11... | collective-permute-start | bytes 614408 | tf_op jit(solution)/shard_map/ppermute | solution.py:19
  16.5 0.7 %collective-permute-done.2.refs_3_ = bf16[2,400,128]{2,1,0:T(8,128)(2,1)S(1)} collective-permute-done((bf16[2,400,128]{2,1,0:T(8,128)(2,1)S(1)}, bf16[2,400,128]{2,1,0:T(8,128)(2,1)S(1)}, u32[]{:S(2)}, u32[]{:S(2)}) %collective-permute-start.2) | collective-permute-done | bytes 204832 | tf_op jit(solution)/shard_map/ppermute | solution.py:19
  17.2 0.7 %collective-permute-start.4 = (bf16[2,400,128]{2,1,0:T(8,128)(2,1)S(1)}, bf16[2,400,128]{2,1,0:T(8,128)(2,1)S(1)}, u32[]{:S(2)}, u32[]{:S(2)}) collective-permute-start(bf16[2,400,128]{2,1,0:T(8,128)(2,1)S(1)} %collective-permute-done.2.refs_3_), channel_id=1, source_target_pairs={{0,0},{1,2},{2,1},{3,3},{4,4},{5,6},{6,5},{7,7},{8,8},{9,10},{10,9... | collective-permute-start | bytes 614408 | tf_op jit(solution)/shard_map/ppermute | solution.py:19
  17.9 2.9 %collective-permute-start.3 = (bf16[2,400,128]{2,1,0:T(8,128)(2,1)S(1)}, bf16[2,400,128]{2,1,0:T(8,128)(2,1)S(1)}, u32[]{:S(2)}, u32[]{:S(2)}) collective-permute-start(bf16[2,400,128]{2,1,0:T(8,128)(2,1)S(1)} %collective-permute-done.2.refs_3_), channel_id=1, source_target_pairs={{0,1},{1,0},{2,3},{3,2},{4,5},{5,4},{6,7},{7,6},{8,9},{9,8},{10,11... | collective-permute-start | bytes 614408 | tf_op jit(solution)/shard_map/ppermute | solution.py:19
  20.8 0.6 stack.62.info
  21.5 0.4 collective-permute-done.3.refs_4_
  22.3 0.7 %copy-done.9 = bf16[2,400,128]{2,1,0:T(8,128)(2,1)} copy-done((bf16[2,400,128]{2,1,0:T(8,128)(2,1)}, bf16[2,400,128]{2,1,0:T(8,128)(2,1)S(1)}, u32[]{:S(2)}) %copy-start.9) | copy-done | bytes 204824
  23.0 5.4 %shard_map.74.own = bf16[256,1280]{1,0:T(8,128)(2,1)} custom-call(s32[18]{0:T(128)} %stack.62.info, s32[2,7]{1,0:T(2,128)} %a_cols.1, s32[4]{0:T(128)} %over_rows.1, s32[4]{0:T(128)} %over_cols.1, bf16[2,400,128]{2,1,0:T(8,128)(2,1)} %copy-done, bf16[2,400,128]{2,1,0:T(8,128)(2,1)} %copy-done.1, bf16[2,400,128]{2,1,0:T(8,128)(2,1)} %copy-done.5, ...), custom_call_target="tpu_custom_call" | custom-call | flops 536870912 | bytes 4194304 | tf_op jit(solution)/shard_map/pallas_call | solution.py:184
  28.4 2.7 %collective-permute-start.8 = (bf16[256,1280]{1,0:T(8,128)(2,1)}, bf16[256,1280]{1,0:T(8,128)(2,1)S(1)}, u32[]{:S(2)}, u32[]{:S(2)}) collective-permute-start(bf16[256,1280]{1,0:T(8,128)(2,1)} %shard_map.74.own), channel_id=1, source_target_pairs={{0,1},{1,0},{2,3},{3,2},{4,5},{5,4},{6,7},{7,6},{8,9},{9,8},{10,11... | collective-permute-start | bytes 1966088 | tf_op jit(solution)/shard_map/ppermute | solution.py:19
  31.2 0.6 pad_add_fusion.1.place
  31.8 1.3 %slice_convert_fusion = s32[2,1,3]{2,1,0:T(1,128)} fusion(bf16[2,400,128]{2,1,0:T(8,128)(2,1)} %copy-done.1), kind=kLoop, calls=%fused_computation.7 | loop fusion | flops 6 | bytes 36 | tf_op jit(solution)/shard_map/convert_element_type | solution.py:156
  33.0 2.5 %shard_map.73.left = bf16[6,64,512]{2,1,0:T(8,128)(2,1)} custom-call(s32[7]{0:T(128)} %pad_add_fusion.1.place, bf16[2,400,128]{2,1,0:T(8,128)(2,1)} %copy-done, bf16[2,400,128]{2,1,0:T(8,128)(2,1)} %copy-done.1, s32[2,3]{1,0:T(2,128)} %own_cols.1, s32[2,3]{1,0:T(2,128)} %bitcast.16), custom_call_target="tpu_custom_call" | custom-call | bytes 1048576 | tf_op jit(solution)/shard_map/pallas_call | solution.py:170
  35.5 0.9 %copy-done.13 = bf16[256,1280]{1,0:T(8,128)(2,1)} copy-done((bf16[256,1280]{1,0:T(8,128)(2,1)}, bf16[256,1280]{1,0:T(8,128)(2,1)S(1)}, u32[]{:S(2)}) %copy-start.13) | copy-done | bytes 655384
  36.4 3.6 %shard_map.75 = (bf16[64,1280]{1,0:T(8,128)(2,1)}, bf16[64,1280]{1,0:T(8,128)(2,1)}, bf16[64,1280]{1,0:T(8,128)(2,1)}, f32[64,1280]{1,0:T(8,128)}, f32[64,1280]{1,0:T(8,128)}, /*index=5*/f32[64,1280]{1,0:T(8,128)}) custom-call(bf16[6,64,512]{2,1,0:T(8,128)(2,1)} %shard_map.73.left, bf16[256,1280]{1,0:T(8,128)(2,1)} %shard_map.74.own, ...), custom_call_target="tpu_custom_call" | custom-call | flops 536870912 | bytes 4194304 | tf_op jit(solution)/shard_map/pallas_call | solution.py:205
  40.0 1.5 %collective-permute-start.10 = (bf16[64,1280]{1,0:T(8,128)(2,1)}, bf16[64,1280]{1,0:T(8,128)(2,1)S(1)}, u32[]{:S(2)}, u32[]{:S(2)}) collective-permute-start(bf16[64,1280]{1,0:T(8,128)(2,1)} %get-tuple-element.14), channel_id=1, source_target_pairs={{0,2},{1,3},{2,0},{3,1},{4,6},{5,7},{6,4},{7,5},{8,10},{9,11},{10,... | collective-permute-start | bytes 491528 | tf_op jit(solution)/shard_map/ppermute | solution.py:19
  41.5 0.5 collective-permute-start.9
  42.0 1.5 %collective-permute-start.12 = (bf16[64,1280]{1,0:T(8,128)(2,1)}, bf16[64,1280]{1,0:T(8,128)(2,1)S(1)}, u32[]{:S(2)}, u32[]{:S(2)}) collective-permute-start(bf16[64,1280]{1,0:T(8,128)(2,1)} %get-tuple-element.16), channel_id=1, source_target_pairs={{0,2},{1,3},{2,0},{3,1},{4,6},{5,7},{6,4},{7,5},{8,10},{9,11},{10,... | collective-permute-start | bytes 491528 | tf_op jit(solution)/shard_map/ppermute | solution.py:19
  43.5 3.7 %collective-permute-done.10 = bf16[64,1280]{1,0:T(8,128)(2,1)S(1)} collective-permute-done((bf16[64,1280]{1,0:T(8,128)(2,1)}, bf16[64,1280]{1,0:T(8,128)(2,1)S(1)}, u32[]{:S(2)}, u32[]{:S(2)}) %collective-permute-start.10) | collective-permute-done | bytes 163872 | tf_op jit(solution)/shard_map/ppermute | solution.py:19
  47.3 1.1 %add_convert_fusion.1 = bf16[64,1280]{1,0:T(8,128)(2,1)S(1)} fusion(f32[64,1280]{1,0:T(8,128)} %get-tuple-element.13, bf16[64,1280]{1,0:T(8,128)(2,1)S(1)} %collective-permute-done.10), kind=kLoop, calls=%fused_computation.1 | loop fusion | flops 245760 | bytes 655360 | tf_op jit(solution)/shard_map/convert_element_type | solution.py:216
  48.4 5.2 %collective-permute-done.12 = bf16[64,1280]{1,0:T(8,128)(2,1)S(1)} collective-permute-done((bf16[64,1280]{1,0:T(8,128)(2,1)}, bf16[64,1280]{1,0:T(8,128)(2,1)S(1)}, u32[]{:S(2)}, u32[]{:S(2)}) %collective-permute-start.12) | collective-permute-done | bytes 163872 | tf_op jit(solution)/shard_map/ppermute | solution.py:19
  53.6 3.6 %collective-permute-start.13 = (bf16[64,1280]{1,0:T(8,128)(2,1)S(1)}, bf16[64,1280]{1,0:T(8,128)(2,1)S(1)}, u32[]{:S(2)}, u32[]{:S(2)}) collective-permute-start(bf16[64,1280]{1,0:T(8,128)(2,1)S(1)} %add_convert_fusion), channel_id=1, source_target_pairs={{0,28},{1,29},{2,30},{3,31},{4,8},{5,9},{6,10},{7,11},{8,4},{9,5},... | collective-permute-start | bytes 491528 | tf_op jit(solution)/shard_map/ppermute | solution.py:19
  57.2 0.6 pad_add_fusion.info
  57.8 4.0 %collective-permute-done.13.odd = bf16[64,1280]{1,0:T(8,128)(2,1)S(1)} collective-permute-done((bf16[64,1280]{1,0:T(8,128)(2,1)S(1)}, bf16[64,1280]{1,0:T(8,128)(2,1)S(1)}, u32[]{:S(2)}, u32[]{:S(2)}) %collective-permute-start.13) | collective-permute-done | bytes 163872 | tf_op jit(solution)/shard_map/ppermute | solution.py:19
  61.9 0.7 %copy-done.12 = bf16[64,1280]{1,0:T(8,128)(2,1)} copy-done((bf16[64,1280]{1,0:T(8,128)(2,1)}, bf16[64,1280]{1,0:T(8,128)(2,1)S(1)}, u32[]{:S(2)}) %copy-start.12) | copy-done | bytes 163864
  62.5 2.1 %shard_map.76 = f32[64,1792]{1,0:T(8,128)} custom-call(s32[2]{0:T(128)} %pad_add_fusion.info, f32[64,1280]{1,0:T(8,128)} %get-tuple-element.11.own, bf16[64,1280]{1,0:T(8,128)(2,1)} %copy-done.10, bf16[64,1280]{1,0:T(8,128)(2,1)} %copy-done.11, bf16[64,1280]{1,0:T(8,128)(2,1)} %copy-done.12), custom_call_target="tpu_custom_call" | custom-call | tf_op jit(solution)/shard_map/pallas_call | solution.py:217
  (39 shorter events, 0.6 us)
Async XLA Ops:
  1.6 20.3 %copy-start = (bf16[2,400,128]{2,1,0:T(8,128)(2,1)}, bf16[2,400,128]{2,1,0:T(8,128)(2,1)S(1)}, u32[]{:S(2)}) copy-start(bf16[2,400,128]{2,1,0:T(8,128)(2,1)S(1)} %pad_maximum_fusion.own.refs_0_) | copy-start | bytes 614404
  1.7 11.3 %collective-permute-start.5 = (bf16[2,400,128]{2,1,0:T(8,128)(2,1)S(1)}, bf16[2,400,128]{2,1,0:T(8,128)(2,1)S(1)}, u32[]{:S(2)}, u32[]{:S(2)}) collective-permute-start(bf16[2,400,128]{2,1,0:T(8,128)(2,1)S(1)} %pad_maximum_fusion.own.refs_0_), channel_id=1, source_target_pairs={{0,28},{1,29},{2,30},{3,31},{4,8},{5,9},{6,10},{7,11},{8,4},{9,5},... | collective-permute-start | bytes 614408 | tf_op jit(solution)/shard_map/ppermute | solution.py:19
  7.8 9.5 %collective-permute-start.2 = (bf16[2,400,128]{2,1,0:T(8,128)(2,1)S(1)}, bf16[2,400,128]{2,1,0:T(8,128)(2,1)S(1)}, u32[]{:S(2)}, u32[]{:S(2)}) collective-permute-start(bf16[2,400,128]{2,1,0:T(8,128)(2,1)S(1)} %pad_maximum_fusion.own.refs_0_), channel_id=1, source_target_pairs={{0,4},{1,5},{2,6},{3,7},{4,0},{5,1},{6,2},{7,3},{8,12},{9,13},{10,... | collective-permute-start | bytes 614408 | tf_op jit(solution)/shard_map/ppermute | solution.py:19
  7.8 10.1 %collective-permute-start.1 = (bf16[2,400,128]{2,1,0:T(8,128)(2,1)S(1)}, bf16[2,400,128]{2,1,0:T(8,128)(2,1)S(1)}, u32[]{:S(2)}, u32[]{:S(2)}) collective-permute-start(bf16[2,400,128]{2,1,0:T(8,128)(2,1)S(1)} %pad_maximum_fusion.own.refs_0_), channel_id=1, source_target_pairs={{0,0},{1,2},{2,1},{3,3},{4,4},{5,6},{6,5},{7,7},{8,8},{9,10},{10,9... | collective-permute-start | bytes 614408 | tf_op jit(solution)/shard_map/ppermute | solution.py:19
  8.4 13.0 %collective-permute-start = (bf16[2,400,128]{2,1,0:T(8,128)(2,1)S(1)}, bf16[2,400,128]{2,1,0:T(8,128)(2,1)S(1)}, u32[]{:S(2)}, u32[]{:S(2)}) collective-permute-start(bf16[2,400,128]{2,1,0:T(8,128)(2,1)S(1)} %pad_maximum_fusion.own.refs_0_), channel_id=1, source_target_pairs={{0,1},{1,0},{2,3},{3,2},{4,5},{5,4},{6,7},{7,6},{8,9},{9,8},{10,11... | collective-permute-start | bytes 614408 | tf_op jit(solution)/shard_map/ppermute | solution.py:19
  12.9 9.0 %copy-start.3 = (bf16[2,400,128]{2,1,0:T(8,128)(2,1)}, bf16[2,400,128]{2,1,0:T(8,128)(2,1)S(1)}, u32[]{:S(2)}) copy-start(bf16[2,400,128]{2,1,0:T(8,128)(2,1)S(1)} %collective-permute-done.5.refs_6_) | copy-start | bytes 614404
  12.9 8.5 %collective-permute-start.7 = (bf16[2,400,128]{2,1,0:T(8,128)(2,1)S(1)}, bf16[2,400,128]{2,1,0:T(8,128)(2,1)S(1)}, u32[]{:S(2)}, u32[]{:S(2)}) collective-permute-start(bf16[2,400,128]{2,1,0:T(8,128)(2,1)S(1)} %collective-permute-done.5.refs_6_), channel_id=1, source_target_pairs={{0,0},{1,2},{2,1},{3,3},{4,4},{5,6},{6,5},{7,7},{8,8},{9,10},{10,9... | collective-permute-start | bytes 614408 | tf_op jit(solution)/shard_map/ppermute | solution.py:19
  13.6 7.8 %collective-permute-start.6 = (bf16[2,400,128]{2,1,0:T(8,128)(2,1)S(1)}, bf16[2,400,128]{2,1,0:T(8,128)(2,1)S(1)}, u32[]{:S(2)}, u32[]{:S(2)}) collective-permute-start(bf16[2,400,128]{2,1,0:T(8,128)(2,1)S(1)} %collective-permute-done.5.refs_6_), channel_id=1, source_target_pairs={{0,1},{1,0},{2,3},{3,2},{4,5},{5,4},{6,7},{7,6},{8,9},{9,8},{10,11... | collective-permute-start | bytes 614408 | tf_op jit(solution)/shard_map/ppermute | solution.py:19
  17.2 4.7 %copy-start.4 = (bf16[2,400,128]{2,1,0:T(8,128)(2,1)}, bf16[2,400,128]{2,1,0:T(8,128)(2,1)S(1)}, u32[]{:S(2)}) copy-start(bf16[2,400,128]{2,1,0:T(8,128)(2,1)S(1)} %collective-permute-done.2.refs_3_) | copy-start | bytes 614404
  17.2 4.2 %collective-permute-start.4 = (bf16[2,400,128]{2,1,0:T(8,128)(2,1)S(1)}, bf16[2,400,128]{2,1,0:T(8,128)(2,1)S(1)}, u32[]{:S(2)}, u32[]{:S(2)}) collective-permute-start(bf16[2,400,128]{2,1,0:T(8,128)(2,1)S(1)} %collective-permute-done.2.refs_3_), channel_id=1, source_target_pairs={{0,0},{1,2},{2,1},{3,3},{4,4},{5,6},{6,5},{7,7},{8,8},{9,10},{10,9... | collective-permute-start | bytes 614408 | tf_op jit(solution)/shard_map/ppermute | solution.py:19
  17.9 4.0 %copy-start.5 = (bf16[2,400,128]{2,1,0:T(8,128)(2,1)}, bf16[2,400,128]{2,1,0:T(8,128)(2,1)S(1)}, u32[]{:S(2)}) copy-start(bf16[2,400,128]{2,1,0:T(8,128)(2,1)S(1)} %collective-permute-done.1.refs_2_) | copy-start | bytes 614404
  17.9 4.0 %collective-permute-start.3 = (bf16[2,400,128]{2,1,0:T(8,128)(2,1)S(1)}, bf16[2,400,128]{2,1,0:T(8,128)(2,1)S(1)}, u32[]{:S(2)}, u32[]{:S(2)}) collective-permute-start(bf16[2,400,128]{2,1,0:T(8,128)(2,1)S(1)} %collective-permute-done.2.refs_3_), channel_id=1, source_target_pairs={{0,1},{1,0},{2,3},{3,2},{4,5},{5,4},{6,7},{7,6},{8,9},{9,8},{10,11... | collective-permute-start | bytes 614408 | tf_op jit(solution)/shard_map/ppermute | solution.py:19
  21.4 0.7 %copy-start.1 = (bf16[2,400,128]{2,1,0:T(8,128)(2,1)}, bf16[2,400,128]{2,1,0:T(8,128)(2,1)S(1)}, u32[]{:S(2)}) copy-start(bf16[2,400,128]{2,1,0:T(8,128)(2,1)S(1)} %collective-permute-done.mate.refs_1_) | copy-start | bytes 614404
  21.4 0.7 %copy-start.6 = (bf16[2,400,128]{2,1,0:T(8,128)(2,1)}, bf16[2,400,128]{2,1,0:T(8,128)(2,1)S(1)}, u32[]{:S(2)}) copy-start(bf16[2,400,128]{2,1,0:T(8,128)(2,1)S(1)} %collective-permute-done.7.refs_8_) | copy-start | bytes 614404
  21.4 0.8 %copy-start.7 = (bf16[2,400,128]{2,1,0:T(8,128)(2,1)}, bf16[2,400,128]{2,1,0:T(8,128)(2,1)S(1)}, u32[]{:S(2)}) copy-start(bf16[2,400,128]{2,1,0:T(8,128)(2,1)S(1)} %collective-permute-done.6.refs_7_) | copy-start | bytes 614404
  21.5 0.9 %copy-start.8 = (bf16[2,400,128]{2,1,0:T(8,128)(2,1)}, bf16[2,400,128]{2,1,0:T(8,128)(2,1)S(1)}, u32[]{:S(2)}) copy-start(bf16[2,400,128]{2,1,0:T(8,128)(2,1)S(1)} %collective-permute-done.4.refs_5_) | copy-start | bytes 614404
  22.3 0.7 %copy-start.9 = (bf16[2,400,128]{2,1,0:T(8,128)(2,1)}, bf16[2,400,128]{2,1,0:T(8,128)(2,1)S(1)}, u32[]{:S(2)}) copy-start(bf16[2,400,128]{2,1,0:T(8,128)(2,1)S(1)} %collective-permute-done.3.refs_4_) | copy-start | bytes 614404
  28.4 7.1 %collective-permute-start.8 = (bf16[256,1280]{1,0:T(8,128)(2,1)}, bf16[256,1280]{1,0:T(8,128)(2,1)S(1)}, u32[]{:S(2)}, u32[]{:S(2)}) collective-permute-start(bf16[256,1280]{1,0:T(8,128)(2,1)} %shard_map.74.own), channel_id=1, source_target_pairs={{0,1},{1,0},{2,3},{3,2},{4,5},{5,4},{6,7},{7,6},{8,9},{9,8},{10,11... | collective-permute-start | bytes 1966088 | tf_op jit(solution)/shard_map/ppermute | solution.py:19
  35.5 0.9 %copy-start.13 = (bf16[256,1280]{1,0:T(8,128)(2,1)}, bf16[256,1280]{1,0:T(8,128)(2,1)S(1)}, u32[]{:S(2)}) copy-start(bf16[256,1280]{1,0:T(8,128)(2,1)S(1)} %collective-permute-done.8.mate) | copy-start | bytes 1966084
  40.0 7.3 %collective-permute-start.10 = (bf16[64,1280]{1,0:T(8,128)(2,1)}, bf16[64,1280]{1,0:T(8,128)(2,1)S(1)}, u32[]{:S(2)}, u32[]{:S(2)}) collective-permute-start(bf16[64,1280]{1,0:T(8,128)(2,1)} %get-tuple-element.14), channel_id=1, source_target_pairs={{0,2},{1,3},{2,0},{3,1},{4,6},{5,7},{6,4},{7,5},{8,10},{9,11},{10,... | collective-permute-start | bytes 491528 | tf_op jit(solution)/shard_map/ppermute | solution.py:19
  41.5 16.3 %collective-permute-start.9 = (bf16[64,1280]{1,0:T(8,128)(2,1)}, bf16[64,1280]{1,0:T(8,128)(2,1)S(1)}, u32[]{:S(2)}, u32[]{:S(2)}) collective-permute-start(bf16[64,1280]{1,0:T(8,128)(2,1)} %get-tuple-element.12), channel_id=1, source_target_pairs={{0,2},{1,3},{2,0},{3,1},{4,6},{5,7},{6,4},{7,5},{8,10},{9,11},{10,... | collective-permute-start | bytes 491528 | tf_op jit(solution)/shard_map/ppermute | solution.py:19
  42.0 11.6 %collective-permute-start.12 = (bf16[64,1280]{1,0:T(8,128)(2,1)}, bf16[64,1280]{1,0:T(8,128)(2,1)S(1)}, u32[]{:S(2)}, u32[]{:S(2)}) collective-permute-start(bf16[64,1280]{1,0:T(8,128)(2,1)} %get-tuple-element.16), channel_id=1, source_target_pairs={{0,2},{1,3},{2,0},{3,1},{4,6},{5,7},{6,4},{7,5},{8,10},{9,11},{10,... | collective-permute-start | bytes 491528 | tf_op jit(solution)/shard_map/ppermute | solution.py:19
  47.2 6.3 %copy-start.2 = (f32[64,1280]{1,0:T(8,128)S(1)}, f32[64,1280]{1,0:T(8,128)}, u32[]{:S(2)}) copy-start(f32[64,1280]{1,0:T(8,128)} %get-tuple-element.15) | copy-start | bytes 983044
  48.3 9.5 %collective-permute-start.11 = (bf16[64,1280]{1,0:T(8,128)(2,1)S(1)}, bf16[64,1280]{1,0:T(8,128)(2,1)S(1)}, u32[]{:S(2)}, u32[]{:S(2)}) collective-permute-start(bf16[64,1280]{1,0:T(8,128)(2,1)S(1)} %add_convert_fusion.1), channel_id=1, source_target_pairs={{0,4},{1,5},{2,6},{3,7},{4,0},{5,1},{6,2},{7,3},{8,12},{9,13},{10,... | collective-permute-start | bytes 491528 | tf_op jit(solution)/shard_map/ppermute | solution.py:19
  53.6 8.3 %collective-permute-start.13 = (bf16[64,1280]{1,0:T(8,128)(2,1)S(1)}, bf16[64,1280]{1,0:T(8,128)(2,1)S(1)}, u32[]{:S(2)}, u32[]{:S(2)}) collective-permute-start(bf16[64,1280]{1,0:T(8,128)(2,1)S(1)} %add_convert_fusion), channel_id=1, source_target_pairs={{0,28},{1,29},{2,30},{3,31},{4,8},{5,9},{6,10},{7,11},{8,4},{9,5},... | collective-permute-start | bytes 491528 | tf_op jit(solution)/shard_map/ppermute | solution.py:19
  57.8 4.0 %copy-start.10 = (bf16[64,1280]{1,0:T(8,128)(2,1)}, bf16[64,1280]{1,0:T(8,128)(2,1)S(1)}, u32[]{:S(2)}) copy-start(bf16[64,1280]{1,0:T(8,128)(2,1)S(1)} %collective-permute-done.9.across) | copy-start | bytes 491524
  57.8 4.0 %copy-start.11 = (bf16[64,1280]{1,0:T(8,128)(2,1)}, bf16[64,1280]{1,0:T(8,128)(2,1)S(1)}, u32[]{:S(2)}) copy-start(bf16[64,1280]{1,0:T(8,128)(2,1)S(1)} %collective-permute-done.11.even) | copy-start | bytes 491524
  61.8 0.7 %copy-start.12 = (bf16[64,1280]{1,0:T(8,128)(2,1)}, bf16[64,1280]{1,0:T(8,128)(2,1)S(1)}, u32[]{:S(2)}) copy-start(bf16[64,1280]{1,0:T(8,128)(2,1)S(1)} %collective-permute-done.13.odd) | copy-start | bytes 491524

commit v2 on v1

v2 whole, which is shorter than its diff:
```python
import functools

import jax
import jax.numpy as jnp
from jax import lax
from jax.experimental import pallas as pl
from jax.experimental.pallas import tpu as pltpu
from jax.sharding import PartitionSpec as P

CB = 2
AXES = ("slab", "cross")
PAD = 16


def exchange(value, slabs, parts, move):
    pairs = []
    for s in range(slabs):
        for c in range(parts):
            t, d = move(s, c)
            pairs.append((s * parts + c, t * parts + d))
    return lax.ppermute(value, AXES, pairs)


def moves(slabs, parts):
    def odd(s):
        t = s - 1 if s % 2 == 0 else s + 1
        return t if 0 <= t < slabs else s

    def across(c):
        d = c - 1 if c % 2 == 0 else c + 1
        return d if 0 <= d < parts else c

    return {
        "even": lambda s, c: (s ^ 1, c),
        "odd": lambda s, c: (odd(s), c),
        "pair": lambda s, c: (s, c ^ 1),
        "across": lambda s, c: (s, across(c)),
        "other": lambda s, c: (s, c ^ 2),
    }


def pack_kernel(cols, tiles, out, sem):
    blocks, kp, tile = tiles.shape[0], tiles.shape[1], tiles.shape[-1]
    copies = []
    for n in range(blocks):
        for m in range(kp):
            copies.append(
                pltpu.make_async_copy(
                    tiles.at[n, m], out.at[n, m * tile : (m + 1) * tile], sem.at[n * kp + m]
                )
            )
    for copy in copies:
        copy.start()
    lane = lax.broadcasted_iota(jnp.int32, (PAD, tile), 1)
    for n in range(blocks):
        row = jnp.zeros((PAD, tile), jnp.int32)
        for m in range(kp):
            row = jnp.where(lane == m, cols[n, m], row)
        out[n, kp * tile :] = row.astype(jnp.float32).astype(jnp.bfloat16)
    for copy in copies:
        copy.wait()


def columns_of(sources, cols_v, cols_s, sem):
    for slot, source in sources:
        blocks, tile = source.shape[0], source.shape[-1]
        for n in range(blocks):
            row = source[n, source.shape[1] - PAD :].astype(jnp.float32)
            cols_v[slot * blocks + n] = row[:8].astype(jnp.int32)
    copy = pltpu.make_async_copy(cols_v, cols_s, sem)
    copy.start()
    return copy


def prepare_kernel(kp, own, mate, out, cols_v, cols_s, sem):
    blocks, tile = own.shape[0], own.shape[-1]
    half = tile // 2
    copy = columns_of(((0, own), (1, mate)), cols_v, cols_s, sem)
    part = lax.axis_index("cross")
    slab = lax.axis_index("slab")
    lower = lax.rem(part, 2) == 0
    side = lax.div(part, 2)
    even = lax.rem(slab, 2)
    out[...] = jnp.zeros_like(out)
    copy.wait()
    for d, source in enumerate((own, mate)):
        for n in range(blocks):
            for m in range(kp):
                piece = source[n, m * tile : (m + 1) * tile, :]
                piece = jnp.where(lower, piece[:, :half], piece[:, half:])
                at = (d * blocks + n) * tile
                q = cols_s[d * blocks + n, 0, m]
                block, owner = lax.div(q, CB), lax.rem(q, CB)
                to_even = (block == 2) == (even == 0)
                place = jnp.where(block == 1, 2, jnp.where(to_even, 1, 0))
                place += jnp.where(owner == side, 3, 0)
                out[place, :, at : at + tile] = piece.T


def product_kernel(slabs, parts, a_cols, over_rows, over_cols, *refs):
    sources = refs[:9]
    a_tiles, over_tiles, out, ext, acc, cols_v, cols_s, sem = refs[9:]
    blocks, taps, tile = a_tiles.shape[0], a_tiles.shape[1], a_tiles.shape[-1]
    kp = ext.shape[-1] // tile
    slab = lax.axis_index("slab")
    part = lax.axis_index("cross")
    r_even = 2 - 2 * lax.rem(slab, 2)
    u_pair = 2 - 2 * lax.rem(part, 2)
    r_odd, u_across = 2 - r_even, 2 - u_pair
    r_there = slab + r_odd - 1
    u_there = part + u_across - 1
    odd_ok = (r_there >= 0) & (r_there < slabs)
    across_ok = (u_there >= 0) & (u_there < parts)
    slots = [(3 * r + u) for r in (1, r_even, r_odd) for u in (1, u_pair, u_across)]
    valid = [
        None, None, across_ok, None, None, across_ok, odd_ok, odd_ok, odd_ok & across_ok
    ]
    copy = columns_of(list(zip(slots, sources)), cols_v, cols_s, sem)
    for slot, ok, source in zip(slots, valid, sources):
        for n in range(blocks):
            for m in range(kp):
                piece = source[n, m * tile : (m + 1) * tile, :]
                if ok is not None:
                    piece = jnp.where(ok, piece, jnp.zeros_like(piece))
                ext[slot * blocks + n, :, m * tile : (m + 1) * tile] = piece
    acc[...] = jnp.zeros_like(acc)
    copy.wait()

    def add(n, col, matrix):
        piece = jnp.dot(matrix, ext[col], preferred_element_type=jnp.float32)
        shift = (col // (3 * blocks)) * CB
        for m in range(kp):
            j = shift + cols_s[col, 0, m]
            acc[n, j] += piece[:, m * tile : (m + 1) * tile]

    for n in range(blocks):
        for k in range(taps):
            add(n, a_cols[n, k], a_tiles[n, k])
    for o in range(over_tiles.shape[0]):
        add(over_rows[o], over_cols[o], over_tiles[o])
    for n in range(blocks):
        for j in range(acc.shape[1]):
            out[n * tile : (n + 1) * tile, j * tile : (j + 1) * tile] = acc[n, j].astype(
                jnp.bfloat16
            )


def partial_kernel(left, own, mate, *outs):
    count, half = left.shape[0], left.shape[1]
    rows = own.shape[0]
    for i in range(count):
        block = left[i]
        total = jnp.dot(block[:, :rows], own[...], preferred_element_type=jnp.float32)
        total += jnp.dot(block[:, rows:], mate[...], preferred_element_type=jnp.float32)
        outs[i][...] = total.astype(outs[i].dtype)


def final_kernel(slabs, own, across, even, odd, out):
    width = (out.shape[1] - own.shape[1]) // 2
    span = own.shape[1]
    slab = lax.axis_index("slab")
    first = lax.rem(slab, 2) == 0
    there = jnp.where(first, slab - 1, slab + 1)
    ok = (there >= 0) & (there < slabs)
    odd_value = jnp.where(ok, odd[...].astype(jnp.float32), 0.0)
    even_value = even[...].astype(jnp.float32)
    lower = jnp.where(first, odd_value, even_value)
    upper = jnp.where(first, even_value, odd_value)
    middle = own[...] + across[...].astype(jnp.float32)
    out[...] = jnp.zeros_like(out)
    out[:, :span] = lower
    out[:, width : width + span] += middle
    out[:, 2 * width : 2 * width + span] += upper


def vmem(count):
    return [pl.BlockSpec(memory_space=pltpu.VMEM)] * count


def smem(count):
    return [pl.BlockSpec(memory_space=pltpu.SMEM)] * count


def cost(flops, size):
    return pl.CostEstimate(flops=flops, bytes_accessed=size, transcendentals=0)


def grant(mib):
    return pltpu.CompilerParams(vmem_limit_bytes=mib << 20)


def fast_body(slabs, parts, a_tiles, a_cols, over_tiles, over_rows, over_cols, p_tiles, p_cols):
    blocks, kp, tile = p_tiles.shape[0], p_tiles.shape[1], p_tiles.shape[-1]
    width = CB * tile
    span = blocks * tile
    half = tile // 2
    step = moves(slabs, parts)

    def send(value, name):
        return exchange(value, slabs, parts, step[name])

    def column_scratch(count):
        return [
            pltpu.VMEM((count * blocks, 8, tile), jnp.int32),
            pltpu.SMEM((count * blocks, 8, tile), jnp.int32),
            pltpu.SemaphoreType.DMA,
        ]

    own = pl.pallas_call(
        pack_kernel,
        out_shape=jax.ShapeDtypeStruct((blocks, kp * tile + PAD, tile), jnp.bfloat16),
        in_specs=smem(1) + [pl.BlockSpec(memory_space=pl.ANY)],
        out_specs=vmem(1)[0],
        scratch_shapes=[pltpu.SemaphoreType.DMA((blocks * kp,))],
        compiler_params=grant(2),
        cost_estimate=cost(0, 1 << 19),
        name="pack",
    )(p_cols, p_tiles)
    even = send(own, "even")
    odd = send(own, "odd")
    mate = send(own, "pair")
    own_x = send(own, "across")
    left = pl.pallas_call(
        functools.partial(prepare_kernel, kp),
        out_shape=jax.ShapeDtypeStruct((3 * CB, half, 2 * span), jnp.bfloat16),
        in_specs=vmem(2),
        out_specs=vmem(1)[0],
        scratch_shapes=column_scratch(2),
        compiler_params=grant(4),
        cost_estimate=cost(0, 1 << 20),
        name="prepare",
    )(own, mate)
    even, left = lax.optimization_barrier((even, left))
    even_p, odd_p = send(even, "pair"), send(odd, "pair")
    even_x, odd_x = send(even, "across"), send(odd, "across")
    product = pl.pallas_call(
        functools.partial(product_kernel, slabs, parts),
        out_shape=jax.ShapeDtypeStruct((span, 5 * width), jnp.bfloat16),
        in_specs=smem(3) + vmem(11),
        out_specs=vmem(1)[0],
        scratch_shapes=[
            pltpu.VMEM((9 * blocks, tile, kp * tile), jnp.bfloat16),
            pltpu.VMEM((blocks, 5 * CB, tile, tile), jnp.float32),
        ]
        + column_scratch(9),
        compiler_params=grant(12),
        cost_estimate=cost(1 << 29, 1 << 22),
        name="product",
    )(
        a_cols, over_rows, over_cols,
        own, mate, own_x, even, even_p, even_x, odd, odd_p, odd_x,
        a_tiles, over_tiles,
    )
    product_mate = send(product, "pair")

    kinds = [jnp.bfloat16] * 3 + [jnp.float32] * 3
    x_odd, x_even, x_own, b_odd, b_even, b_own = pl.pallas_call(
        partial_kernel,
        out_shape=[jax.ShapeDtypeStruct((half, 5 * width), kind) for kind in kinds],
        in_specs=vmem(3),
        out_specs=vmem(6),
        compiler_params=grant(8),
        cost_estimate=cost(1 << 29, 1 << 22),
        name="partial",
    )(left, product, product_mate)
    g_odd = send(x_odd, "other")
    g_even = send(x_even, "other")
    g_odd, x_own = lax.optimization_barrier((g_odd, x_own))
    s_odd = send((b_odd + g_odd.astype(jnp.float32)).astype(jnp.bfloat16), "odd")
    g_own = send(x_own, "other")
    s_even = send((b_even + g_even.astype(jnp.float32)).astype(jnp.bfloat16), "even")
    return pl.pallas_call(
        functools.partial(final_kernel, slabs),
        out_shape=jax.ShapeDtypeStruct((half, 7 * width), jnp.float32),
        in_specs=vmem(4),
        out_specs=vmem(1)[0],
        compiler_params=grant(4),
        name="final",
    )(b_own, g_own, s_even, s_odd)


SPECS = (
    P(AXES, None, None, None),
    P(AXES, None),
    P(AXES, None, None),
    P(AXES),
    P(AXES),
    P(AXES, None, None, None),
    P(AXES, None),
)


def solution(mesh):
    slabs, parts = mesh.shape["slab"], mesh.shape["cross"]

    def body(*args):
        return fast_body(slabs, parts, *args)

    return jax.shard_map(
        body, mesh=mesh, in_specs=SPECS, out_specs=P(AXES, None), check_vma=False
    )
```

time: 65 us -> 52.1 us (0.80)
  starting transfers between devices: 26.8 us -> 20.3 us
  waiting for transfers between devices: 15.7 us -> 21.5 us
  Pallas kernels: 13.6 us -> 8.22 us
  other arithmetic: 5.18 us -> 0.06 us
  local copies, waits for them, and re-layouts: 3.23 us -> 1.64 us
    ppermute x14, starting transfers between devices: 26.8 us -> 20.3 us  [exchange(): return lax.ppermute(value, AXES, pairs)]
    ppermute x14, waiting for transfers between devices: 15.7 us -> 21.5 us  [exchange(): return lax.ppermute(value, AXES, pairs)]
    pallas_call x3 -> x4, Pallas kernels: 9.99 us -> 6.74 us  [the longest x1 3.42 us: fast_body(): pl.pallas_call(functools.partial(product_kernel, slabs, parts), out_shape...]
    pallas_call x1, Pallas kernels: 3.61 us -> 1.49 us  [fast_body(): pl.pallas_call(partial_kernel, out_shape=[jax.ShapeDtypeStruct((half, 5 *...]
    concatenate x2 -> x0, other arithmetic: 1.53 us -> none  [the longest x1 0.94 us: fast_body(): jnp.concatenate([p_tiles.reshape(blocks, kp * tile, tile), cols], axis=1)]
    another operation x2 -> x0, other arithmetic: 1.29 us -> none
    convert_element_type x1 -> x0, other arithmetic: 1.26 us -> none  [fast_body(): mate_cols = mate[:, kp * tile, :kp].astype(jnp.int32)]
    convert_element_type x1, other arithmetic: 1.06 us -> 0.03 us  [fast_body(): (b_even + g_even.astype(jnp.float32)).astype(jnp.bfloat16)]
  transfers between devices with their start and end apart: 14 -> 14, of which waited for: 6 -> 6; matrix products, arithmetic and copies ran while one was open for 6% -> 0% of each run, Pallas kernels for 4% -> 3%
where the time goes in v2:
time: 52.1 us; the launch traced here: 51.9 us
  waiting for transfers between devices  21.5 us (41%)
  starting transfers between devices  20.3 us (39%)
  Pallas kernels  8.22 us (16%)
  local copies, waits for them, and re-layouts  1.64 us (3%)
    ppermute x14, waiting for transfers between devices, exchange(): return lax.ppermute(value, AXES, pairs)  21.5 us
    ppermute x14, starting transfers between devices, exchange(): return lax.ppermute(value, AXES, pairs)  20.3 us
    pallas_call x1, Pallas kernels, fast_body(): pl.pallas_call(functools.partial(product_kernel, slabs, parts), out_shape...  3.42 us
    unnamed x14, local copies, waits for them, and re-layouts  1.64 us
    pallas_call x1, Pallas kernels, fast_body(): pl.pallas_call(functools.partial(prepare_kernel, kp), out_shape=jax.Shape...  1.5 us
    pallas_call x1, Pallas kernels, fast_body(): pl.pallas_call(partial_kernel, out_shape=[jax.ShapeDtypeStruct((half, 5 *...  1.49 us
  transfers between devices with their start and end apart: 14, of which 6 were waited for; matrix products, arithmetic and copies ran while one was open for 0% of the time, Pallas kernels for 3%

profile of v2, /device:TPU:0, one launch (start us, length us, event | category | flops | bytes accessed | tf_op | source)
XLA Modules:
  0.0 51.9 jit_solution(4252762197014687730)
XLA Ops:
  0.0 0.9 %copy-done.1 = bf16[2,3,128,128]{3,2,1,0:T(8,128)(2,1)S(1)} copy-done((bf16[2,3,128,128]{3,2,1,0:T(8,128)(2,1)S(1)}, bf16[2,3,128,128]{3,2,1,0:T(8,128)(2,1)}, u32[]{:S(2)}) %copy-start.1) | copy-done | bytes 196632
  0.9 0.7 %copy-done.3 = s32[2,3]{1,0:T(2,128)S(1)} copy-done((s32[2,3]{1,0:T(2,128)S(1)}, s32[2,3]{1,0:T(2,128)}, u32[]{:S(2)}) %copy-start.3) | copy-done | bytes 48
  1.6 0.9 %pack.1.own.refs_0_ = bf16[2,400,128]{2,1,0:T(8,128)(2,1)S(1)} custom-call(s32[2,3]{1,0:T(2,128)S(1)} %copy-done.3, bf16[2,3,128,128]{3,2,1,0:T(8,128)(2,1)S(1)} %copy-done.1), custom_call_target="tpu_custom_call" | custom-call | bytes 524288 | tf_op jit(solution)/shard_map/pack/pallas_call | solution.py:209
  2.5 0.0 copy-start
  2.5 0.0 copy-start.2
  2.5 0.0 copy-start.4
  2.5 0.0 copy-start.5
  2.5 0.0 copy-start.6
  2.5 0.6 %collective-permute-start.1 = (bf16[2,400,128]{2,1,0:T(8,128)(2,1)S(1)}, bf16[2,400,128]{2,1,0:T(8,128)(2,1)S(1)}, u32[]{:S(2)}, u32[]{:S(2)}) collective-permute-start(bf16[2,400,128]{2,1,0:T(8,128)(2,1)S(1)} %pack.1.own.refs_0_), channel_id=1, source_target_pairs={{0,1},{1,0},{2,3},{3,2},{4,5},{5,4},{6,7},{7,6},{8,9},{9,8},{10,11... | collective-permute-start | bytes 614408 | tf_op jit(solution)/shard_map/ppermute | solution.py:21
  3.1 2.6 %collective-permute-start = (bf16[2,400,128]{2,1,0:T(8,128)(2,1)S(1)}, bf16[2,400,128]{2,1,0:T(8,128)(2,1)S(1)}, u32[]{:S(2)}, u32[]{:S(2)}) collective-permute-start(bf16[2,400,128]{2,1,0:T(8,128)(2,1)S(1)} %pack.1.own.refs_0_), channel_id=1, source_target_pairs={{0,4},{1,5},{2,6},{3,7},{4,0},{5,1},{6,2},{7,3},{8,12},{9,13},{10,... | collective-permute-start | bytes 614408 | tf_op jit(solution)/shard_map/ppermute | solution.py:21
  5.7 0.7 %collective-permute-start.5 = (bf16[2,400,128]{2,1,0:T(8,128)(2,1)S(1)}, bf16[2,400,128]{2,1,0:T(8,128)(2,1)S(1)}, u32[]{:S(2)}, u32[]{:S(2)}) collective-permute-start(bf16[2,400,128]{2,1,0:T(8,128)(2,1)S(1)} %pack.1.own.refs_0_), channel_id=1, source_target_pairs={{0,0},{1,1},{2,2},{3,3},{4,8},{5,9},{6,10},{7,11},{8,4},{9,5},{10,... | collective-permute-start | bytes 614408 | tf_op jit(solution)/shard_map/ppermute | solution.py:21
  6.4 0.7 %collective-permute-start.2 = (bf16[2,400,128]{2,1,0:T(8,128)(2,1)S(1)}, bf16[2,400,128]{2,1,0:T(8,128)(2,1)S(1)}, u32[]{:S(2)}, u32[]{:S(2)}) collective-permute-start(bf16[2,400,128]{2,1,0:T(8,128)(2,1)S(1)} %pack.1.own.refs_0_), channel_id=1, source_target_pairs={{0,0},{1,2},{2,1},{3,3},{4,4},{5,6},{6,5},{7,7},{8,8},{9,10},{10,9... | collective-permute-start | bytes 614408 | tf_op jit(solution)/shard_map/ppermute | solution.py:21
  7.1 1.5 %prepare.1.left = bf16[6,64,512]{2,1,0:T(8,128)(2,1)S(1)} custom-call(bf16[2,400,128]{2,1,0:T(8,128)(2,1)S(1)} %pack.1.own.refs_0_, bf16[2,400,128]{2,1,0:T(8,128)(2,1)S(1)} %collective-permute-done.1.mate.refs_1_), custom_call_target="tpu_custom_call" | custom-call | bytes 1048576 | tf_op jit(solution)/shard_map/prepare/pallas_call | solution.py:223
  8.6 6.5 %collective-permute-done.refs_3_ = bf16[2,400,128]{2,1,0:T(8,128)(2,1)S(1)} collective-permute-done((bf16[2,400,128]{2,1,0:T(8,128)(2,1)S(1)}, bf16[2,400,128]{2,1,0:T(8,128)(2,1)S(1)}, u32[]{:S(2)}, u32[]{:S(2)}) %collective-permute-start) | collective-permute-done | bytes 204832 | tf_op jit(solution)/shard_map/ppermute | solution.py:21
  15.0 0.7 %collective-permute-start.7 = (bf16[2,400,128]{2,1,0:T(8,128)(2,1)S(1)}, bf16[2,400,128]{2,1,0:T(8,128)(2,1)S(1)}, u32[]{:S(2)}, u32[]{:S(2)}) collective-permute-start(bf16[2,400,128]{2,1,0:T(8,128)(2,1)S(1)} %collective-permute-done.5.refs_6_), channel_id=1, source_target_pairs={{0,0},{1,2},{2,1},{3,3},{4,4},{5,6},{6,5},{7,7},{8,8},{9,10},{10,9... | collective-permute-start | bytes 614408 | tf_op jit(solution)/shard_map/ppermute | solution.py:21
  15.7 2.9 %collective-permute-start.6 = (bf16[2,400,128]{2,1,0:T(8,128)(2,1)S(1)}, bf16[2,400,128]{2,1,0:T(8,128)(2,1)S(1)}, u32[]{:S(2)}, u32[]{:S(2)}) collective-permute-start(bf16[2,400,128]{2,1,0:T(8,128)(2,1)S(1)} %collective-permute-done.5.refs_6_), channel_id=1, source_target_pairs={{0,1},{1,0},{2,3},{3,2},{4,5},{5,4},{6,7},{7,6},{8,9},{9,8},{10,11... | collective-permute-start | bytes 614408 | tf_op jit(solution)/shard_map/ppermute | solution.py:21
  18.6 0.7 %collective-permute-start.4 = (bf16[2,400,128]{2,1,0:T(8,128)(2,1)S(1)}, bf16[2,400,128]{2,1,0:T(8,128)(2,1)S(1)}, u32[]{:S(2)}, u32[]{:S(2)}) collective-permute-start(bf16[2,400,128]{2,1,0:T(8,128)(2,1)S(1)} %collective-permute-done.refs_3_), channel_id=1, source_target_pairs={{0,0},{1,2},{2,1},{3,3},{4,4},{5,6},{6,5},{7,7},{8,8},{9,10},{10,9... | collective-permute-start | bytes 614408 | tf_op jit(solution)/shard_map/ppermute | solution.py:21
  19.3 1.3 %collective-permute-start.3 = (bf16[2,400,128]{2,1,0:T(8,128)(2,1)S(1)}, bf16[2,400,128]{2,1,0:T(8,128)(2,1)S(1)}, u32[]{:S(2)}, u32[]{:S(2)}) collective-permute-start(bf16[2,400,128]{2,1,0:T(8,128)(2,1)S(1)} %collective-permute-done.refs_3_), channel_id=1, source_target_pairs={{0,1},{1,0},{2,3},{3,2},{4,5},{5,4},{6,7},{7,6},{8,9},{9,8},{10,11... | collective-permute-start | bytes 614408 | tf_op jit(solution)/shard_map/ppermute | solution.py:21
  20.6 1.1 %collective-permute-done.3.refs_4_ = bf16[2,400,128]{2,1,0:T(8,128)(2,1)S(1)} collective-permute-done((bf16[2,400,128]{2,1,0:T(8,128)(2,1)S(1)}, bf16[2,400,128]{2,1,0:T(8,128)(2,1)S(1)}, u32[]{:S(2)}, u32[]{:S(2)}) %collective-permute-start.3) | collective-permute-done | bytes 204832 | tf_op jit(solution)/shard_map/ppermute | solution.py:21
  21.7 3.4 %product.1.own = bf16[256,1280]{1,0:T(8,128)(2,1)S(1)} custom-call(s32[2,7]{1,0:T(2,128)S(1)} %copy-done.4, s32[4]{0:T(128)S(1)} %copy-done.5, s32[4]{0:T(128)S(1)} %copy-done.6, bf16[2,400,128]{2,1,0:T(8,128)(2,1)S(1)} %pack.1.own.refs_0_, bf16[2,400,128]{2,1,0:T(8,128)(2,1)S(1)} %collective-permute-done.1.mate.refs_1_, ...), custom_call_target="tpu_custom_call" | custom-call | flops 536870912 | bytes 4194304 | tf_op jit(solution)/shard_map/product/pallas_call | solution.py:236
  25.1 4.1 %collective-permute-start.8 = (bf16[256,1280]{1,0:T(8,128)(2,1)S(1)}, bf16[256,1280]{1,0:T(8,128)(2,1)S(1)}, u32[]{:S(2)}, u32[]{:S(2)}) collective-permute-start(bf16[256,1280]{1,0:T(8,128)(2,1)S(1)} %product.1.own), channel_id=1, source_target_pairs={{0,1},{1,0},{2,3},{3,2},{4,5},{5,4},{6,7},{7,6},{8,9},{9,8},{10,11... | collective-permute-start | bytes 1966088 | tf_op jit(solution)/shard_map/ppermute | solution.py:21
  29.2 1.7 %collective-permute-done.8.mate = bf16[256,1280]{1,0:T(8,128)(2,1)S(1)} collective-permute-done((bf16[256,1280]{1,0:T(8,128)(2,1)S(1)}, bf16[256,1280]{1,0:T(8,128)(2,1)S(1)}, u32[]{:S(2)}, u32[]{:S(2)}) %collective-permute-start.8) | collective-permute-done | bytes 655392 | tf_op jit(solution)/shard_map/ppermute | solution.py:21
  30.9 1.5 %partial.1 = (bf16[64,1280]{1,0:T(8,128)(2,1)S(1)}, bf16[64,1280]{1,0:T(8,128)(2,1)S(1)}, bf16[64,1280]{1,0:T(8,128)(2,1)S(1)}, f32[64,1280]{1,0:T(8,128)S(1)}, ...) custom-call(bf16[6,64,512]{2,1,0:T(8,128)(2,1)S(1)} %prepare.1.left, bf16[256,1280]{1,0:T(8,128)(2,1)S(1)} %product.1.own, ...), custom_call_target="tpu_custom_call" | custom-call | flops 536870912 | bytes 4194304 | tf_op jit(solution)/shard_map/partial/pallas_call | solution.py:257
  32.4 0.5 %collective-permute-start.9 = (bf16[64,1280]{1,0:T(8,128)(2,1)S(1)}, bf16[64,1280]{1,0:T(8,128)(2,1)S(1)}, u32[]{:S(2)}, u32[]{:S(2)}) collective-permute-start(bf16[64,1280]{1,0:T(8,128)(2,1)S(1)} %get-tuple-element.18), channel_id=1, source_target_pairs={{0,2},{1,3},{2,0},{3,1},{4,6},{5,7},{6,4},{7,5},{8,10},{9,11},{10,... | collective-permute-start | bytes 491528 | tf_op jit(solution)/shard_map/ppermute | solution.py:21
  33.0 1.6 %collective-permute-start.11 = (bf16[64,1280]{1,0:T(8,128)(2,1)S(1)}, bf16[64,1280]{1,0:T(8,128)(2,1)S(1)}, u32[]{:S(2)}, u32[]{:S(2)}) collective-permute-start(bf16[64,1280]{1,0:T(8,128)(2,1)S(1)} %get-tuple-element.22), channel_id=1, source_target_pairs={{0,2},{1,3},{2,0},{3,1},{4,6},{5,7},{6,4},{7,5},{8,10},{9,11},{10,... | collective-permute-start | bytes 491528 | tf_op jit(solution)/shard_map/ppermute | solution.py:21
  34.5 5.0 %collective-permute-done.9 = bf16[64,1280]{1,0:T(8,128)(2,1)S(1)} collective-permute-done((bf16[64,1280]{1,0:T(8,128)(2,1)S(1)}, bf16[64,1280]{1,0:T(8,128)(2,1)S(1)}, u32[]{:S(2)}, u32[]{:S(2)}) %collective-permute-start.9) | collective-permute-done | bytes 163872 | tf_op jit(solution)/shard_map/ppermute | solution.py:21
  39.6 0.5 collective-permute-start.10
  40.1 0.7 %collective-permute-start.13 = (bf16[64,1280]{1,0:T(8,128)(2,1)S(1)}, bf16[64,1280]{1,0:T(8,128)(2,1)S(1)}, u32[]{:S(2)}, u32[]{:S(2)}) collective-permute-start(bf16[64,1280]{1,0:T(8,128)(2,1)S(1)} %add_convert_fusion), channel_id=1, source_target_pairs={{0,0},{1,1},{2,2},{3,3},{4,8},{5,9},{6,10},{7,11},{8,4},{9,5},{10,... | collective-permute-start | bytes 491528 | tf_op jit(solution)/shard_map/ppermute | solution.py:21
  40.7 2.3 %collective-permute-done.11 = bf16[64,1280]{1,0:T(8,128)(2,1)S(1)} collective-permute-done((bf16[64,1280]{1,0:T(8,128)(2,1)S(1)}, bf16[64,1280]{1,0:T(8,128)(2,1)S(1)}, u32[]{:S(2)}, u32[]{:S(2)}) %collective-permute-start.11) | collective-permute-done | bytes 163872 | tf_op jit(solution)/shard_map/ppermute | solution.py:21
  43.1 3.0 %collective-permute-start.12 = (bf16[64,1280]{1,0:T(8,128)(2,1)S(1)}, bf16[64,1280]{1,0:T(8,128)(2,1)S(1)}, u32[]{:S(2)}, u32[]{:S(2)}) collective-permute-start(bf16[64,1280]{1,0:T(8,128)(2,1)S(1)} %add_convert_fusion.1), channel_id=1, source_target_pairs={{0,4},{1,5},{2,6},{3,7},{4,0},{5,1},{6,2},{7,3},{8,12},{9,13},{10,... | collective-permute-start | bytes 491528 | tf_op jit(solution)/shard_map/ppermute | solution.py:21
  46.1 4.8 %collective-permute-done.12.even = bf16[64,1280]{1,0:T(8,128)(2,1)S(1)} collective-permute-done((bf16[64,1280]{1,0:T(8,128)(2,1)S(1)}, bf16[64,1280]{1,0:T(8,128)(2,1)S(1)}, u32[]{:S(2)}, u32[]{:S(2)}) %collective-permute-start.12) | collective-permute-done | bytes 163872 | tf_op jit(solution)/shard_map/ppermute | solution.py:21
  50.9 0.9 %final.1 = f32[64,1792]{1,0:T(8,128)} custom-call(f32[64,1280]{1,0:T(8,128)S(1)} %get-tuple-element.17.own, bf16[64,1280]{1,0:T(8,128)(2,1)S(1)} %collective-permute-done.10.across, bf16[64,1280]{1,0:T(8,128)(2,1)S(1)} %collective-permute-done.12.even, bf16[64,1280]{1,0:T(8,128)(2,1)S(1)} %collective-permute-done.13.odd), custom_call_target="tpu_custom_call" | custom-call | tf_op jit(solution)/shard_map/final/pallas_call | solution.py:272
  (17 shorter events, 0.1 us)
Async XLA Ops:
  0.0 0.9 %copy-start.1 = (bf16[2,3,128,128]{3,2,1,0:T(8,128)(2,1)S(1)}, bf16[2,3,128,128]{3,2,1,0:T(8,128)(2,1)}, u32[]{:S(2)}) copy-start(bf16[2,3,128,128]{3,2,1,0:T(8,128)(2,1)} %tiles.1) | copy-start | bytes 589828
  0.9 0.7 %copy-start.3 = (s32[2,3]{1,0:T(2,128)S(1)}, s32[2,3]{1,0:T(2,128)}, u32[]{:S(2)}) copy-start(s32[2,3]{1,0:T(2,128)} %cols.1) | copy-start | bytes 76
  2.5 19.2 %copy-start = (bf16[2,7,128,128]{3,2,1,0:T(8,128)(2,1)S(1)}, bf16[2,7,128,128]{3,2,1,0:T(8,128)(2,1)}, u32[]{:S(2)}) copy-start(bf16[2,7,128,128]{3,2,1,0:T(8,128)(2,1)} %refs_9_.1) | copy-start | bytes 1376260
  2.5 19.2 %copy-start.2 = (bf16[4,128,128]{2,1,0:T(8,128)(2,1)S(1)}, bf16[4,128,128]{2,1,0:T(8,128)(2,1)}, u32[]{:S(2)}) copy-start(bf16[4,128,128]{2,1,0:T(8,128)(2,1)} %refs_10_.1) | copy-start | bytes 393220
  2.5 19.2 %copy-start.4 = (s32[2,7]{1,0:T(2,128)S(1)}, s32[2,7]{1,0:T(2,128)}, u32[]{:S(2)}) copy-start(s32[2,7]{1,0:T(2,128)} %a_cols.1) | copy-start | bytes 172
  2.5 19.2 %copy-start.5 = (s32[4]{0:T(128)S(1)}, s32[4]{0:T(128)}, u32[]{:S(2)}) copy-start(s32[4]{0:T(128)} %over_rows.1) | copy-start | bytes 52
  2.5 19.2 %copy-start.6 = (s32[4]{0:T(128)S(1)}, s32[4]{0:T(128)}, u32[]{:S(2)}) copy-start(s32[4]{0:T(128)} %over_cols.1) | copy-start | bytes 52
  2.5 4.5 %collective-permute-start.1 = (bf16[2,400,128]{2,1,0:T(8,128)(2,1)S(1)}, bf16[2,400,128]{2,1,0:T(8,128)(2,1)S(1)}, u32[]{:S(2)}, u32[]{:S(2)}) collective-permute-start(bf16[2,400,128]{2,1,0:T(8,128)(2,1)S(1)} %pack.1.own.refs_0_), channel_id=1, source_target_pairs={{0,1},{1,0},{2,3},{3,2},{4,5},{5,4},{6,7},{7,6},{8,9},{9,8},{10,11... | collective-permute-start | bytes 614408 | tf_op jit(solution)/shard_map/ppermute | solution.py:21
  3.1 11.9 %collective-permute-start = (bf16[2,400,128]{2,1,0:T(8,128)(2,1)S(1)}, bf16[2,400,128]{2,1,0:T(8,128)(2,1)S(1)}, u32[]{:S(2)}, u32[]{:S(2)}) collective-permute-start(bf16[2,400,128]{2,1,0:T(8,128)(2,1)S(1)} %pack.1.own.refs_0_), channel_id=1, source_target_pairs={{0,4},{1,5},{2,6},{3,7},{4,0},{5,1},{6,2},{7,3},{8,12},{9,13},{10,... | collective-permute-start | bytes 614408 | tf_op jit(solution)/shard_map/ppermute | solution.py:21
  5.7 9.3 %collective-permute-start.5 = (bf16[2,400,128]{2,1,0:T(8,128)(2,1)S(1)}, bf16[2,400,128]{2,1,0:T(8,128)(2,1)S(1)}, u32[]{:S(2)}, u32[]{:S(2)}) collective-permute-start(bf16[2,400,128]{2,1,0:T(8,128)(2,1)S(1)} %pack.1.own.refs_0_), channel_id=1, source_target_pairs={{0,0},{1,1},{2,2},{3,3},{4,8},{5,9},{6,10},{7,11},{8,4},{9,5},{10,... | collective-permute-start | bytes 614408 | tf_op jit(solution)/shard_map/ppermute | solution.py:21
  6.4 14.2 %collective-permute-start.2 = (bf16[2,400,128]{2,1,0:T(8,128)(2,1)S(1)}, bf16[2,400,128]{2,1,0:T(8,128)(2,1)S(1)}, u32[]{:S(2)}, u32[]{:S(2)}) collective-permute-start(bf16[2,400,128]{2,1,0:T(8,128)(2,1)S(1)} %pack.1.own.refs_0_), channel_id=1, source_target_pairs={{0,0},{1,2},{2,1},{3,3},{4,4},{5,6},{6,5},{7,7},{8,8},{9,10},{10,9... | collective-permute-start | bytes 614408 | tf_op jit(solution)/shard_map/ppermute | solution.py:21
  15.0 5.6 %collective-permute-start.7 = (bf16[2,400,128]{2,1,0:T(8,128)(2,1)S(1)}, bf16[2,400,128]{2,1,0:T(8,128)(2,1)S(1)}, u32[]{:S(2)}, u32[]{:S(2)}) collective-permute-start(bf16[2,400,128]{2,1,0:T(8,128)(2,1)S(1)} %collective-permute-done.5.refs_6_), channel_id=1, source_target_pairs={{0,0},{1,2},{2,1},{3,3},{4,4},{5,6},{6,5},{7,7},{8,8},{9,10},{10,9... | collective-permute-start | bytes 614408 | tf_op jit(solution)/shard_map/ppermute | solution.py:21
  15.7 4.9 %collective-permute-start.6 = (bf16[2,400,128]{2,1,0:T(8,128)(2,1)S(1)}, bf16[2,400,128]{2,1,0:T(8,128)(2,1)S(1)}, u32[]{:S(2)}, u32[]{:S(2)}) collective-permute-start(bf16[2,400,128]{2,1,0:T(8,128)(2,1)S(1)} %collective-permute-done.5.refs_6_), channel_id=1, source_target_pairs={{0,1},{1,0},{2,3},{3,2},{4,5},{5,4},{6,7},{7,6},{8,9},{9,8},{10,11... | collective-permute-start | bytes 614408 | tf_op jit(solution)/shard_map/ppermute | solution.py:21
  18.6 2.0 %collective-permute-start.4 = (bf16[2,400,128]{2,1,0:T(8,128)(2,1)S(1)}, bf16[2,400,128]{2,1,0:T(8,128)(2,1)S(1)}, u32[]{:S(2)}, u32[]{:S(2)}) collective-permute-start(bf16[2,400,128]{2,1,0:T(8,128)(2,1)S(1)} %collective-permute-done.refs_3_), channel_id=1, source_target_pairs={{0,0},{1,2},{2,1},{3,3},{4,4},{5,6},{6,5},{7,7},{8,8},{9,10},{10,9... | collective-permute-start | bytes 614408 | tf_op jit(solution)/shard_map/ppermute | solution.py:21
  19.3 2.4 %collective-permute-start.3 = (bf16[2,400,128]{2,1,0:T(8,128)(2,1)S(1)}, bf16[2,400,128]{2,1,0:T(8,128)(2,1)S(1)}, u32[]{:S(2)}, u32[]{:S(2)}) collective-permute-start(bf16[2,400,128]{2,1,0:T(8,128)(2,1)S(1)} %collective-permute-done.refs_3_), channel_id=1, source_target_pairs={{0,1},{1,0},{2,3},{3,2},{4,5},{5,4},{6,7},{7,6},{8,9},{9,8},{10,11... | collective-permute-start | bytes 614408 | tf_op jit(solution)/shard_map/ppermute | solution.py:21
  25.1 5.8 %collective-permute-start.8 = (bf16[256,1280]{1,0:T(8,128)(2,1)S(1)}, bf16[256,1280]{1,0:T(8,128)(2,1)S(1)}, u32[]{:S(2)}, u32[]{:S(2)}) collective-permute-start(bf16[256,1280]{1,0:T(8,128)(2,1)S(1)} %product.1.own), channel_id=1, source_target_pairs={{0,1},{1,0},{2,3},{3,2},{4,5},{5,4},{6,7},{7,6},{8,9},{9,8},{10,11... | collective-permute-start | bytes 1966088 | tf_op jit(solution)/shard_map/ppermute | solution.py:21
  32.4 7.1 %collective-permute-start.9 = (bf16[64,1280]{1,0:T(8,128)(2,1)S(1)}, bf16[64,1280]{1,0:T(8,128)(2,1)S(1)}, u32[]{:S(2)}, u32[]{:S(2)}) collective-permute-start(bf16[64,1280]{1,0:T(8,128)(2,1)S(1)} %get-tuple-element.18), channel_id=1, source_target_pairs={{0,2},{1,3},{2,0},{3,1},{4,6},{5,7},{6,4},{7,5},{8,10},{9,11},{10,... | collective-permute-start | bytes 491528 | tf_op jit(solution)/shard_map/ppermute | solution.py:21
  33.0 10.1 %collective-permute-start.11 = (bf16[64,1280]{1,0:T(8,128)(2,1)S(1)}, bf16[64,1280]{1,0:T(8,128)(2,1)S(1)}, u32[]{:S(2)}, u32[]{:S(2)}) collective-permute-start(bf16[64,1280]{1,0:T(8,128)(2,1)S(1)} %get-tuple-element.22), channel_id=1, source_target_pairs={{0,2},{1,3},{2,0},{3,1},{4,6},{5,7},{6,4},{7,5},{8,10},{9,11},{10,... | collective-permute-start | bytes 491528 | tf_op jit(solution)/shard_map/ppermute | solution.py:21
  39.6 6.5 %collective-permute-start.10 = (bf16[64,1280]{1,0:T(8,128)(2,1)S(1)}, bf16[64,1280]{1,0:T(8,128)(2,1)S(1)}, u32[]{:S(2)}, u32[]{:S(2)}) collective-permute-start(bf16[64,1280]{1,0:T(8,128)(2,1)S(1)} %get-tuple-element.20), channel_id=1, source_target_pairs={{0,2},{1,3},{2,0},{3,1},{4,6},{5,7},{6,4},{7,5},{8,10},{9,11},{10,... | collective-permute-start | bytes 491528 | tf_op jit(solution)/shard_map/ppermute | solution.py:21
  40.1 6.0 %collective-permute-start.13 = (bf16[64,1280]{1,0:T(8,128)(2,1)S(1)}, bf16[64,1280]{1,0:T(8,128)(2,1)S(1)}, u32[]{:S(2)}, u32[]{:S(2)}) collective-permute-start(bf16[64,1280]{1,0:T(8,128)(2,1)S(1)} %add_convert_fusion), channel_id=1, source_target_pairs={{0,0},{1,1},{2,2},{3,3},{4,8},{5,9},{6,10},{7,11},{8,4},{9,5},{10,... | collective-permute-start | bytes 491528 | tf_op jit(solution)/shard_map/ppermute | solution.py:21
  43.1 7.8 %collective-permute-start.12 = (bf16[64,1280]{1,0:T(8,128)(2,1)S(1)}, bf16[64,1280]{1,0:T(8,128)(2,1)S(1)}, u32[]{:S(2)}, u32[]{:S(2)}) collective-permute-start(bf16[64,1280]{1,0:T(8,128)(2,1)S(1)} %add_convert_fusion.1), channel_id=1, source_target_pairs={{0,4},{1,5},{2,6},{3,7},{4,0},{5,1},{6,2},{7,3},{8,12},{9,13},{10,... | collective-permute-start | bytes 491528 | tf_op jit(solution)/shard_map/ppermute | solution.py:21

commit v3 on v2

v3 whole, which is shorter than its diff:
```python
import functools

import jax
import jax.numpy as jnp
from jax import lax
from jax.experimental import pallas as pl
from jax.experimental.pallas import tpu as pltpu
from jax.sharding import PartitionSpec as P


CB = 2
AXES = ("slab", "cross")
PAD = 16
PHASES = ((0, 1, 2, 3, 4, 5, 6, 7), (8,))


def exchange(value, slabs, parts, move):
    pairs = []
    for s in range(slabs):
        for c in range(parts):
            t, d = move(s, c)
            pairs.append((s * parts + c, t * parts + d))
    return lax.ppermute(value, AXES, pairs)


def moves(slabs, parts):
    stand_in = 2 if slabs % 4 == 0 else 1

    def odd(s, c):
        t = s - 1 if s % 2 == 0 else s + 1
        return (t, c) if 0 <= t < slabs else (s, c ^ 1)

    def across(s, c):
        d = c - 1 if c % 2 == 0 else c + 1
        return (s, d) if 0 <= d < parts else (s ^ stand_in, c)

    return {
        "even": lambda s, c: (s ^ 1, c),
        "even_other": lambda s, c: (s ^ 1, c ^ 2),
        "odd": odd,
        "pair": lambda s, c: (s, c ^ 1),
        "across": across,
        "other": lambda s, c: (s, c ^ 2),
    }


def pack(p_tiles, p_cols):
    blocks, kp, tile = p_tiles.shape[0], p_tiles.shape[1], p_tiles.shape[-1]
    cols = jnp.pad(p_cols, ((0, 0), (0, tile - kp)))[:, None, :]
    cols = jnp.broadcast_to(cols, (blocks, PAD, tile)).astype(jnp.bfloat16)
    return jnp.concatenate([p_tiles.reshape(blocks, kp * tile, tile), cols], axis=1)


def columns_of(sources, cols_v, cols_s, sem):
    for slot, source in sources:
        blocks = source.shape[0]
        for n in range(blocks):
            row = source[n, source.shape[1] - PAD :].astype(jnp.float32)
            cols_v[pl.ds(slot * blocks + n, 1)] = row[:1].astype(jnp.int32)
    copy = pltpu.make_async_copy(cols_v, cols_s, sem)
    copy.start()
    return copy


def prepare_kernel(kp, own, mate, out, cols_v, cols_s, sem):
    blocks, tile = own.shape[0], own.shape[-1]
    half = tile // 2
    copy = columns_of(((0, own), (1, mate)), cols_v, cols_s, sem)
    part = lax.axis_index("cross")
    slab = lax.axis_index("slab")
    lower = lax.rem(part, 2) == 0
    side = lax.div(part, 2)
    even = lax.rem(slab, 2)
    out[...] = jnp.zeros_like(out)
    copy.wait()
    for d, source in enumerate((own, mate)):
        for n in range(blocks):
            for m in range(kp):
                piece = source[n, m * tile : (m + 1) * tile, :]
                piece = jnp.where(lower, piece[:, :half], piece[:, half:])
                at = (d * blocks + n) * tile
                q = cols_s[d * blocks + n, m]
                block, owner = lax.div(q, CB), lax.rem(q, CB)
                to_even = (block == 2) == (even == 0)
                place = jnp.where(block == 1, 2, jnp.where(to_even, 1, 0))
                place += jnp.where(owner == side, 3, 0)
                out[place, :, at : at + tile] = piece.T


def product_kernel(slabs, parts, phase, last, a_cols, over_rows, over_cols, *refs):
    sources, refs = refs[: len(phase)], refs[len(phase) :]
    a_tiles, over_tiles, refs = refs[0], refs[1], refs[2:]
    first = phase[0] == 0
    if not first:
        refs = refs[1:]
    if last:
        out, refs = refs[0], refs[1:]
    acc, ext, cols_v, cols_s, sem = refs
    blocks, taps, tile = a_tiles.shape[0], a_tiles.shape[1], a_tiles.shape[-1]
    kp = ext.shape[-1] // tile
    slab = lax.axis_index("slab")
    part = lax.axis_index("cross")
    r_even = 2 - 2 * lax.rem(slab, 2)
    u_pair = 2 - 2 * lax.rem(part, 2)
    r_odd, u_across = 2 - r_even, 2 - u_pair
    r_there = slab + r_odd - 1
    u_there = part + u_across - 1
    odd_ok = (r_there >= 0) & (r_there < slabs)
    across_ok = (u_there >= 0) & (u_there < parts)
    slots = [(3 * r + u) for r in (1, r_even, r_odd) for u in (1, u_pair, u_across)]
    valid = [
        None, None, across_ok, None, None, across_ok, odd_ok, odd_ok, odd_ok & across_ok
    ]
    copy = columns_of([(slots[i], x) for i, x in zip(phase, sources)], cols_v, cols_s, sem)
    for i, source in zip(phase, sources):
        for n in range(blocks):
            for m in range(kp):
                piece = source[n, m * tile : (m + 1) * tile, :]
                if first and valid[i] is not None:
                    piece = jnp.where(valid[i], piece, jnp.zeros_like(piece))
                ext[slots[i] * blocks + n, :, m * tile : (m + 1) * tile] = piece
    if first:
        for i in range(9):
            if i not in phase:
                for n in range(blocks):
                    ext[slots[i] * blocks + n] = jnp.zeros(ext.shape[1:], ext.dtype)
                    cols_v[pl.ds(slots[i] * blocks + n, 1)] = jnp.zeros((1, tile), cols_v.dtype)
        acc[...] = jnp.zeros_like(acc)
    copy.wait()

    def add(n, col, matrix):
        piece = jnp.dot(matrix[...], ext[col], preferred_element_type=jnp.float32)
        shift = (col // (3 * blocks)) * CB
        for m in range(kp):
            j = shift + cols_s[col, m]
            acc[n, j] += piece[:, m * tile : (m + 1) * tile]

    def visit(n, col, matrix):
        if first:
            add(n, col, matrix)
            return
        slot = lax.div(col, blocks)
        here = jnp.bool_(False)
        for i in phase:
            match = slot == slots[i]
            here = here | (match if valid[i] is None else match & valid[i])

        @pl.when(here)
        def _():
            add(n, col, matrix)

    for n in range(blocks):
        for k in range(taps):
            visit(n, a_cols[n, k], a_tiles.at[n, k])
    for o in range(over_tiles.shape[0]):
        visit(over_rows[o], over_cols[o], over_tiles.at[o])
    if last:
        for n in range(blocks):
            for j in range(acc.shape[1]):
                out[n * tile : (n + 1) * tile, j * tile : (j + 1) * tile] = acc[n, j].astype(
                    jnp.bfloat16
                )


def partial_kernel(left, own, mate, *outs):
    count = left.shape[0]
    rows = own.shape[0]
    for i in range(count):
        block = left[i]
        total = jnp.dot(block[:, :rows], own[...], preferred_element_type=jnp.float32)
        total += jnp.dot(block[:, rows:], mate[...], preferred_element_type=jnp.float32)
        outs[i][...] = total.astype(outs[i].dtype)


def final_kernel(slabs, own, across, even, even_x, odd, out):
    width = (out.shape[1] - own.shape[1]) // 2
    span = own.shape[1]
    slab = lax.axis_index("slab")
    first = lax.rem(slab, 2) == 0
    there = jnp.where(first, slab - 1, slab + 1)
    ok = (there >= 0) & (there < slabs)
    odd_value = jnp.where(ok, odd[...].astype(jnp.float32), 0.0)
    even_value = even[...].astype(jnp.float32) + even_x[...].astype(jnp.float32)
    lower = jnp.where(first, odd_value, even_value)
    upper = jnp.where(first, even_value, odd_value)
    middle = own[...] + across[...].astype(jnp.float32)
    out[...] = jnp.zeros_like(out)
    out[:, :span] = lower
    out[:, width : width + span] += middle
    out[:, 2 * width : 2 * width + span] += upper


def vmem(count):
    return [pl.BlockSpec(memory_space=pltpu.VMEM)] * count


def smem(count):
    return [pl.BlockSpec(memory_space=pltpu.SMEM)] * count


def cost(flops, size):
    return pl.CostEstimate(flops=flops, bytes_accessed=size, transcendentals=0)


def grant(mib):
    return pltpu.CompilerParams(vmem_limit_bytes=mib << 20)


def fast_body(slabs, parts, a_tiles, a_cols, over_tiles, over_rows, over_cols, p_tiles, p_cols):
    blocks, kp, tile = p_tiles.shape[0], p_tiles.shape[1], p_tiles.shape[-1]
    width = CB * tile
    span = blocks * tile
    half = tile // 2
    step = moves(slabs, parts)

    def send(value, name):
        return exchange(value, slabs, parts, step[name])

    def column_scratch(count):
        return [
            pltpu.VMEM((count * blocks, tile), jnp.int32),
            pltpu.SMEM((count * blocks, tile), jnp.int32),
            pltpu.SemaphoreType.DMA,
        ]

    own = pack(p_tiles, p_cols)
    even = send(own, "even")
    mate = send(own, "pair")
    own_x = send(own, "across")
    left = pl.pallas_call(
        functools.partial(prepare_kernel, kp),
        out_shape=jax.ShapeDtypeStruct((3 * CB, half, 2 * span), jnp.bfloat16),
        in_specs=vmem(2),
        out_specs=vmem(1)[0],
        scratch_shapes=column_scratch(2),
        compiler_params=grant(4),
        cost_estimate=cost(1 << 30, 1 << 24),
        name="prepare",
    )(own, mate)
    odd = send(own, "odd")
    even_x = send(even, "across")
    even_p = send(even, "pair")
    odd_x = send(odd, "across")
    odd_p = send(odd, "pair")
    sources = (own, mate, own_x, even, even_p, even_x, odd, odd_p, odd_x)
    sums = jax.ShapeDtypeStruct((blocks, 5 * CB, tile, tile), jnp.float32)
    rounded = jax.ShapeDtypeStruct((span, 5 * width), jnp.bfloat16)
    carried = ()
    for index, phase in enumerate(PHASES):
        last = index == len(PHASES) - 1
        results = pl.pallas_call(
            functools.partial(product_kernel, slabs, parts, phase, last),
            out_shape=(rounded, sums) if last else (sums,),
            in_specs=smem(3) + vmem(len(phase) + 2 + len(carried)),
            out_specs=(vmem(1)[0],) * (1 + last),
            scratch_shapes=[pltpu.VMEM((9 * blocks, tile, kp * tile), jnp.bfloat16)]
            + column_scratch(9),
            input_output_aliases={len(phase) + 5: int(last)} if carried else {},
            compiler_params=grant(8),
            cost_estimate=cost(1 << 30, 1 << 24),
            name="product",
        )(
            a_cols, over_rows, over_cols, *(sources[i] for i in phase), a_tiles, over_tiles,
            *carried,
        )
        carried = results[-1:]
    product = results[0]
    product_mate = send(product, "pair")

    kinds = [jnp.bfloat16] * 3 + [jnp.float32, jnp.bfloat16, jnp.float32]
    x_odd, x_even, x_own, b_odd, b_even, b_own = pl.pallas_call(
        partial_kernel,
        out_shape=[jax.ShapeDtypeStruct((half, 5 * width), kind) for kind in kinds],
        in_specs=vmem(3),
        out_specs=vmem(6),
        compiler_params=grant(8),
        cost_estimate=cost(1 << 29, 1 << 22),
        name="partial",
    )(left, product, product_mate)
    g_odd = send(x_odd, "other")
    g_even_x = send(x_even, "even_other")
    g_even = send(b_even, "even")
    g_own = send(x_own, "other")
    s_odd = send((b_odd + g_odd.astype(jnp.float32)).astype(jnp.bfloat16), "odd")
    return pl.pallas_call(
        functools.partial(final_kernel, slabs),
        out_shape=jax.ShapeDtypeStruct((half, 7 * width), jnp.float32),
        in_specs=vmem(5),
        out_specs=vmem(1)[0],
        compiler_params=grant(4),
        name="final",
    )(b_own, g_own, g_even, g_even_x, s_odd)


SPECS = (
    P(AXES, None, None, None),
    P(AXES, None),
    P(AXES, None, None),
    P(AXES),
    P(AXES),
    P(AXES, None, None, None),
    P(AXES, None),
)


def solution(mesh):
    slabs, parts = mesh.shape["slab"], mesh.shape["cross"]

    def body(*args):
        return fast_body(slabs, parts, *args)

    return jax.shard_map(
        body, mesh=mesh, in_specs=SPECS, out_specs=P(AXES, None), check_vma=False
    )
```

time: 52.1 us -> 47.6 us (0.914); the launches traced: 51.9 us -> 46.8 us
  starting transfers between devices: 20.3 us -> 13.4 us
  local copies, waits for them, and re-layouts: 1.64 us -> 3.93 us
  other arithmetic: 0.06 us -> 1.65 us
  waiting for transfers between devices: 21.5 us -> 20.2 us
  Pallas kernels: 8.22 us -> 7.51 us
    ppermute x14, starting transfers between devices: 20.3 us -> 13.4 us  [exchange(): return lax.ppermute(value, AXES, pairs)]
    unnamed x14 -> x12, local copies, waits for them, and re-layouts: 1.64 us -> 3.91 us
    ppermute x14, waiting for transfers between devices: 21.5 us -> 20.2 us  [exchange(): return lax.ppermute(value, AXES, pairs)]
    concatenate x0 -> x1, other arithmetic: none -> 0.94 us  [pack(): jnp.concatenate([p_tiles.reshape(blocks, kp * tile, tile), cols], axis=1)]
    another operation x0 -> x1, other arithmetic: none -> 0.68 us
  transfers between devices with their start and end apart: 14 -> 14, of which waited for: 6 -> 6; matrix products, arithmetic and copies ran while one was open for 0% -> 0% of each run, Pallas kernels for 3% -> 8%
where the time goes in v3:
time: 47.6 us; the launch traced here: 46.8 us
  waiting for transfers between devices  20.2 us (42%)
  starting transfers between devices  13.4 us (28%)
  Pallas kernels  7.51 us (16%)
  local copies, waits for them, and re-layouts  3.93 us (8%)
  other arithmetic  1.65 us (3%)
    ppermute x14, waiting for transfers between devices, exchange(): return lax.ppermute(value, AXES, pairs)  20.2 us
    ppermute x14, starting transfers between devices, exchange(): return lax.ppermute(value, AXES, pairs)  13.4 us
    unnamed x12, local copies, waits for them, and re-layouts  3.91 us
    pallas_call x2, Pallas kernels, fast_body(): pl.pallas_call(functools.partial(product_kernel, slabs, parts, phase, las...  3.83 us
    pallas_call x1, Pallas kernels, fast_body(): pl.pallas_call(partial_kernel, out_shape=[jax.ShapeDtypeStruct((half, 5 *...  1.47 us
    pallas_call x1, Pallas kernels, fast_body(): pl.pallas_call(functools.partial(prepare_kernel, kp), out_shape=jax.Shape...  1.26 us
  transfers between devices with their start and end apart: 14, of which 6 were waited for; matrix products, arithmetic and copies ran while one was open for 0% of the time, Pallas kernels for 8%

profile of v3, /device:TPU:0, one launch (start us, length us, event | category | flops | bytes accessed | tf_op | source)
XLA Modules:
  0.0 46.8 jit_solution(9057117572843968895)
XLA Ops:
  0.0 0.7 %convert.4 = bf16[2,3]{1,0:T(2,128)(2,1)S(1)} convert(s32[2,3]{1,0:T(2,128)} %param.13) | non-fusion elementwise | flops 6 | bytes 36 | tf_op jit(solution)/shard_map/convert
  0.7 0.9 %pad_maximum_fusion.own.refs_0_ = bf16[2,400,128]{2,1,0:T(8,128)(2,1)S(1)} fusion(bf16[2,16,128]{2,1,0:T(8,128)(2,1)S(1)} %broadcast_in_dim.2, bf16[2,384,128]{2,1,0:T(8,128)(2,1)} %bitcast.1), kind=kLoop, calls=%fused_computation.1 | loop fusion | flops 409600 | bytes 409600 | tf_op jit(solution)/shard_map/concatenate | solution.py:51
  1.6 3.1 %collective-permute-start.4 = (bf16[2,400,128]{2,1,0:T(8,128)(2,1)S(1)}, bf16[2,400,128]{2,1,0:T(8,128)(2,1)S(1)}, u32[]{:S(2)}, u32[]{:S(2)}) collective-permute-start(bf16[2,400,128]{2,1,0:T(8,128)(2,1)S(1)} %pad_maximum_fusion.own.refs_0_), channel_id=1, source_target_pairs={{0,4},{1,5},{2,6},{3,7},{4,0},{5,1},{6,2},{7,3},{8,12},{9,13},{10,... | collective-permute-start | bytes 614408 | tf_op jit(solution)/shard_map/ppermute | solution.py:23
  4.7 0.0 collective-permute-start.1
  4.7 1.6 %collective-permute-start.3 = (bf16[2,400,128]{2,1,0:T(8,128)(2,1)S(1)}, bf16[2,400,128]{2,1,0:T(8,128)(2,1)S(1)}, u32[]{:S(2)}, u32[]{:S(2)}) collective-permute-start(bf16[2,400,128]{2,1,0:T(8,128)(2,1)S(1)} %pad_maximum_fusion.own.refs_0_), channel_id=1, source_target_pairs={{0,8},{1,2},{2,1},{3,11},{4,12},{5,6},{6,5},{7,15},{8,0},{9,10},{1... | collective-permute-start | bytes 614408 | tf_op jit(solution)/shard_map/ppermute | solution.py:23
  6.3 0.0 collective-permute-start
  6.3 7.1 %collective-permute-done.4.refs_3_ = bf16[2,400,128]{2,1,0:T(8,128)(2,1)S(1)} collective-permute-done((bf16[2,400,128]{2,1,0:T(8,128)(2,1)S(1)}, bf16[2,400,128]{2,1,0:T(8,128)(2,1)S(1)}, u32[]{:S(2)}, u32[]{:S(2)}) %collective-permute-start.4) | collective-permute-done | bytes 204832 | tf_op jit(solution)/shard_map/ppermute | solution.py:23
  13.4 2.5 %collective-permute-start.6 = (bf16[2,400,128]{2,1,0:T(8,128)(2,1)S(1)}, bf16[2,400,128]{2,1,0:T(8,128)(2,1)S(1)}, u32[]{:S(2)}, u32[]{:S(2)}) collective-permute-start(bf16[2,400,128]{2,1,0:T(8,128)(2,1)S(1)} %collective-permute-done.4.refs_3_), channel_id=1, source_target_pairs={{0,8},{1,2},{2,1},{3,11},{4,12},{5,6},{6,5},{7,15},{8,0},{9,10},{1... | collective-permute-start | bytes 614408 | tf_op jit(solution)/shard_map/ppermute | solution.py:23
  16.0 0.5 %collective-permute-start.7 = (bf16[2,400,128]{2,1,0:T(8,128)(2,1)S(1)}, bf16[2,400,128]{2,1,0:T(8,128)(2,1)S(1)}, u32[]{:S(2)}, u32[]{:S(2)}) collective-permute-start(bf16[2,400,128]{2,1,0:T(8,128)(2,1)S(1)} %collective-permute-done.1.refs_6_), channel_id=1, source_target_pairs={{0,1},{1,0},{2,3},{3,2},{4,5},{5,4},{6,7},{7,6},{8,9},{9,8},{10,11... | collective-permute-start | bytes 614408 | tf_op jit(solution)/shard_map/ppermute | solution.py:23
  16.5 1.2 %collective-permute-start.2 = (bf16[2,400,128]{2,1,0:T(8,128)(2,1)S(1)}, bf16[2,400,128]{2,1,0:T(8,128)(2,1)S(1)}, u32[]{:S(2)}, u32[]{:S(2)}) collective-permute-start(bf16[2,400,128]{2,1,0:T(8,128)(2,1)S(1)} %collective-permute-done.1.refs_6_), channel_id=1, source_target_pairs={{0,8},{1,2},{2,1},{3,11},{4,12},{5,6},{6,5},{7,15},{8,0},{9,10},{1... | collective-permute-start | bytes 614408 | tf_op jit(solution)/shard_map/ppermute | solution.py:23
  17.7 2.0 %collective-permute-done.6.refs_5_ = bf16[2,400,128]{2,1,0:T(8,128)(2,1)S(1)} collective-permute-done((bf16[2,400,128]{2,1,0:T(8,128)(2,1)S(1)}, bf16[2,400,128]{2,1,0:T(8,128)(2,1)S(1)}, u32[]{:S(2)}, u32[]{:S(2)}) %collective-permute-start.6) | collective-permute-done | bytes 204832 | tf_op jit(solution)/shard_map/ppermute | solution.py:23
  19.7 0.0 collective-permute-done.5.refs_4_
  19.7 1.0 %copy-done = bf16[2,7,128,128]{3,2,1,0:T(8,128)(2,1)S(1)} copy-done((bf16[2,7,128,128]{3,2,1,0:T(8,128)(2,1)S(1)}, bf16[2,7,128,128]{3,2,1,0:T(8,128)(2,1)}, u32[]{:S(2)}) %copy-start) | copy-done | bytes 458776
  20.7 0.9 %copy-done.2 = bf16[4,128,128]{2,1,0:T(8,128)(2,1)S(1)} copy-done((bf16[4,128,128]{2,1,0:T(8,128)(2,1)S(1)}, bf16[4,128,128]{2,1,0:T(8,128)(2,1)}, u32[]{:S(2)}) %copy-start.2) | copy-done | bytes 131096
  21.6 0.7 %copy-done.3 = s32[2,7]{1,0:T(2,128)S(1)} copy-done((s32[2,7]{1,0:T(2,128)S(1)}, s32[2,7]{1,0:T(2,128)}, u32[]{:S(2)}) %copy-start.3) | copy-done | bytes 80
  22.3 0.7 %copy-done.4 = s32[4]{0:T(128)S(1)} copy-done((s32[4]{0:T(128)S(1)}, s32[4]{0:T(128)}, u32[]{:S(2)}) %copy-start.4) | copy-done | bytes 40
  23.0 0.7 %copy-done.5 = s32[4]{0:T(128)S(1)} copy-done((s32[4]{0:T(128)S(1)}, s32[4]{0:T(128)}, u32[]{:S(2)}) %copy-start.5) | copy-done | bytes 40
  23.6 2.3 %product.2.refs_3_ = f32[2,10,128,128]{3,2,1,0:T(8,128)S(1)} custom-call(s32[2,7]{1,0:T(2,128)S(1)} %copy-done.3, s32[4]{0:T(128)S(1)} %copy-done.4, s32[4]{0:T(128)S(1)} %copy-done.5, bf16[2,400,128]{2,1,0:T(8,128)(2,1)S(1)} %pad_maximum_fusion.own.refs_0_, bf16[2,400,128]{2,1,0:T(8,128)(2,1)S(1)} %collective-permute-done.mate.refs_1_, ...), custom_call_target="tpu_custom_call" | custom-call | flops 1073741824 | bytes 16777216 | tf_op jit(solution)/shard_map/product/pallas_call | solution.py:251
  25.9 1.6 %product.3 = (bf16[256,1280]{1,0:T(8,128)(2,1)S(1)}, f32[2,10,128,128]{3,2,1,0:T(8,128)S(1)}) custom-call(s32[2,7]{1,0:T(2,128)S(1)} %copy-done.3, s32[4]{0:T(128)S(1)} %copy-done.4, s32[4]{0:T(128)S(1)} %copy-done.5, bf16[2,400,128]{2,1,0:T(8,128)(2,1)S(1)} %collective-permute-done.2.refs_0_, ...), custom_call_target="tpu_custom_call", output_to_operand_aliasing={{1}: (6, {})} | custom-call | flops 1073741824 | bytes 16777216 | tf_op jit(solution)/shard_map/product/pallas_call | solution.py:251
  27.5 0.1 collective-permute-start.8
  27.6 1.3 %prepare.1.left = bf16[6,64,512]{2,1,0:T(8,128)(2,1)S(1)} custom-call(bf16[2,400,128]{2,1,0:T(8,128)(2,1)S(1)} %pad_maximum_fusion.own.refs_0_, bf16[2,400,128]{2,1,0:T(8,128)(2,1)S(1)} %collective-permute-done.mate.refs_1_), custom_call_target="tpu_custom_call" | custom-call | flops 1073741824 | bytes 16777216 | tf_op jit(solution)/shard_map/prepare/pallas_call | solution.py:230
  28.8 0.8 %collective-permute-done.8.mate = bf16[256,1280]{1,0:T(8,128)(2,1)S(1)} collective-permute-done((bf16[256,1280]{1,0:T(8,128)(2,1)S(1)}, bf16[256,1280]{1,0:T(8,128)(2,1)S(1)}, u32[]{:S(2)}, u32[]{:S(2)}) %collective-permute-start.8) | collective-permute-done | bytes 655392 | tf_op jit(solution)/shard_map/ppermute | solution.py:23
  29.7 1.5 %partial.1 = (bf16[64,1280]{1,0:T(8,128)(2,1)S(1)}, bf16[64,1280]{1,0:T(8,128)(2,1)S(1)}, bf16[64,1280]{1,0:T(8,128)(2,1)S(1)}, f32[64,1280]{1,0:T(8,128)S(1)}, ...) custom-call(bf16[6,64,512]{2,1,0:T(8,128)(2,1)S(1)} %prepare.1.left, bf16[256,1280]{1,0:T(8,128)(2,1)S(1)} %get-tuple-element.12.own, ...), custom_call_target="tpu_custom_call" | custom-call | flops 536870912 | bytes 4194304 | tf_op jit(solution)/shard_map/partial/pallas_call | solution.py:271
  31.1 0.5 collective-permute-start.12
  31.6 1.6 %collective-permute-start.9 = (bf16[64,1280]{1,0:T(8,128)(2,1)S(1)}, bf16[64,1280]{1,0:T(8,128)(2,1)S(1)}, u32[]{:S(2)}, u32[]{:S(2)}) collective-permute-start(bf16[64,1280]{1,0:T(8,128)(2,1)S(1)} %get-tuple-element.14), channel_id=1, source_target_pairs={{0,2},{1,3},{2,0},{3,1},{4,6},{5,7},{6,4},{7,5},{8,10},{9,11},{10,... | collective-permute-start | bytes 491528 | tf_op jit(solution)/shard_map/ppermute | solution.py:23
  33.2 2.0 %collective-permute-start.10 = (bf16[64,1280]{1,0:T(8,128)(2,1)S(1)}, bf16[64,1280]{1,0:T(8,128)(2,1)S(1)}, u32[]{:S(2)}, u32[]{:S(2)}) collective-permute-start(bf16[64,1280]{1,0:T(8,128)(2,1)S(1)} %get-tuple-element.15), channel_id=1, source_target_pairs={{0,4},{1,5},{2,6},{3,7},{4,0},{5,1},{6,2},{7,3},{8,12},{9,13},{10,... | collective-permute-start | bytes 491528 | tf_op jit(solution)/shard_map/ppermute | solution.py:23
  35.2 0.4 collective-permute-start.11
  35.5 2.7 %collective-permute-done.12 = bf16[64,1280]{1,0:T(8,128)(2,1)S(1)} collective-permute-done((bf16[64,1280]{1,0:T(8,128)(2,1)S(1)}, bf16[64,1280]{1,0:T(8,128)(2,1)S(1)}, u32[]{:S(2)}, u32[]{:S(2)}) %collective-permute-start.12) | collective-permute-done | bytes 163872 | tf_op jit(solution)/shard_map/ppermute | solution.py:23
  38.3 0.1 collective-permute-start.13
  38.4 3.4 %collective-permute-done.9.across = bf16[64,1280]{1,0:T(8,128)(2,1)S(1)} collective-permute-done((bf16[64,1280]{1,0:T(8,128)(2,1)S(1)}, bf16[64,1280]{1,0:T(8,128)(2,1)S(1)}, u32[]{:S(2)}, u32[]{:S(2)}) %collective-permute-start.9) | collective-permute-done | bytes 163872 | tf_op jit(solution)/shard_map/ppermute | solution.py:23
  41.8 4.1 %collective-permute-done.11.even_x = bf16[64,1280]{1,0:T(8,128)(2,1)S(1)} collective-permute-done((bf16[64,1280]{1,0:T(8,128)(2,1)S(1)}, bf16[64,1280]{1,0:T(8,128)(2,1)S(1)}, u32[]{:S(2)}, u32[]{:S(2)}) %collective-permute-start.11) | collective-permute-done | bytes 163872 | tf_op jit(solution)/shard_map/ppermute | solution.py:23
  45.9 1.0 %final.1 = f32[64,1792]{1,0:T(8,128)} custom-call(f32[64,1280]{1,0:T(8,128)S(1)} %get-tuple-element.13.own, bf16[64,1280]{1,0:T(8,128)(2,1)S(1)} %collective-permute-done.9.across, bf16[64,1280]{1,0:T(8,128)(2,1)S(1)} %collective-permute-done.10.even, bf16[64,1280]{1,0:T(8,128)(2,1)S(1)} %collective-permute-done.11.even_x, ...), custom_call_target="tpu_custom_call" | custom-call | tf_op jit(solution)/shard_map/final/pallas_call | solution.py:285
  (18 shorter events, 0.1 us)
Async XLA Ops:
  1.6 11.8 %collective-permute-start.4 = (bf16[2,400,128]{2,1,0:T(8,128)(2,1)S(1)}, bf16[2,400,128]{2,1,0:T(8,128)(2,1)S(1)}, u32[]{:S(2)}, u32[]{:S(2)}) collective-permute-start(bf16[2,400,128]{2,1,0:T(8,128)(2,1)S(1)} %pad_maximum_fusion.own.refs_0_), channel_id=1, source_target_pairs={{0,4},{1,5},{2,6},{3,7},{4,0},{5,1},{6,2},{7,3},{8,12},{9,13},{10,... | collective-permute-start | bytes 614408 | tf_op jit(solution)/shard_map/ppermute | solution.py:23
  4.7 11.3 %collective-permute-start.1 = (bf16[2,400,128]{2,1,0:T(8,128)(2,1)S(1)}, bf16[2,400,128]{2,1,0:T(8,128)(2,1)S(1)}, u32[]{:S(2)}, u32[]{:S(2)}) collective-permute-start(bf16[2,400,128]{2,1,0:T(8,128)(2,1)S(1)} %pad_maximum_fusion.own.refs_0_), channel_id=1, source_target_pairs={{0,1},{1,0},{2,3},{3,2},{4,8},{5,9},{6,10},{7,11},{8,4},{9,5},{10,... | collective-permute-start | bytes 614408 | tf_op jit(solution)/shard_map/ppermute | solution.py:23
  4.7 11.8 %collective-permute-start.3 = (bf16[2,400,128]{2,1,0:T(8,128)(2,1)S(1)}, bf16[2,400,128]{2,1,0:T(8,128)(2,1)S(1)}, u32[]{:S(2)}, u32[]{:S(2)}) collective-permute-start(bf16[2,400,128]{2,1,0:T(8,128)(2,1)S(1)} %pad_maximum_fusion.own.refs_0_), channel_id=1, source_target_pairs={{0,8},{1,2},{2,1},{3,11},{4,12},{5,6},{6,5},{7,15},{8,0},{9,10},{1... | collective-permute-start | bytes 614408 | tf_op jit(solution)/shard_map/ppermute | solution.py:23
  6.3 11.4 %collective-permute-start = (bf16[2,400,128]{2,1,0:T(8,128)(2,1)S(1)}, bf16[2,400,128]{2,1,0:T(8,128)(2,1)S(1)}, u32[]{:S(2)}, u32[]{:S(2)}) collective-permute-start(bf16[2,400,128]{2,1,0:T(8,128)(2,1)S(1)} %pad_maximum_fusion.own.refs_0_), channel_id=1, source_target_pairs={{0,1},{1,0},{2,3},{3,2},{4,5},{5,4},{6,7},{7,6},{8,9},{9,8},{10,11... | collective-permute-start | bytes 614408 | tf_op jit(solution)/shard_map/ppermute | solution.py:23
  13.4 6.3 %collective-permute-start.6 = (bf16[2,400,128]{2,1,0:T(8,128)(2,1)S(1)}, bf16[2,400,128]{2,1,0:T(8,128)(2,1)S(1)}, u32[]{:S(2)}, u32[]{:S(2)}) collective-permute-start(bf16[2,400,128]{2,1,0:T(8,128)(2,1)S(1)} %collective-permute-done.4.refs_3_), channel_id=1, source_target_pairs={{0,8},{1,2},{2,1},{3,11},{4,12},{5,6},{6,5},{7,15},{8,0},{9,10},{1... | collective-permute-start | bytes 614408 | tf_op jit(solution)/shard_map/ppermute | solution.py:23
  16.0 3.7 %collective-permute-start.5 = (bf16[2,400,128]{2,1,0:T(8,128)(2,1)S(1)}, bf16[2,400,128]{2,1,0:T(8,128)(2,1)S(1)}, u32[]{:S(2)}, u32[]{:S(2)}) collective-permute-start(bf16[2,400,128]{2,1,0:T(8,128)(2,1)S(1)} %collective-permute-done.4.refs_3_), channel_id=1, source_target_pairs={{0,1},{1,0},{2,3},{3,2},{4,5},{5,4},{6,7},{7,6},{8,9},{9,8},{10,11... | collective-permute-start | bytes 614408 | tf_op jit(solution)/shard_map/ppermute | solution.py:23
  16.0 3.7 %collective-permute-start.7 = (bf16[2,400,128]{2,1,0:T(8,128)(2,1)S(1)}, bf16[2,400,128]{2,1,0:T(8,128)(2,1)S(1)}, u32[]{:S(2)}, u32[]{:S(2)}) collective-permute-start(bf16[2,400,128]{2,1,0:T(8,128)(2,1)S(1)} %collective-permute-done.1.refs_6_), channel_id=1, source_target_pairs={{0,1},{1,0},{2,3},{3,2},{4,5},{5,4},{6,7},{7,6},{8,9},{9,8},{10,11... | collective-permute-start | bytes 614408 | tf_op jit(solution)/shard_map/ppermute | solution.py:23
  16.5 9.4 %collective-permute-start.2 = (bf16[2,400,128]{2,1,0:T(8,128)(2,1)S(1)}, bf16[2,400,128]{2,1,0:T(8,128)(2,1)S(1)}, u32[]{:S(2)}, u32[]{:S(2)}) collective-permute-start(bf16[2,400,128]{2,1,0:T(8,128)(2,1)S(1)} %collective-permute-done.1.refs_6_), channel_id=1, source_target_pairs={{0,8},{1,2},{2,1},{3,11},{4,12},{5,6},{6,5},{7,15},{8,0},{9,10},{1... | collective-permute-start | bytes 614408 | tf_op jit(solution)/shard_map/ppermute | solution.py:23
  19.7 1.0 %copy-start = (bf16[2,7,128,128]{3,2,1,0:T(8,128)(2,1)S(1)}, bf16[2,7,128,128]{3,2,1,0:T(8,128)(2,1)}, u32[]{:S(2)}) copy-start(bf16[2,7,128,128]{3,2,1,0:T(8,128)(2,1)} %refs_1_.1) | copy-start | bytes 1376260
  20.7 0.9 %copy-start.2 = (bf16[4,128,128]{2,1,0:T(8,128)(2,1)S(1)}, bf16[4,128,128]{2,1,0:T(8,128)(2,1)}, u32[]{:S(2)}) copy-start(bf16[4,128,128]{2,1,0:T(8,128)(2,1)} %refs_2_.1) | copy-start | bytes 393220
  21.6 0.7 %copy-start.3 = (s32[2,7]{1,0:T(2,128)S(1)}, s32[2,7]{1,0:T(2,128)}, u32[]{:S(2)}) copy-start(s32[2,7]{1,0:T(2,128)} %a_cols.3) | copy-start | bytes 172
  22.3 0.7 %copy-start.4 = (s32[4]{0:T(128)S(1)}, s32[4]{0:T(128)}, u32[]{:S(2)}) copy-start(s32[4]{0:T(128)} %over_rows.3) | copy-start | bytes 52
  23.0 0.7 %copy-start.5 = (s32[4]{0:T(128)S(1)}, s32[4]{0:T(128)}, u32[]{:S(2)}) copy-start(s32[4]{0:T(128)} %over_cols.3) | copy-start | bytes 52
  23.6 2.3 %copy-start.1 = (bf16[2,7,128,128]{3,2,1,0:T(8,128)(2,1)S(1)}, bf16[2,7,128,128]{3,2,1,0:T(8,128)(2,1)}, u32[]{:S(2)}) copy-start(bf16[2,7,128,128]{3,2,1,0:T(8,128)(2,1)} %refs_1_.1) | copy-start | bytes 1376260
  27.5 2.2 %collective-permute-start.8 = (bf16[256,1280]{1,0:T(8,128)(2,1)S(1)}, bf16[256,1280]{1,0:T(8,128)(2,1)S(1)}, u32[]{:S(2)}, u32[]{:S(2)}) collective-permute-start(bf16[256,1280]{1,0:T(8,128)(2,1)S(1)} %get-tuple-element.12.own), channel_id=1, source_target_pairs={{0,1},{1,0},{2,3},{3,2},{4,5},{5,4},{6,7},{7,6},{8,9},{9,8},{10,11... | collective-permute-start | bytes 1966088 | tf_op jit(solution)/shard_map/ppermute | solution.py:23
  31.1 7.1 %collective-permute-start.12 = (bf16[64,1280]{1,0:T(8,128)(2,1)S(1)}, bf16[64,1280]{1,0:T(8,128)(2,1)S(1)}, u32[]{:S(2)}, u32[]{:S(2)}) collective-permute-start(bf16[64,1280]{1,0:T(8,128)(2,1)S(1)} %get-tuple-element.18), channel_id=1, source_target_pairs={{0,2},{1,3},{2,0},{3,1},{4,6},{5,7},{6,4},{7,5},{8,10},{9,11},{10,... | collective-permute-start | bytes 491528 | tf_op jit(solution)/shard_map/ppermute | solution.py:23
  31.6 10.2 %collective-permute-start.9 = (bf16[64,1280]{1,0:T(8,128)(2,1)S(1)}, bf16[64,1280]{1,0:T(8,128)(2,1)S(1)}, u32[]{:S(2)}, u32[]{:S(2)}) collective-permute-start(bf16[64,1280]{1,0:T(8,128)(2,1)S(1)} %get-tuple-element.14), channel_id=1, source_target_pairs={{0,2},{1,3},{2,0},{3,1},{4,6},{5,7},{6,4},{7,5},{8,10},{9,11},{10,... | collective-permute-start | bytes 491528 | tf_op jit(solution)/shard_map/ppermute | solution.py:23
  33.2 8.6 %collective-permute-start.10 = (bf16[64,1280]{1,0:T(8,128)(2,1)S(1)}, bf16[64,1280]{1,0:T(8,128)(2,1)S(1)}, u32[]{:S(2)}, u32[]{:S(2)}) collective-permute-start(bf16[64,1280]{1,0:T(8,128)(2,1)S(1)} %get-tuple-element.15), channel_id=1, source_target_pairs={{0,4},{1,5},{2,6},{3,7},{4,0},{5,1},{6,2},{7,3},{8,12},{9,13},{10,... | collective-permute-start | bytes 491528 | tf_op jit(solution)/shard_map/ppermute | solution.py:23
  35.2 10.7 %collective-permute-start.11 = (bf16[64,1280]{1,0:T(8,128)(2,1)S(1)}, bf16[64,1280]{1,0:T(8,128)(2,1)S(1)}, u32[]{:S(2)}, u32[]{:S(2)}) collective-permute-start(bf16[64,1280]{1,0:T(8,128)(2,1)S(1)} %get-tuple-element.16), channel_id=1, source_target_pairs={{0,6},{1,7},{2,4},{3,5},{4,2},{5,3},{6,0},{7,1},{8,14},{9,15},{10,... | collective-permute-start | bytes 491528 | tf_op jit(solution)/shard_map/ppermute | solution.py:23
  38.3 7.6 %collective-permute-start.13 = (bf16[64,1280]{1,0:T(8,128)(2,1)S(1)}, bf16[64,1280]{1,0:T(8,128)(2,1)S(1)}, u32[]{:S(2)}, u32[]{:S(2)}) collective-permute-start(bf16[64,1280]{1,0:T(8,128)(2,1)S(1)} %add_convert_fusion), channel_id=1, source_target_pairs={{0,1},{1,0},{2,3},{3,2},{4,8},{5,9},{6,10},{7,11},{8,4},{9,5},{10,... | collective-permute-start | bytes 491528 | tf_op jit(solution)/shard_map/ppermute | solution.py:23

commit v4 on v3

--- a/solution.py
+++ b/solution.py
@@ -11,7 +11,7 @@
 CB = 2
 AXES = ("slab", "cross")
 PAD = 16
-PHASES = ((0, 1, 2, 3, 4, 5, 6, 7), (8,))
+LAST = 8
 
 
 def exchange(value, slabs, parts, move):
@@ -52,11 +52,10 @@
 
 
 def columns_of(sources, cols_v, cols_s, sem):
-    for slot, source in sources:
-        blocks = source.shape[0]
-        for n in range(blocks):
+    for at, source in sources:
+        for n in range(source.shape[0]):
             row = source[n, source.shape[1] - PAD :].astype(jnp.float32)
-            cols_v[pl.ds(slot * blocks + n, 1)] = row[:1].astype(jnp.int32)
+            cols_v[pl.ds(at + n, 1)] = row[:1].astype(jnp.int32)
     copy = pltpu.make_async_copy(cols_v, cols_s, sem)
     copy.start()
     return copy
@@ -65,7 +64,7 @@
 def prepare_kernel(kp, own, mate, out, cols_v, cols_s, sem):
     blocks, tile = own.shape[0], own.shape[-1]
     half = tile // 2
-    copy = columns_of(((0, own), (1, mate)), cols_v, cols_s, sem)
+    copy = columns_of(((0, own), (blocks, mate)), cols_v, cols_s, sem)
     part = lax.axis_index("cross")
     slab = lax.axis_index("slab")
     lower = lax.rem(part, 2) == 0
@@ -87,89 +86,113 @@
                 out[place, :, at : at + tile] = piece.T
 
 
-def product_kernel(slabs, parts, phase, last, a_cols, over_rows, over_cols, *refs):
-    sources, refs = refs[: len(phase)], refs[len(phase) :]
-    a_tiles, over_tiles, refs = refs[0], refs[1], refs[2:]
-    first = phase[0] == 0
-    if not first:
-        refs = refs[1:]
-    if last:
-        out, refs = refs[0], refs[1:]
-    acc, ext, cols_v, cols_s, sem = refs
+class Place:
+    def __init__(self, slabs, parts, blocks):
+        slab, part = lax.axis_index("slab"), lax.axis_index("cross")
+        r_even = 2 - 2 * lax.rem(slab, 2)
+        u_pair = 2 - 2 * lax.rem(part, 2)
+        r_odd, u_across = 2 - r_even, 2 - u_pair
+        r_there, u_there = slab + r_odd - 1, part + u_across - 1
+        odd_ok = (r_there >= 0) & (r_there < slabs)
+        across_ok = (u_there >= 0) & (u_there < parts)
+        self.shift = [r * CB for r in (1, r_even, r_odd) for _ in range(3)]
+        self.first = [
+            (3 * r + u) * blocks for r in (1, r_even, r_odd) for u in (1, u_pair, u_across)
+        ]
+        self.valid = [
+            None, None, across_ok, None, None, across_ok, odd_ok, odd_ok, odd_ok & across_ok
+        ]
+
+
+def fetch(source, at, ok, ext):
+    blocks, tile = source.shape[0], source.shape[-1]
+    kp = ext.shape[-1] // tile
+    for n in range(blocks):
+        for m in range(kp):
+            piece = source[n, m * tile : (m + 1) * tile, :]
+            if ok is not None:
+                piece = jnp.where(ok, piece, jnp.zeros_like(piece))
+            ext[at + n, :, m * tile : (m + 1) * tile] = piece
+
+
+def product_kernel(slabs, parts, a_cols, over_rows, over_cols, *refs):
+    early = [i for i in range(9) if i != LAST]
+    sources, refs = refs[:8], refs[8:]
+    a_tiles, over_tiles, out, acc, ext, cols_v, cols_s, sem = refs
     blocks, taps, tile = a_tiles.shape[0], a_tiles.shape[1], a_tiles.shape[-1]
     kp = ext.shape[-1] // tile
-    slab = lax.axis_index("slab")
-    part = lax.axis_index("cross")
-    r_even = 2 - 2 * lax.rem(slab, 2)
-    u_pair = 2 - 2 * lax.rem(part, 2)
-    r_odd, u_across = 2 - r_even, 2 - u_pair
-    r_there = slab + r_odd - 1
-    u_there = part + u_across - 1
-    odd_ok = (r_there >= 0) & (r_there < slabs)
-    across_ok = (u_there >= 0) & (u_there < parts)
-    slots = [(3 * r + u) for r in (1, r_even, r_odd) for u in (1, u_pair, u_across)]
-    valid = [
-        None, None, across_ok, None, None, across_ok, odd_ok, odd_ok, odd_ok & across_ok
-    ]
-    copy = columns_of([(slots[i], x) for i, x in zip(phase, sources)], cols_v, cols_s, sem)
-    for i, source in zip(phase, sources):
-        for n in range(blocks):
-            for m in range(kp):
-                piece = source[n, m * tile : (m + 1) * tile, :]
-                if first and valid[i] is not None:
-                    piece = jnp.where(valid[i], piece, jnp.zeros_like(piece))
-                ext[slots[i] * blocks + n, :, m * tile : (m + 1) * tile] = piece
-    if first:
-        for i in range(9):
-            if i not in phase:
-                for n in range(blocks):
-                    ext[slots[i] * blocks + n] = jnp.zeros(ext.shape[1:], ext.dtype)
-                    cols_v[pl.ds(slots[i] * blocks + n, 1)] = jnp.zeros((1, tile), cols_v.dtype)
-        acc[...] = jnp.zeros_like(acc)
+    place = Place(slabs, parts, blocks)
+    copy = columns_of(
+        [(place.first[i], source) for i, source in zip(early, sources)], cols_v, cols_s, sem
+    )
+    for i, source in zip(early, sources):
+        fetch(source, place.first[i], place.valid[i], ext)
+    for n in range(blocks):
+        ext[place.first[LAST] + n] = jnp.zeros(ext.shape[1:], ext.dtype)
+        cols_v[pl.ds(place.first[LAST] + n, 1)] = jnp.zeros((1, tile), jnp.int32)
+    acc[...] = jnp.zeros_like(acc)
     copy.wait()
 
     def add(n, col, matrix):
-        piece = jnp.dot(matrix[...], ext[col], preferred_element_type=jnp.float32)
+        piece = jnp.dot(matrix, ext[col], preferred_element_type=jnp.float32)
         shift = (col // (3 * blocks)) * CB
         for m in range(kp):
-            j = shift + cols_s[col, m]
-            acc[n, j] += piece[:, m * tile : (m + 1) * tile]
-
-    def visit(n, col, matrix):
-        if first:
-            add(n, col, matrix)
-            return
-        slot = lax.div(col, blocks)
-        here = jnp.bool_(False)
-        for i in phase:
-            match = slot == slots[i]
-            here = here | (match if valid[i] is None else match & valid[i])
-
-        @pl.when(here)
-        def _():
-            add(n, col, matrix)
+            acc[n, shift + cols_s[col, m]] += piece[:, m * tile : (m + 1) * tile]
 
     for n in range(blocks):
         for k in range(taps):
-            visit(n, a_cols[n, k], a_tiles.at[n, k])
+            add(n, a_cols[n, k], a_tiles[n, k])
     for o in range(over_tiles.shape[0]):
-        visit(over_rows[o], over_cols[o], over_tiles.at[o])
-    if last:
+        add(over_rows[o], over_cols[o], over_tiles[o])
+    for n in range(blocks):
+        for j in range(acc.shape[1]):
+            out[n * tile : (n + 1) * tile, j * tile : (j + 1) * tile] = acc[n, j].astype(
+                jnp.bfloat16
+            )
+
+
+def last_kernel(slabs, parts, a_cols, over_rows, over_cols, source, a_tiles, over_tiles,
+                acc_in, out_in, acc, out, ext, cols_v, cols_s, sem):
+    blocks, taps, tile = a_tiles.shape[0], a_tiles.shape[1], a_tiles.shape[-1]
+    kp = ext.shape[-1] // tile
+    place = Place(slabs, parts, blocks)
+    first, shift = place.first[LAST], place.shift[LAST]
+
+    @pl.when(place.valid[LAST])
+    def _():
+        copy = columns_of([(0, source)], cols_v, cols_s, sem)
+        fetch(source, 0, None, ext)
+        copy.wait()
+
+        def visit(n, col, matrix):
+            row = col - first
+
+            @pl.when((row >= 0) & (row < blocks))
+            def _():
+                piece = jnp.dot(matrix[...], ext[row], preferred_element_type=jnp.float32)
+                at = pl.multiple_of(n * tile, tile)
+                for m in range(kp):
+                    j = shift + cols_s[row, m]
+                    total = acc[n, j] + piece[:, m * tile : (m + 1) * tile]
+                    acc[n, j] = total
+                    to = pl.multiple_of(j * tile, tile)
+                    out[pl.ds(at, tile), pl.ds(to, tile)] = total.astype(jnp.bfloat16)
+
         for n in range(blocks):
-            for j in range(acc.shape[1]):
-                out[n * tile : (n + 1) * tile, j * tile : (j + 1) * tile] = acc[n, j].astype(
-                    jnp.bfloat16
-                )
+            for k in range(taps):
+                visit(n, a_cols[n, k], a_tiles.at[n, k])
+        for o in range(over_tiles.shape[0]):
+            visit(over_rows[o], over_cols[o], over_tiles.at[o])
 
 
 def partial_kernel(left, own, mate, *outs):
-    count = left.shape[0]
+    count, half = left.shape[0], left.shape[1]
     rows = own.shape[0]
+    stack = left[...].reshape(count * half, 2 * rows)
+    total = jnp.dot(stack[:, :rows], own[...], preferred_element_type=jnp.float32)
+    total += jnp.dot(stack[:, rows:], mate[...], preferred_element_type=jnp.float32)
     for i in range(count):
-        block = left[i]
-        total = jnp.dot(block[:, :rows], own[...], preferred_element_type=jnp.float32)
-        total += jnp.dot(block[:, rows:], mate[...], preferred_element_type=jnp.float32)
-        outs[i][...] = total.astype(outs[i].dtype)
+        outs[i][...] = total[i * half : (i + 1) * half].astype(outs[i].dtype)
 
 
 def final_kernel(slabs, own, across, even, even_x, odd, out):
@@ -245,26 +268,29 @@
     sources = (own, mate, own_x, even, even_p, even_x, odd, odd_p, odd_x)
     sums = jax.ShapeDtypeStruct((blocks, 5 * CB, tile, tile), jnp.float32)
     rounded = jax.ShapeDtypeStruct((span, 5 * width), jnp.bfloat16)
-    carried = ()
-    for index, phase in enumerate(PHASES):
-        last = index == len(PHASES) - 1
-        results = pl.pallas_call(
-            functools.partial(product_kernel, slabs, parts, phase, last),
-            out_shape=(rounded, sums) if last else (sums,),
-            in_specs=smem(3) + vmem(len(phase) + 2 + len(carried)),
-            out_specs=(vmem(1)[0],) * (1 + last),
-            scratch_shapes=[pltpu.VMEM((9 * blocks, tile, kp * tile), jnp.bfloat16)]
-            + column_scratch(9),
-            input_output_aliases={len(phase) + 5: int(last)} if carried else {},
-            compiler_params=grant(8),
-            cost_estimate=cost(1 << 30, 1 << 24),
-            name="product",
-        )(
-            a_cols, over_rows, over_cols, *(sources[i] for i in phase), a_tiles, over_tiles,
-            *carried,
-        )
-        carried = results[-1:]
-    product = results[0]
+    product, acc = pl.pallas_call(
+        functools.partial(product_kernel, slabs, parts),
+        out_shape=(rounded, sums),
+        in_specs=smem(3) + vmem(10),
+        out_specs=vmem(2),
+        scratch_shapes=[pltpu.VMEM((9 * blocks, tile, kp * tile), jnp.bfloat16)]
+        + column_scratch(9),
+        compiler_params=grant(8),
+        cost_estimate=cost(1 << 30, 1 << 24),
+        name="product",
+    )(a_cols, over_rows, over_cols, *sources[:LAST], *sources[LAST + 1 :], a_tiles, over_tiles)
+    acc, product = pl.pallas_call(
+        functools.partial(last_kernel, slabs, parts),
+        out_shape=(sums, rounded),
+        in_specs=smem(3) + vmem(5),
+        out_specs=vmem(2),
+        scratch_shapes=[pltpu.VMEM((blocks, tile, kp * tile), jnp.bfloat16)]
+        + column_scratch(1),
+        input_output_aliases={6: 0, 7: 1},
+        compiler_params=grant(4),
+        cost_estimate=cost(1 << 30, 1 << 24),
+        name="last",
+    )(a_cols, over_rows, over_cols, sources[LAST], a_tiles, over_tiles, acc, product)
     product_mate = send(product, "pair")
 
     kinds = [jnp.bfloat16] * 3 + [jnp.float32, jnp.bfloat16, jnp.float32]

time: 47.6 us -> 46.7 us (0.981)
  the two profiles are of different devices: /device:TPU:0 before, /device:TPU:8 now
where the time goes in v4:
time: 46.7 us; the launch traced here: 46.5 us
  waiting for transfers between devices  21.4 us (46%)
  starting transfers between devices  13.6 us (29%)
  Pallas kernels  5.81 us (12%)
  local copies, waits for them, and re-layouts  3.93 us (8%)
  other arithmetic  1.65 us (4%)
    ppermute x14, waiting for transfers between devices, exchange(): return lax.ppermute(value, AXES, pairs)  21.4 us
    ppermute x14, starting transfers between devices, exchange(): return lax.ppermute(value, AXES, pairs)  13.6 us
    unnamed x10, local copies, waits for them, and re-layouts  3.91 us
    pallas_call x1, Pallas kernels, fast_body(): pl.pallas_call(functools.partial(product_kernel, slabs, parts), out_shape...  2.33 us
    pallas_call x1, Pallas kernels, fast_body(): pl.pallas_call(functools.partial(prepare_kernel, kp), out_shape=jax.Shape...  1.26 us
    pallas_call x1, Pallas kernels, fast_body(): pl.pallas_call(functools.partial(final_kernel, slabs), out_shape=jax.Shap...  0.95 us
    concatenate x1, other arithmetic, pack(): jnp.concatenate([p_tiles.reshape(blocks, kp * tile, tile), cols], axis=1)  0.94 us
  transfers between devices with their start and end apart: 14, of which 6 were waited for; matrix products, arithmetic and copies ran while one was open for 0% of the time, Pallas kernels for 8%

profile of v4, /device:TPU:8, one launch (start us, length us, event | category | flops | bytes accessed | tf_op | source)
XLA Modules:
  0.0 46.5 jit_solution(358528636224736445)
XLA Ops:
  0.0 0.7 %convert.4 = bf16[2,3]{1,0:T(2,128)(2,1)S(1)} convert(s32[2,3]{1,0:T(2,128)} %param.13) | non-fusion elementwise | flops 6 | bytes 36 | tf_op jit(solution)/shard_map/convert
  0.7 0.9 %pad_maximum_fusion.own.refs_0_ = bf16[2,400,128]{2,1,0:T(8,128)(2,1)S(1)} fusion(bf16[2,16,128]{2,1,0:T(8,128)(2,1)S(1)} %broadcast_in_dim.2, bf16[2,384,128]{2,1,0:T(8,128)(2,1)} %bitcast.1), kind=kLoop, calls=%fused_computation.1 | loop fusion | flops 409600 | bytes 409600 | tf_op jit(solution)/shard_map/concatenate | solution.py:51
  1.6 1.6 %collective-permute-start.4 = (bf16[2,400,128]{2,1,0:T(8,128)(2,1)S(1)}, bf16[2,400,128]{2,1,0:T(8,128)(2,1)S(1)}, u32[]{:S(2)}, u32[]{:S(2)}) collective-permute-start(bf16[2,400,128]{2,1,0:T(8,128)(2,1)S(1)} %pad_maximum_fusion.own.refs_0_), channel_id=1, source_target_pairs={{0,4},{1,5},{2,6},{3,7},{4,0},{5,1},{6,2},{7,3},{8,12},{9,13},{10,... | collective-permute-start | bytes 614408 | tf_op jit(solution)/shard_map/ppermute | solution.py:23
  3.2 0.4 collective-permute-start.3
  3.7 1.5 %collective-permute-start = (bf16[2,400,128]{2,1,0:T(8,128)(2,1)S(1)}, bf16[2,400,128]{2,1,0:T(8,128)(2,1)S(1)}, u32[]{:S(2)}, u32[]{:S(2)}) collective-permute-start(bf16[2,400,128]{2,1,0:T(8,128)(2,1)S(1)} %pad_maximum_fusion.own.refs_0_), channel_id=1, source_target_pairs={{0,1},{1,0},{2,3},{3,2},{4,5},{5,4},{6,7},{7,6},{8,9},{9,8},{10,11... | collective-permute-start | bytes 614408 | tf_op jit(solution)/shard_map/ppermute | solution.py:23
  5.2 7.7 %collective-permute-done.4.refs_3_ = bf16[2,400,128]{2,1,0:T(8,128)(2,1)S(1)} collective-permute-done((bf16[2,400,128]{2,1,0:T(8,128)(2,1)S(1)}, bf16[2,400,128]{2,1,0:T(8,128)(2,1)S(1)}, u32[]{:S(2)}, u32[]{:S(2)}) %collective-permute-start.4) | collective-permute-done | bytes 204832 | tf_op jit(solution)/shard_map/ppermute | solution.py:23
  12.9 1.6 %collective-permute-start.5 = (bf16[2,400,128]{2,1,0:T(8,128)(2,1)S(1)}, bf16[2,400,128]{2,1,0:T(8,128)(2,1)S(1)}, u32[]{:S(2)}, u32[]{:S(2)}) collective-permute-start(bf16[2,400,128]{2,1,0:T(8,128)(2,1)S(1)} %collective-permute-done.4.refs_3_), channel_id=1, source_target_pairs={{0,1},{1,0},{2,3},{3,2},{4,5},{5,4},{6,7},{7,6},{8,9},{9,8},{10,11... | collective-permute-start | bytes 614408 | tf_op jit(solution)/shard_map/ppermute | solution.py:23
  14.5 0.0 collective-permute-done.1.refs_6_
  14.5 0.0 collective-permute-start.7
  14.5 0.9 %collective-permute-start.2 = (bf16[2,400,128]{2,1,0:T(8,128)(2,1)S(1)}, bf16[2,400,128]{2,1,0:T(8,128)(2,1)S(1)}, u32[]{:S(2)}, u32[]{:S(2)}) collective-permute-start(bf16[2,400,128]{2,1,0:T(8,128)(2,1)S(1)} %collective-permute-done.1.refs_6_), channel_id=1, source_target_pairs={{0,8},{1,2},{2,1},{3,11},{4,12},{5,6},{6,5},{7,15},{8,0},{9,10},{1... | collective-permute-start | bytes 614408 | tf_op jit(solution)/shard_map/ppermute | solution.py:23
  15.5 3.2 %collective-permute-done.6.refs_5_ = bf16[2,400,128]{2,1,0:T(8,128)(2,1)S(1)} collective-permute-done((bf16[2,400,128]{2,1,0:T(8,128)(2,1)S(1)}, bf16[2,400,128]{2,1,0:T(8,128)(2,1)S(1)}, u32[]{:S(2)}, u32[]{:S(2)}) %collective-permute-start.6) | collective-permute-done | bytes 204832 | tf_op jit(solution)/shard_map/ppermute | solution.py:23
  18.7 1.0 %copy-done = bf16[2,7,128,128]{3,2,1,0:T(8,128)(2,1)S(1)} copy-done((bf16[2,7,128,128]{3,2,1,0:T(8,128)(2,1)S(1)}, bf16[2,7,128,128]{3,2,1,0:T(8,128)(2,1)}, u32[]{:S(2)}) %copy-start) | copy-done | bytes 458776
  19.7 0.9 %copy-done.1 = bf16[4,128,128]{2,1,0:T(8,128)(2,1)S(1)} copy-done((bf16[4,128,128]{2,1,0:T(8,128)(2,1)S(1)}, bf16[4,128,128]{2,1,0:T(8,128)(2,1)}, u32[]{:S(2)}) %copy-start.1) | copy-done | bytes 131096
  20.6 0.7 %copy-done.2 = s32[2,7]{1,0:T(2,128)S(1)} copy-done((s32[2,7]{1,0:T(2,128)S(1)}, s32[2,7]{1,0:T(2,128)}, u32[]{:S(2)}) %copy-start.2) | copy-done | bytes 80
  21.3 0.7 %copy-done.3 = s32[4]{0:T(128)S(1)} copy-done((s32[4]{0:T(128)S(1)}, s32[4]{0:T(128)}, u32[]{:S(2)}) %copy-start.3) | copy-done | bytes 40
  21.9 0.7 %copy-done.4 = s32[4]{0:T(128)S(1)} copy-done((s32[4]{0:T(128)S(1)}, s32[4]{0:T(128)}, u32[]{:S(2)}) %copy-start.4) | copy-done | bytes 40
  22.6 2.3 %product.1 = (bf16[256,1280]{1,0:T(8,128)(2,1)S(1)}, f32[2,10,128,128]{3,2,1,0:T(8,128)S(1)}) custom-call(s32[2,7]{1,0:T(2,128)S(1)} %copy-done.2, s32[4]{0:T(128)S(1)} %copy-done.3, s32[4]{0:T(128)S(1)} %copy-done.4, bf16[2,400,128]{2,1,0:T(8,128)(2,1)S(1)} %pad_maximum_fusion.own.refs_0_, bf16[2,400,128]{2,1,0:T(8,128)(2,1)S(1)} %collective-permute-done.mate.refs_1_, ...), custom_call_target="tpu_custom_call" | custom-call | flops 1073741824 | bytes 16777216 | tf_op jit(solution)/shard_map/product/pallas_call | solution.py:271
  24.9 0.6 %last.1 = (f32[2,10,128,128]{3,2,1,0:T(8,128)S(1)}, bf16[256,1280]{1,0:T(8,128)(2,1)S(1)}) custom-call(s32[2,7]{1,0:T(2,128)S(1)} %copy-done.2, s32[4]{0:T(128)S(1)} %copy-done.3, s32[4]{0:T(128)S(1)} %copy-done.4, bf16[2,400,128]{2,1,0:T(8,128)(2,1)S(1)} %collective-permute-done.2.source, ...), custom_call_target="tpu_custom_call", output_to_operand_aliasing={{0}: (6, {}), {1}: (7, {})} | custom-call | flops 1073741824 | bytes 16777216 | tf_op jit(solution)/shard_map/last/pallas_call | solution.py:282
  25.6 0.7 %collective-permute-start.8 = (bf16[256,1280]{1,0:T(8,128)(2,1)S(1)}, bf16[256,1280]{1,0:T(8,128)(2,1)S(1)}, u32[]{:S(2)}, u32[]{:S(2)}) collective-permute-start(bf16[256,1280]{1,0:T(8,128)(2,1)S(1)} %get-tuple-element.16.own), channel_id=1, source_target_pairs={{0,1},{1,0},{2,3},{3,2},{4,5},{5,4},{6,7},{7,6},{8,9},{9,8},{10,11... | collective-permute-start | bytes 1966088 | tf_op jit(solution)/shard_map/ppermute | solution.py:23
  26.3 1.3 %prepare.1.left = bf16[6,64,512]{2,1,0:T(8,128)(2,1)S(1)} custom-call(bf16[2,400,128]{2,1,0:T(8,128)(2,1)S(1)} %pad_maximum_fusion.own.refs_0_, bf16[2,400,128]{2,1,0:T(8,128)(2,1)S(1)} %collective-permute-done.mate.refs_1_), custom_call_target="tpu_custom_call" | custom-call | flops 1073741824 | bytes 16777216 | tf_op jit(solution)/shard_map/prepare/pallas_call | solution.py:253
  27.6 0.5 collective-permute-done.8.mate
  28.0 0.7 %partial.1 = (bf16[64,1280]{1,0:T(8,128)(2,1)S(1)}, bf16[64,1280]{1,0:T(8,128)(2,1)S(1)}, bf16[64,1280]{1,0:T(8,128)(2,1)S(1)}, f32[64,1280]{1,0:T(8,128)S(1)}, ...) custom-call(bf16[6,64,512]{2,1,0:T(8,128)(2,1)S(1)} %prepare.1.left, bf16[256,1280]{1,0:T(8,128)(2,1)S(1)} %get-tuple-element.16.own, ...), custom_call_target="tpu_custom_call" | custom-call | flops 536870912 | bytes 4194304 | tf_op jit(solution)/shard_map/partial/pallas_call | solution.py:297
  28.7 2.2 %collective-permute-start.12 = (bf16[64,1280]{1,0:T(8,128)(2,1)S(1)}, bf16[64,1280]{1,0:T(8,128)(2,1)S(1)}, u32[]{:S(2)}, u32[]{:S(2)}) collective-permute-start(bf16[64,1280]{1,0:T(8,128)(2,1)S(1)} %get-tuple-element.22), channel_id=1, source_target_pairs={{0,2},{1,3},{2,0},{3,1},{4,6},{5,7},{6,4},{7,5},{8,10},{9,11},{10,... | collective-permute-start | bytes 491528 | tf_op jit(solution)/shard_map/ppermute | solution.py:23
  30.9 0.1 collective-permute-start.9
  30.9 1.4 %collective-permute-start.10 = (bf16[64,1280]{1,0:T(8,128)(2,1)S(1)}, bf16[64,1280]{1,0:T(8,128)(2,1)S(1)}, u32[]{:S(2)}, u32[]{:S(2)}) collective-permute-start(bf16[64,1280]{1,0:T(8,128)(2,1)S(1)} %get-tuple-element.19), channel_id=1, source_target_pairs={{0,4},{1,5},{2,6},{3,7},{4,0},{5,1},{6,2},{7,3},{8,12},{9,13},{10,... | collective-permute-start | bytes 491528 | tf_op jit(solution)/shard_map/ppermute | solution.py:23
  32.3 2.0 %collective-permute-start.11 = (bf16[64,1280]{1,0:T(8,128)(2,1)S(1)}, bf16[64,1280]{1,0:T(8,128)(2,1)S(1)}, u32[]{:S(2)}, u32[]{:S(2)}) collective-permute-start(bf16[64,1280]{1,0:T(8,128)(2,1)S(1)} %get-tuple-element.20), channel_id=1, source_target_pairs={{0,6},{1,7},{2,4},{3,5},{4,2},{5,3},{6,0},{7,1},{8,14},{9,15},{10,... | collective-permute-start | bytes 491528 | tf_op jit(solution)/shard_map/ppermute | solution.py:23
  34.4 1.6 %collective-permute-done.12 = bf16[64,1280]{1,0:T(8,128)(2,1)S(1)} collective-permute-done((bf16[64,1280]{1,0:T(8,128)(2,1)S(1)}, bf16[64,1280]{1,0:T(8,128)(2,1)S(1)}, u32[]{:S(2)}, u32[]{:S(2)}) %collective-permute-start.12) | collective-permute-done | bytes 163872 | tf_op jit(solution)/shard_map/ppermute | solution.py:23
  35.9 1.1 %collective-permute-start.13 = (bf16[64,1280]{1,0:T(8,128)(2,1)S(1)}, bf16[64,1280]{1,0:T(8,128)(2,1)S(1)}, u32[]{:S(2)}, u32[]{:S(2)}) collective-permute-start(bf16[64,1280]{1,0:T(8,128)(2,1)S(1)} %add_convert_fusion), channel_id=1, source_target_pairs={{0,1},{1,0},{2,3},{3,2},{4,8},{5,9},{6,10},{7,11},{8,4},{9,5},{10,... | collective-permute-start | bytes 491528 | tf_op jit(solution)/shard_map/ppermute | solution.py:23
  37.0 2.4 %collective-permute-done.9.across = bf16[64,1280]{1,0:T(8,128)(2,1)S(1)} collective-permute-done((bf16[64,1280]{1,0:T(8,128)(2,1)S(1)}, bf16[64,1280]{1,0:T(8,128)(2,1)S(1)}, u32[]{:S(2)}, u32[]{:S(2)}) %collective-permute-start.9) | collective-permute-done | bytes 163872 | tf_op jit(solution)/shard_map/ppermute | solution.py:23
  39.4 0.0 collective-permute-done.10.even
  39.4 6.1 %collective-permute-done.11.even_x = bf16[64,1280]{1,0:T(8,128)(2,1)S(1)} collective-permute-done((bf16[64,1280]{1,0:T(8,128)(2,1)S(1)}, bf16[64,1280]{1,0:T(8,128)(2,1)S(1)}, u32[]{:S(2)}, u32[]{:S(2)}) %collective-permute-start.11) | collective-permute-done | bytes 163872 | tf_op jit(solution)/shard_map/ppermute | solution.py:23
  45.5 1.0 %final.1 = f32[64,1792]{1,0:T(8,128)} custom-call(f32[64,1280]{1,0:T(8,128)S(1)} %get-tuple-element.17.own, bf16[64,1280]{1,0:T(8,128)(2,1)S(1)} %collective-permute-done.9.across, bf16[64,1280]{1,0:T(8,128)(2,1)S(1)} %collective-permute-done.10.even, bf16[64,1280]{1,0:T(8,128)(2,1)S(1)} %collective-permute-done.11.even_x, ...), custom_call_target="tpu_custom_call" | custom-call | tf_op jit(solution)/shard_map/final/pallas_call | solution.py:311
  (16 shorter events, 0.1 us)
Async XLA Ops:
  1.6 11.3 %collective-permute-start.4 = (bf16[2,400,128]{2,1,0:T(8,128)(2,1)S(1)}, bf16[2,400,128]{2,1,0:T(8,128)(2,1)S(1)}, u32[]{:S(2)}, u32[]{:S(2)}) collective-permute-start(bf16[2,400,128]{2,1,0:T(8,128)(2,1)S(1)} %pad_maximum_fusion.own.refs_0_), channel_id=1, source_target_pairs={{0,4},{1,5},{2,6},{3,7},{4,0},{5,1},{6,2},{7,3},{8,12},{9,13},{10,... | collective-permute-start | bytes 614408 | tf_op jit(solution)/shard_map/ppermute | solution.py:23
  3.2 11.3 %collective-permute-start.1 = (bf16[2,400,128]{2,1,0:T(8,128)(2,1)S(1)}, bf16[2,400,128]{2,1,0:T(8,128)(2,1)S(1)}, u32[]{:S(2)}, u32[]{:S(2)}) collective-permute-start(bf16[2,400,128]{2,1,0:T(8,128)(2,1)S(1)} %pad_maximum_fusion.own.refs_0_), channel_id=1, source_target_pairs={{0,1},{1,0},{2,3},{3,2},{4,8},{5,9},{6,10},{7,11},{8,4},{9,5},{10,... | collective-permute-start | bytes 614408 | tf_op jit(solution)/shard_map/ppermute | solution.py:23
  3.2 11.3 %collective-permute-start.3 = (bf16[2,400,128]{2,1,0:T(8,128)(2,1)S(1)}, bf16[2,400,128]{2,1,0:T(8,128)(2,1)S(1)}, u32[]{:S(2)}, u32[]{:S(2)}) collective-permute-start(bf16[2,400,128]{2,1,0:T(8,128)(2,1)S(1)} %pad_maximum_fusion.own.refs_0_), channel_id=1, source_target_pairs={{0,8},{1,2},{2,1},{3,11},{4,12},{5,6},{6,5},{7,15},{8,0},{9,10},{1... | collective-permute-start | bytes 614408 | tf_op jit(solution)/shard_map/ppermute | solution.py:23
  3.7 11.8 %collective-permute-start = (bf16[2,400,128]{2,1,0:T(8,128)(2,1)S(1)}, bf16[2,400,128]{2,1,0:T(8,128)(2,1)S(1)}, u32[]{:S(2)}, u32[]{:S(2)}) collective-permute-start(bf16[2,400,128]{2,1,0:T(8,128)(2,1)S(1)} %pad_maximum_fusion.own.refs_0_), channel_id=1, source_target_pairs={{0,1},{1,0},{2,3},{3,2},{4,5},{5,4},{6,7},{7,6},{8,9},{9,8},{10,11... | collective-permute-start | bytes 614408 | tf_op jit(solution)/shard_map/ppermute | solution.py:23
  12.9 5.8 %collective-permute-start.6 = (bf16[2,400,128]{2,1,0:T(8,128)(2,1)S(1)}, bf16[2,400,128]{2,1,0:T(8,128)(2,1)S(1)}, u32[]{:S(2)}, u32[]{:S(2)}) collective-permute-start(bf16[2,400,128]{2,1,0:T(8,128)(2,1)S(1)} %collective-permute-done.4.refs_3_), channel_id=1, source_target_pairs={{0,8},{1,2},{2,1},{3,11},{4,12},{5,6},{6,5},{7,15},{8,0},{9,10},{1... | collective-permute-start | bytes 614408 | tf_op jit(solution)/shard_map/ppermute | solution.py:23
  12.9 5.8 %collective-permute-start.5 = (bf16[2,400,128]{2,1,0:T(8,128)(2,1)S(1)}, bf16[2,400,128]{2,1,0:T(8,128)(2,1)S(1)}, u32[]{:S(2)}, u32[]{:S(2)}) collective-permute-start(bf16[2,400,128]{2,1,0:T(8,128)(2,1)S(1)} %collective-permute-done.4.refs_3_), channel_id=1, source_target_pairs={{0,1},{1,0},{2,3},{3,2},{4,5},{5,4},{6,7},{7,6},{8,9},{9,8},{10,11... | collective-permute-start | bytes 614408 | tf_op jit(solution)/shard_map/ppermute | solution.py:23
  14.5 4.2 %collective-permute-start.7 = (bf16[2,400,128]{2,1,0:T(8,128)(2,1)S(1)}, bf16[2,400,128]{2,1,0:T(8,128)(2,1)S(1)}, u32[]{:S(2)}, u32[]{:S(2)}) collective-permute-start(bf16[2,400,128]{2,1,0:T(8,128)(2,1)S(1)} %collective-permute-done.1.refs_6_), channel_id=1, source_target_pairs={{0,1},{1,0},{2,3},{3,2},{4,5},{5,4},{6,7},{7,6},{8,9},{9,8},{10,11... | collective-permute-start | bytes 614408 | tf_op jit(solution)/shard_map/ppermute | solution.py:23
  14.5 10.4 %collective-permute-start.2 = (bf16[2,400,128]{2,1,0:T(8,128)(2,1)S(1)}, bf16[2,400,128]{2,1,0:T(8,128)(2,1)S(1)}, u32[]{:S(2)}, u32[]{:S(2)}) collective-permute-start(bf16[2,400,128]{2,1,0:T(8,128)(2,1)S(1)} %collective-permute-done.1.refs_6_), channel_id=1, source_target_pairs={{0,8},{1,2},{2,1},{3,11},{4,12},{5,6},{6,5},{7,15},{8,0},{9,10},{1... | collective-permute-start | bytes 614408 | tf_op jit(solution)/shard_map/ppermute | solution.py:23
  18.7 1.0 %copy-start = (bf16[2,7,128,128]{3,2,1,0:T(8,128)(2,1)S(1)}, bf16[2,7,128,128]{3,2,1,0:T(8,128)(2,1)}, u32[]{:S(2)}) copy-start(bf16[2,7,128,128]{3,2,1,0:T(8,128)(2,1)} %a_tiles.1) | copy-start | bytes 1376260
  19.7 0.9 %copy-start.1 = (bf16[4,128,128]{2,1,0:T(8,128)(2,1)S(1)}, bf16[4,128,128]{2,1,0:T(8,128)(2,1)}, u32[]{:S(2)}) copy-start(bf16[4,128,128]{2,1,0:T(8,128)(2,1)} %over_tiles.1) | copy-start | bytes 393220
  20.6 0.7 %copy-start.2 = (s32[2,7]{1,0:T(2,128)S(1)}, s32[2,7]{1,0:T(2,128)}, u32[]{:S(2)}) copy-start(s32[2,7]{1,0:T(2,128)} %a_cols.3) | copy-start | bytes 172
  21.3 0.7 %copy-start.3 = (s32[4]{0:T(128)S(1)}, s32[4]{0:T(128)}, u32[]{:S(2)}) copy-start(s32[4]{0:T(128)} %over_rows.3) | copy-start | bytes 52
  21.9 0.7 %copy-start.4 = (s32[4]{0:T(128)S(1)}, s32[4]{0:T(128)}, u32[]{:S(2)}) copy-start(s32[4]{0:T(128)} %over_cols.3) | copy-start | bytes 52
  25.6 2.5 %collective-permute-start.8 = (bf16[256,1280]{1,0:T(8,128)(2,1)S(1)}, bf16[256,1280]{1,0:T(8,128)(2,1)S(1)}, u32[]{:S(2)}, u32[]{:S(2)}) collective-permute-start(bf16[256,1280]{1,0:T(8,128)(2,1)S(1)} %get-tuple-element.16.own), channel_id=1, source_target_pairs={{0,1},{1,0},{2,3},{3,2},{4,5},{5,4},{6,7},{7,6},{8,9},{9,8},{10,11... | collective-permute-start | bytes 1966088 | tf_op jit(solution)/shard_map/ppermute | solution.py:23
  28.7 7.2 %collective-permute-start.12 = (bf16[64,1280]{1,0:T(8,128)(2,1)S(1)}, bf16[64,1280]{1,0:T(8,128)(2,1)S(1)}, u32[]{:S(2)}, u32[]{:S(2)}) collective-permute-start(bf16[64,1280]{1,0:T(8,128)(2,1)S(1)} %get-tuple-element.22), channel_id=1, source_target_pairs={{0,2},{1,3},{2,0},{3,1},{4,6},{5,7},{6,4},{7,5},{8,10},{9,11},{10,... | collective-permute-start | bytes 491528 | tf_op jit(solution)/shard_map/ppermute | solution.py:23
  30.9 8.6 %collective-permute-start.9 = (bf16[64,1280]{1,0:T(8,128)(2,1)S(1)}, bf16[64,1280]{1,0:T(8,128)(2,1)S(1)}, u32[]{:S(2)}, u32[]{:S(2)}) collective-permute-start(bf16[64,1280]{1,0:T(8,128)(2,1)S(1)} %get-tuple-element.18), channel_id=1, source_target_pairs={{0,2},{1,3},{2,0},{3,1},{4,6},{5,7},{6,4},{7,5},{8,10},{9,11},{10,... | collective-permute-start | bytes 491528 | tf_op jit(solution)/shard_map/ppermute | solution.py:23
  30.9 8.5 %collective-permute-start.10 = (bf16[64,1280]{1,0:T(8,128)(2,1)S(1)}, bf16[64,1280]{1,0:T(8,128)(2,1)S(1)}, u32[]{:S(2)}, u32[]{:S(2)}) collective-permute-start(bf16[64,1280]{1,0:T(8,128)(2,1)S(1)} %get-tuple-element.19), channel_id=1, source_target_pairs={{0,4},{1,5},{2,6},{3,7},{4,0},{5,1},{6,2},{7,3},{8,12},{9,13},{10,... | collective-permute-start | bytes 491528 | tf_op jit(solution)/shard_map/ppermute | solution.py:23
  32.3 13.2 %collective-permute-start.11 = (bf16[64,1280]{1,0:T(8,128)(2,1)S(1)}, bf16[64,1280]{1,0:T(8,128)(2,1)S(1)}, u32[]{:S(2)}, u32[]{:S(2)}) collective-permute-start(bf16[64,1280]{1,0:T(8,128)(2,1)S(1)} %get-tuple-element.20), channel_id=1, source_target_pairs={{0,6},{1,7},{2,4},{3,5},{4,2},{5,3},{6,0},{7,1},{8,14},{9,15},{10,... | collective-permute-start | bytes 491528 | tf_op jit(solution)/shard_map/ppermute | solution.py:23
  35.9 9.6 %collective-permute-start.13 = (bf16[64,1280]{1,0:T(8,128)(2,1)S(1)}, bf16[64,1280]{1,0:T(8,128)(2,1)S(1)}, u32[]{:S(2)}, u32[]{:S(2)}) collective-permute-start(bf16[64,1280]{1,0:T(8,128)(2,1)S(1)} %add_convert_fusion), channel_id=1, source_target_pairs={{0,1},{1,0},{2,3},{3,2},{4,8},{5,9},{6,10},{7,11},{8,4},{9,5},{10,... | collective-permute-start | bytes 491528 | tf_op jit(solution)/shard_map/ppermute | solution.py:23

commit v5 on v4

--- a/solution.py
+++ b/solution.py
@@ -10,7 +10,6 @@
 
 CB = 2
 AXES = ("slab", "cross")
-PAD = 16
 LAST = 8
 
 
@@ -40,45 +39,29 @@
         "odd": odd,
         "pair": lambda s, c: (s, c ^ 1),
         "across": across,
+        "across_self": lambda s, c: (s, across(s, c)[1]),
+        "across_y": lambda s, c: across(s, c) if across(s, c)[0] == s else (s ^ 1, c),
+        "across_x": lambda s, c: across(s, c) if across(s, c)[0] == s else (s, parts - 1 - c),
         "other": lambda s, c: (s, c ^ 2),
     }
 
 
-def pack(p_tiles, p_cols):
-    blocks, kp, tile = p_tiles.shape[0], p_tiles.shape[1], p_tiles.shape[-1]
-    cols = jnp.pad(p_cols, ((0, 0), (0, tile - kp)))[:, None, :]
-    cols = jnp.broadcast_to(cols, (blocks, PAD, tile)).astype(jnp.bfloat16)
-    return jnp.concatenate([p_tiles.reshape(blocks, kp * tile, tile), cols], axis=1)
-
-
-def columns_of(sources, cols_v, cols_s, sem):
-    for at, source in sources:
-        for n in range(source.shape[0]):
-            row = source[n, source.shape[1] - PAD :].astype(jnp.float32)
-            cols_v[pl.ds(at + n, 1)] = row[:1].astype(jnp.int32)
-    copy = pltpu.make_async_copy(cols_v, cols_s, sem)
-    copy.start()
-    return copy
-
-
-def prepare_kernel(kp, own, mate, out, cols_v, cols_s, sem):
-    blocks, tile = own.shape[0], own.shape[-1]
+def prepare_kernel(cols, own, mate, out):
+    blocks, kp, tile = own.shape[0], own.shape[1], own.shape[-1]
     half = tile // 2
-    copy = columns_of(((0, own), (blocks, mate)), cols_v, cols_s, sem)
     part = lax.axis_index("cross")
     slab = lax.axis_index("slab")
     lower = lax.rem(part, 2) == 0
     side = lax.div(part, 2)
     even = lax.rem(slab, 2)
     out[...] = jnp.zeros_like(out)
-    copy.wait()
     for d, source in enumerate((own, mate)):
         for n in range(blocks):
             for m in range(kp):
-                piece = source[n, m * tile : (m + 1) * tile, :]
+                piece = source[n, m]
                 piece = jnp.where(lower, piece[:, :half], piece[:, half:])
                 at = (d * blocks + n) * tile
-                q = cols_s[d * blocks + n, m]
+                q = cols[d * blocks + n, m]
                 block, owner = lax.div(q, CB), lax.rem(q, CB)
                 to_even = (block == 2) == (even == 0)
                 place = jnp.where(block == 1, 2, jnp.where(to_even, 1, 0))
@@ -96,6 +79,7 @@
         odd_ok = (r_there >= 0) & (r_there < slabs)
         across_ok = (u_there >= 0) & (u_there < parts)
         self.shift = [r * CB for r in (1, r_even, r_odd) for _ in range(3)]
+        self.r_even, self.u_pair, self.blocks = r_even, u_pair, blocks
         self.first = [
             (3 * r + u) * blocks for r in (1, r_even, r_odd) for u in (1, u_pair, u_across)
         ]
@@ -104,40 +88,44 @@
         ]
 
 
+    def columns(self, col):
+        b = self.blocks
+        r, rest = lax.div(col, 3 * b), lax.rem(col, 3 * b)
+        u, n = lax.div(rest, b), lax.rem(rest, b)
+        i = jnp.where(r == 1, 0, jnp.where(r == self.r_even, 1, 2))
+        k = jnp.where(u == 1, 0, jnp.where(u == self.u_pair, 1, 2))
+        return (3 * k + i) * b + n
+
+
 def fetch(source, at, ok, ext):
-    blocks, tile = source.shape[0], source.shape[-1]
-    kp = ext.shape[-1] // tile
+    blocks, kp, tile = source.shape[0], source.shape[1], source.shape[-1]
     for n in range(blocks):
         for m in range(kp):
-            piece = source[n, m * tile : (m + 1) * tile, :]
+            piece = source[n, m]
             if ok is not None:
                 piece = jnp.where(ok, piece, jnp.zeros_like(piece))
             ext[at + n, :, m * tile : (m + 1) * tile] = piece
 
 
-def product_kernel(slabs, parts, a_cols, over_rows, over_cols, *refs):
+def product_kernel(slabs, parts, cols, a_cols, over_rows, over_cols, *refs):
     early = [i for i in range(9) if i != LAST]
     sources, refs = refs[:8], refs[8:]
-    a_tiles, over_tiles, out, acc, ext, cols_v, cols_s, sem = refs
+    a_tiles, over_tiles, out, acc, ext = refs
     blocks, taps, tile = a_tiles.shape[0], a_tiles.shape[1], a_tiles.shape[-1]
     kp = ext.shape[-1] // tile
     place = Place(slabs, parts, blocks)
-    copy = columns_of(
-        [(place.first[i], source) for i, source in zip(early, sources)], cols_v, cols_s, sem
-    )
     for i, source in zip(early, sources):
         fetch(source, place.first[i], place.valid[i], ext)
     for n in range(blocks):
         ext[place.first[LAST] + n] = jnp.zeros(ext.shape[1:], ext.dtype)
-        cols_v[pl.ds(place.first[LAST] + n, 1)] = jnp.zeros((1, tile), jnp.int32)
     acc[...] = jnp.zeros_like(acc)
-    copy.wait()
 
     def add(n, col, matrix):
         piece = jnp.dot(matrix, ext[col], preferred_element_type=jnp.float32)
-        shift = (col // (3 * blocks)) * CB
+        shift = lax.div(col, 3 * blocks) * CB
+        row = place.columns(col)
         for m in range(kp):
-            acc[n, shift + cols_s[col, m]] += piece[:, m * tile : (m + 1) * tile]
+            acc[n, shift + cols[row, m]] += piece[:, m * tile : (m + 1) * tile]
 
     for n in range(blocks):
         for k in range(taps):
@@ -151,8 +139,8 @@
             )
 
 
-def last_kernel(slabs, parts, a_cols, over_rows, over_cols, source, a_tiles, over_tiles,
-                acc_in, out_in, acc, out, ext, cols_v, cols_s, sem):
+def last_kernel(slabs, parts, cols, a_cols, over_rows, over_cols, source, a_tiles, over_tiles,
+                acc_in, out_in, acc, out, ext):
     blocks, taps, tile = a_tiles.shape[0], a_tiles.shape[1], a_tiles.shape[-1]
     kp = ext.shape[-1] // tile
     place = Place(slabs, parts, blocks)
@@ -160,9 +148,8 @@
 
     @pl.when(place.valid[LAST])
     def _():
-        copy = columns_of([(0, source)], cols_v, cols_s, sem)
         fetch(source, 0, None, ext)
-        copy.wait()
+        base = ((LAST % 3) * 3 + LAST // 3) * blocks
 
         def visit(n, col, matrix):
             row = col - first
@@ -172,7 +159,7 @@
                 piece = jnp.dot(matrix[...], ext[row], preferred_element_type=jnp.float32)
                 at = pl.multiple_of(n * tile, tile)
                 for m in range(kp):
-                    j = shift + cols_s[row, m]
+                    j = shift + cols[base + row, m]
                     total = acc[n, j] + piece[:, m * tile : (m + 1) * tile]
                     acc[n, j] = total
                     to = pl.multiple_of(j * tile, tile)
@@ -239,29 +226,28 @@
     def send(value, name):
         return exchange(value, slabs, parts, step[name])
 
-    def column_scratch(count):
-        return [
-            pltpu.VMEM((count * blocks, tile), jnp.int32),
-            pltpu.SMEM((count * blocks, tile), jnp.int32),
-            pltpu.SemaphoreType.DMA,
-        ]
-
-    own = pack(p_tiles, p_cols)
+    own = p_tiles
+    cols_even = send(p_cols, "even")
+    cols_odd = send(p_cols, "odd")
+    near = jnp.concatenate([p_cols, cols_even, cols_odd])
+    cols_pair = send(near, "pair")
+    cols_across = send(near, "across")
+    pair_cols = jnp.concatenate([p_cols, cols_pair[:blocks]])
+    all_cols = jnp.concatenate([near, cols_pair, cols_across])
     even = send(own, "even")
     mate = send(own, "pair")
-    own_x = send(own, "across")
+    own_x = send(own, "across_x")
     left = pl.pallas_call(
-        functools.partial(prepare_kernel, kp),
+        prepare_kernel,
         out_shape=jax.ShapeDtypeStruct((3 * CB, half, 2 * span), jnp.bfloat16),
-        in_specs=vmem(2),
+        in_specs=smem(1) + vmem(2),
         out_specs=vmem(1)[0],
-        scratch_shapes=column_scratch(2),
         compiler_params=grant(4),
         cost_estimate=cost(1 << 30, 1 << 24),
         name="prepare",
-    )(own, mate)
+    )(pair_cols, own, mate)
     odd = send(own, "odd")
-    even_x = send(even, "across")
+    even_x = send(even, "across_self")
     even_p = send(even, "pair")
     odd_x = send(odd, "across")
     odd_p = send(odd, "pair")
@@ -271,26 +257,24 @@
     product, acc = pl.pallas_call(
         functools.partial(product_kernel, slabs, parts),
         out_shape=(rounded, sums),
-        in_specs=smem(3) + vmem(10),
+        in_specs=smem(4) + vmem(10),
         out_specs=vmem(2),
-        scratch_shapes=[pltpu.VMEM((9 * blocks, tile, kp * tile), jnp.bfloat16)]
-        + column_scratch(9),
+        scratch_shapes=[pltpu.VMEM((9 * blocks, tile, kp * tile), jnp.bfloat16)],
         compiler_params=grant(8),
         cost_estimate=cost(1 << 30, 1 << 24),
         name="product",
-    )(a_cols, over_rows, over_cols, *sources[:LAST], *sources[LAST + 1 :], a_tiles, over_tiles)
+    )(all_cols, a_cols, over_rows, over_cols, *sources[:LAST], *sources[LAST + 1 :], a_tiles, over_tiles)
     acc, product = pl.pallas_call(
         functools.partial(last_kernel, slabs, parts),
         out_shape=(sums, rounded),
-        in_specs=smem(3) + vmem(5),
+        in_specs=smem(4) + vmem(5),
         out_specs=vmem(2),
-        scratch_shapes=[pltpu.VMEM((blocks, tile, kp * tile), jnp.bfloat16)]
-        + column_scratch(1),
-        input_output_aliases={6: 0, 7: 1},
+        scratch_shapes=[pltpu.VMEM((blocks, tile, kp * tile), jnp.bfloat16)],
+        input_output_aliases={7: 0, 8: 1},
         compiler_params=grant(4),
         cost_estimate=cost(1 << 30, 1 << 24),
         name="last",
-    )(a_cols, over_rows, over_cols, sources[LAST], a_tiles, over_tiles, acc, product)
+    )(all_cols, a_cols, over_rows, over_cols, sources[LAST], a_tiles, over_tiles, acc, product)
     product_mate = send(product, "pair")
 
     kinds = [jnp.bfloat16] * 3 + [jnp.float32, jnp.bfloat16, jnp.float32]

time: 46.7 us -> 50.3 us (1.077)
  starting transfers between devices: 13.6 us -> 20.8 us
  waiting for transfers between devices: 21.4 us -> 17.1 us
  local copies, waits for them, and re-layouts: 3.93 us -> 5.71 us
  other arithmetic: 1.65 us -> 0.73 us
    ppermute x14 -> x18, starting transfers between devices: 13.6 us -> 20.8 us  [exchange(): return lax.ppermute(value, AXES, pairs)]
    ppermute x14 -> x18, waiting for transfers between devices: 21.4 us -> 17.1 us  [exchange(): return lax.ppermute(value, AXES, pairs)]
    unnamed x10 -> x16, local copies, waits for them, and re-layouts: 3.91 us -> 4.85 us
    concatenate x0 -> x1, local copies, waits for them, and re-layouts: none -> 0.86 us  [fast_body(): all_cols = jnp.concatenate([near, cols_pair, cols_across])]
    another operation x1 -> x0, other arithmetic: 0.68 us -> none
  transfers between devices with their start and end apart: 14 -> 18, of which waited for: 6 -> 6; matrix products, arithmetic and copies ran while one was open for 0% -> 3% of each run, Pallas kernels for 8% -> 6%
where the time goes in v5:
time: 50.3 us; the launch traced here: 50 us
  starting transfers between devices  20.8 us (41%)
  waiting for transfers between devices  17.1 us (34%)
  local copies, waits for them, and re-layouts  5.71 us (11%)
  Pallas kernels  5.51 us (11%)
  other arithmetic  0.73 us (1%)
    ppermute x18, starting transfers between devices, exchange(): return lax.ppermute(value, AXES, pairs)  20.8 us
    ppermute x18, waiting for transfers between devices, exchange(): return lax.ppermute(value, AXES, pairs)  17.1 us
    unnamed x16, local copies, waits for them, and re-layouts  4.85 us
    pallas_call x1, Pallas kernels, fast_body(): pl.pallas_call(functools.partial(product_kernel, slabs, parts), out_shape...  1.87 us
    pallas_call x1, Pallas kernels, fast_body(): pl.pallas_call(prepare_kernel, out_shape=jax.ShapeDtypeStruct((3 * CB, ha...  1.23 us
  transfers between devices with their start and end apart: 18, of which 6 were waited for; matrix products, arithmetic and copies ran while one was open for 3% of the time, Pallas kernels for 6%

profile of v5, /device:TPU:8, one launch (start us, length us, event | category | flops | bytes accessed | tf_op | source)
XLA Modules:
  0.0 50.0 jit_solution(11525187058123833190)
XLA Ops:
  0.0 1.5 %collective-permute-start.8 = (bf16[2,3,128,128]{3,2,1,0:T(8,128)(2,1)}, bf16[2,3,128,128]{3,2,1,0:T(8,128)(2,1)S(1)}, u32[]{:S(2)}, u32[]{:S(2)}) collective-permute-start(bf16[2,3,128,128]{3,2,1,0:T(8,128)(2,1)} %refs_0_.1), channel_id=1, source_target_pairs={{0,4},{1,5},{2,6},{3,7},{4,0},{5,1},{6,2},{7,3},{8,12},{9,13},{10,... | collective-permute-start | bytes 589832 | tf_op jit(solution)/shard_map/ppermute | solution.py:22
  1.5 3.0 %collective-permute-start = (s32[2,3]{1,0:T(2,128)}, s32[2,3]{1,0:T(2,128)S(1)}, u32[]{:S(2)}, u32[]{:S(2)}) collective-permute-start(s32[2,3]{1,0:T(2,128)} %param.13), channel_id=1, source_target_pairs={{0,4},{1,5},{2,6},{3,7},{4,0},{5,1},{6,2},{7,3},{8,12},{9,13},{10,... | collective-permute-start | bytes 80 | tf_op jit(solution)/shard_map/ppermute | solution.py:22
  4.6 6.6 %collective-permute-done = s32[2,3]{1,0:T(2,128)S(1)} collective-permute-done((s32[2,3]{1,0:T(2,128)}, s32[2,3]{1,0:T(2,128)S(1)}, u32[]{:S(2)}, u32[]{:S(2)}) %collective-permute-start) | collective-permute-done | bytes 56 | tf_op jit(solution)/shard_map/ppermute | solution.py:22
  11.2 0.7 %pad_add_fusion = s32[6,3]{1,0:T(8,128)S(1)} fusion(s32[2,3]{1,0:T(2,128)S(1)} %collective-permute-done.1, s32[2,3]{1,0:T(2,128)S(1)} %collective-permute-done, s32[2,3]{1,0:T(2,128)} %param.13), kind=kLoop, calls=%fused_computation.1 | loop fusion | flops 36 | bytes 144 | tf_op jit(solution)/shard_map/concatenate | solution.py:232
  11.9 1.6 %collective-permute-start.7 = (bf16[2,3,128,128]{3,2,1,0:T(8,128)(2,1)}, bf16[2,3,128,128]{3,2,1,0:T(8,128)(2,1)S(1)}, u32[]{:S(2)}, u32[]{:S(2)}) collective-permute-start(bf16[2,3,128,128]{3,2,1,0:T(8,128)(2,1)} %refs_0_.1), channel_id=1, source_target_pairs={{0,3},{1,2},{2,1},{3,0},{4,7},{5,6},{6,5},{7,4},{8,11},{9,10},{10,... | collective-permute-start | bytes 589832 | tf_op jit(solution)/shard_map/ppermute | solution.py:22
  13.5 0.7 %collective-permute-start.10 = (bf16[2,3,128,128]{3,2,1,0:T(8,128)(2,1)S(1)}, bf16[2,3,128,128]{3,2,1,0:T(8,128)(2,1)S(1)}, u32[]{:S(2)}, u32[]{:S(2)}) collective-permute-start(bf16[2,3,128,128]{3,2,1,0:T(8,128)(2,1)S(1)} %collective-permute-done.8.refs_3_), channel_id=1, source_target_pairs={{0,0},{1,2},{2,1},{3,3},{4,4},{5,6},{6,5},{7,7},{8,8},{9,10},{10,9... | collective-permute-start | bytes 589832 | tf_op jit(solution)/shard_map/ppermute | solution.py:22
  14.2 3.1 %collective-permute-start.11 = (bf16[2,3,128,128]{3,2,1,0:T(8,128)(2,1)S(1)}, bf16[2,3,128,128]{3,2,1,0:T(8,128)(2,1)S(1)}, u32[]{:S(2)}, u32[]{:S(2)}) collective-permute-start(bf16[2,3,128,128]{3,2,1,0:T(8,128)(2,1)S(1)} %collective-permute-done.5.refs_6_), channel_id=1, source_target_pairs={{0,1},{1,0},{2,3},{3,2},{4,5},{5,4},{6,7},{7,6},{8,9},{9,8},{10,11... | collective-permute-start | bytes 589832 | tf_op jit(solution)/shard_map/ppermute | solution.py:22
  17.3 1.9 %collective-permute-start.9 = (bf16[2,3,128,128]{3,2,1,0:T(8,128)(2,1)S(1)}, bf16[2,3,128,128]{3,2,1,0:T(8,128)(2,1)S(1)}, u32[]{:S(2)}, u32[]{:S(2)}) collective-permute-start(bf16[2,3,128,128]{3,2,1,0:T(8,128)(2,1)S(1)} %collective-permute-done.8.refs_3_), channel_id=1, source_target_pairs={{0,1},{1,0},{2,3},{3,2},{4,5},{5,4},{6,7},{7,6},{8,9},{9,8},{10,11... | collective-permute-start | bytes 589832 | tf_op jit(solution)/shard_map/ppermute | solution.py:22
  19.2 0.9 %concatenate.12.cols = s32[18,3]{1,0:T(8,128)S(1)} concatenate(s32[2,3]{1,0:T(2,128)} %param.13, s32[2,3]{1,0:T(2,128)S(1)} %collective-permute-done, s32[2,3]{1,0:T(2,128)S(1)} %collective-permute-done.1, s32[6,3]{1,0:T(8,128)S(1)} %collective-permute-done.2, s32[6,3]{1,0:T(8,128)S(1)} %collective-permute-done.4), dimensions={0} | concatenate | bytes 432 | tf_op jit(solution)/shard_map/concatenate | solution.py:236
  20.1 0.2 collective-permute-done.9.refs_4_
  20.3 1.0 %copy-done = bf16[2,7,128,128]{3,2,1,0:T(8,128)(2,1)S(1)} copy-done((bf16[2,7,128,128]{3,2,1,0:T(8,128)(2,1)S(1)}, bf16[2,7,128,128]{3,2,1,0:T(8,128)(2,1)}, u32[]{:S(2)}) %copy-start) | copy-done | bytes 458776
  21.3 0.9 %copy-done.1 = bf16[2,3,128,128]{3,2,1,0:T(8,128)(2,1)S(1)} copy-done((bf16[2,3,128,128]{3,2,1,0:T(8,128)(2,1)S(1)}, bf16[2,3,128,128]{3,2,1,0:T(8,128)(2,1)}, u32[]{:S(2)}) %copy-start.1) | copy-done | bytes 196632
  22.2 0.9 %copy-done.3 = bf16[4,128,128]{2,1,0:T(8,128)(2,1)S(1)} copy-done((bf16[4,128,128]{2,1,0:T(8,128)(2,1)S(1)}, bf16[4,128,128]{2,1,0:T(8,128)(2,1)}, u32[]{:S(2)}) %copy-start.3) | copy-done | bytes 131096
  23.1 0.7 %copy-done.4 = s32[2,7]{1,0:T(2,128)S(1)} copy-done((s32[2,7]{1,0:T(2,128)S(1)}, s32[2,7]{1,0:T(2,128)}, u32[]{:S(2)}) %copy-start.4) | copy-done | bytes 80
  23.8 0.7 %copy-done.5 = s32[4]{0:T(128)S(1)} copy-done((s32[4]{0:T(128)S(1)}, s32[4]{0:T(128)}, u32[]{:S(2)}) %copy-start.5) | copy-done | bytes 40
  24.5 0.7 %copy-done.6 = s32[4]{0:T(128)S(1)} copy-done((s32[4]{0:T(128)S(1)}, s32[4]{0:T(128)}, u32[]{:S(2)}) %copy-start.6) | copy-done | bytes 40
  25.1 1.9 %product.1 = (bf16[256,1280]{1,0:T(8,128)(2,1)S(1)}, f32[2,10,128,128]{3,2,1,0:T(8,128)S(1)}) custom-call(s32[18,3]{1,0:T(8,128)S(1)} %concatenate.12.cols, s32[2,7]{1,0:T(2,128)S(1)} %copy-done.4, s32[4]{0:T(128)S(1)} %copy-done.5, s32[4]{0:T(128)S(1)} %copy-done.6, bf16[2,3,128,128]{3,2,1,0:T(8,128)(2,1)S(1)} %copy-done.1, ...), custom_call_target="tpu_custom_call" | custom-call | flops 1073741824 | bytes 16777216 | tf_op jit(solution)/shard_map/product/pallas_call | solution.py:257
  27.0 0.0 copy-start.7
  27.0 0.8 %last.1 = (f32[2,10,128,128]{3,2,1,0:T(8,128)S(1)}, bf16[256,1280]{1,0:T(8,128)(2,1)S(1)}) custom-call(s32[18,3]{1,0:T(8,128)S(1)} %concatenate.12.cols, s32[2,7]{1,0:T(2,128)S(1)} %copy-done.4, s32[4]{0:T(128)S(1)} %copy-done.5, s32[4]{0:T(128)S(1)} %copy-done.6, ...), custom_call_target="tpu_custom_call", output_to_operand_aliasing={{0}: (7, {}), {1}: (8, {})} | custom-call | flops 1073741824 | bytes 16777216 | tf_op jit(solution)/shard_map/last/pallas_call | solution.py:267
  27.8 2.0 %collective-permute-start.12 = (bf16[256,1280]{1,0:T(8,128)(2,1)S(1)}, bf16[256,1280]{1,0:T(8,128)(2,1)S(1)}, u32[]{:S(2)}, u32[]{:S(2)}) collective-permute-start(bf16[256,1280]{1,0:T(8,128)(2,1)S(1)} %get-tuple-element.16.own), channel_id=1, source_target_pairs={{0,1},{1,0},{2,3},{3,2},{4,5},{5,4},{6,7},{7,6},{8,9},{9,8},{10,11... | collective-permute-start | bytes 1966088 | tf_op jit(solution)/shard_map/ppermute | solution.py:22
  29.8 1.2 %prepare.1.left = bf16[6,64,512]{2,1,0:T(8,128)(2,1)S(1)} custom-call(s32[4,3]{1,0:T(4,128)S(1)} %pad_add_fusion.1.cols, bf16[2,3,128,128]{3,2,1,0:T(8,128)(2,1)S(1)} %copy-done.2, bf16[2,3,128,128]{3,2,1,0:T(8,128)(2,1)S(1)} %collective-permute-done.3.mate.refs_1_), custom_call_target="tpu_custom_call" | custom-call | flops 1073741824 | bytes 16777216 | tf_op jit(solution)/shard_map/prepare/pallas_call | solution.py:240
  31.1 0.5 collective-permute-done.12.mate
  31.5 0.7 %partial.1 = (bf16[64,1280]{1,0:T(8,128)(2,1)S(1)}, bf16[64,1280]{1,0:T(8,128)(2,1)S(1)}, bf16[64,1280]{1,0:T(8,128)(2,1)S(1)}, f32[64,1280]{1,0:T(8,128)S(1)}, ...) custom-call(bf16[6,64,512]{2,1,0:T(8,128)(2,1)S(1)} %prepare.1.left, bf16[256,1280]{1,0:T(8,128)(2,1)S(1)} %get-tuple-element.16.own, ...), custom_call_target="tpu_custom_call" | custom-call | flops 536870912 | bytes 4194304 | tf_op jit(solution)/shard_map/partial/pallas_call | solution.py:281
  32.2 2.2 %collective-permute-start.16 = (bf16[64,1280]{1,0:T(8,128)(2,1)S(1)}, bf16[64,1280]{1,0:T(8,128)(2,1)S(1)}, u32[]{:S(2)}, u32[]{:S(2)}) collective-permute-start(bf16[64,1280]{1,0:T(8,128)(2,1)S(1)} %get-tuple-element.22), channel_id=1, source_target_pairs={{0,2},{1,3},{2,0},{3,1},{4,6},{5,7},{6,4},{7,5},{8,10},{9,11},{10,... | collective-permute-start | bytes 491528 | tf_op jit(solution)/shard_map/ppermute | solution.py:22
  34.4 0.1 collective-permute-start.13
  34.5 1.3 %collective-permute-start.14 = (bf16[64,1280]{1,0:T(8,128)(2,1)S(1)}, bf16[64,1280]{1,0:T(8,128)(2,1)S(1)}, u32[]{:S(2)}, u32[]{:S(2)}) collective-permute-start(bf16[64,1280]{1,0:T(8,128)(2,1)S(1)} %get-tuple-element.19), channel_id=1, source_target_pairs={{0,4},{1,5},{2,6},{3,7},{4,0},{5,1},{6,2},{7,3},{8,12},{9,13},{10,... | collective-permute-start | bytes 491528 | tf_op jit(solution)/shard_map/ppermute | solution.py:22
  35.8 2.1 %collective-permute-start.15 = (bf16[64,1280]{1,0:T(8,128)(2,1)S(1)}, bf16[64,1280]{1,0:T(8,128)(2,1)S(1)}, u32[]{:S(2)}, u32[]{:S(2)}) collective-permute-start(bf16[64,1280]{1,0:T(8,128)(2,1)S(1)} %get-tuple-element.20), channel_id=1, source_target_pairs={{0,6},{1,7},{2,4},{3,5},{4,2},{5,3},{6,0},{7,1},{8,14},{9,15},{10,... | collective-permute-start | bytes 491528 | tf_op jit(solution)/shard_map/ppermute | solution.py:22
  37.9 1.6 %collective-permute-done.16 = bf16[64,1280]{1,0:T(8,128)(2,1)S(1)} collective-permute-done((bf16[64,1280]{1,0:T(8,128)(2,1)S(1)}, bf16[64,1280]{1,0:T(8,128)(2,1)S(1)}, u32[]{:S(2)}, u32[]{:S(2)}) %collective-permute-start.16) | collective-permute-done | bytes 163872 | tf_op jit(solution)/shard_map/ppermute | solution.py:22
  39.5 1.2 %collective-permute-start.17 = (bf16[64,1280]{1,0:T(8,128)(2,1)S(1)}, bf16[64,1280]{1,0:T(8,128)(2,1)S(1)}, u32[]{:S(2)}, u32[]{:S(2)}) collective-permute-start(bf16[64,1280]{1,0:T(8,128)(2,1)S(1)} %add_convert_fusion), channel_id=1, source_target_pairs={{0,1},{1,0},{2,3},{3,2},{4,8},{5,9},{6,10},{7,11},{8,4},{9,5},{10,... | collective-permute-start | bytes 491528 | tf_op jit(solution)/shard_map/ppermute | solution.py:22
  40.7 2.2 %collective-permute-done.13.across = bf16[64,1280]{1,0:T(8,128)(2,1)S(1)} collective-permute-done((bf16[64,1280]{1,0:T(8,128)(2,1)S(1)}, bf16[64,1280]{1,0:T(8,128)(2,1)S(1)}, u32[]{:S(2)}, u32[]{:S(2)}) %collective-permute-start.13) | collective-permute-done | bytes 163872 | tf_op jit(solution)/shard_map/ppermute | solution.py:22
  43.0 6.1 %collective-permute-done.15.even_x = bf16[64,1280]{1,0:T(8,128)(2,1)S(1)} collective-permute-done((bf16[64,1280]{1,0:T(8,128)(2,1)S(1)}, bf16[64,1280]{1,0:T(8,128)(2,1)S(1)}, u32[]{:S(2)}, u32[]{:S(2)}) %collective-permute-start.15) | collective-permute-done | bytes 163872 | tf_op jit(solution)/shard_map/ppermute | solution.py:22
  49.1 1.0 %final.1 = f32[64,1792]{1,0:T(8,128)} custom-call(f32[64,1280]{1,0:T(8,128)S(1)} %get-tuple-element.17.own, bf16[64,1280]{1,0:T(8,128)(2,1)S(1)} %collective-permute-done.13.across, bf16[64,1280]{1,0:T(8,128)(2,1)S(1)} %collective-permute-done.14.even, bf16[64,1280]{1,0:T(8,128)(2,1)S(1)} %collective-permute-done.15.even_x, ...), custom_call_target="tpu_custom_call" | custom-call | tf_op jit(solution)/shard_map/final/pallas_call | solution.py:295
  (30 shorter events, 0.1 us)
Async XLA Ops:
  0.0 13.5 %collective-permute-start.8 = (bf16[2,3,128,128]{3,2,1,0:T(8,128)(2,1)}, bf16[2,3,128,128]{3,2,1,0:T(8,128)(2,1)S(1)}, u32[]{:S(2)}, u32[]{:S(2)}) collective-permute-start(bf16[2,3,128,128]{3,2,1,0:T(8,128)(2,1)} %refs_0_.1), channel_id=1, source_target_pairs={{0,4},{1,5},{2,6},{3,7},{4,0},{5,1},{6,2},{7,3},{8,12},{9,13},{10,... | collective-permute-start | bytes 589832 | tf_op jit(solution)/shard_map/ppermute | solution.py:22
  1.5 12.6 %collective-permute-start.5 = (bf16[2,3,128,128]{3,2,1,0:T(8,128)(2,1)}, bf16[2,3,128,128]{3,2,1,0:T(8,128)(2,1)S(1)}, u32[]{:S(2)}, u32[]{:S(2)}) collective-permute-start(bf16[2,3,128,128]{3,2,1,0:T(8,128)(2,1)} %refs_0_.1), channel_id=1, source_target_pairs={{0,1},{1,0},{2,3},{3,2},{4,8},{5,9},{6,10},{7,11},{8,4},{9,5},{10,... | collective-permute-start | bytes 589832 | tf_op jit(solution)/shard_map/ppermute | solution.py:22
  1.5 9.6 %collective-permute-start = (s32[2,3]{1,0:T(2,128)}, s32[2,3]{1,0:T(2,128)S(1)}, u32[]{:S(2)}, u32[]{:S(2)}) collective-permute-start(s32[2,3]{1,0:T(2,128)} %param.13), channel_id=1, source_target_pairs={{0,4},{1,5},{2,6},{3,7},{4,0},{5,1},{6,2},{7,3},{8,12},{9,13},{10,... | collective-permute-start | bytes 80 | tf_op jit(solution)/shard_map/ppermute | solution.py:22
  4.6 6.6 %collective-permute-start.1 = (s32[2,3]{1,0:T(2,128)}, s32[2,3]{1,0:T(2,128)S(1)}, u32[]{:S(2)}, u32[]{:S(2)}) collective-permute-start(s32[2,3]{1,0:T(2,128)} %param.13), channel_id=1, source_target_pairs={{0,1},{1,0},{2,3},{3,2},{4,8},{5,9},{6,10},{7,11},{8,4},{9,5},{10,... | collective-permute-start | bytes 80 | tf_op jit(solution)/shard_map/ppermute | solution.py:22
  4.6 14.6 %collective-permute-start.3 = (bf16[2,3,128,128]{3,2,1,0:T(8,128)(2,1)}, bf16[2,3,128,128]{3,2,1,0:T(8,128)(2,1)S(1)}, u32[]{:S(2)}, u32[]{:S(2)}) collective-permute-start(bf16[2,3,128,128]{3,2,1,0:T(8,128)(2,1)} %refs_0_.1), channel_id=1, source_target_pairs={{0,1},{1,0},{2,3},{3,2},{4,5},{5,4},{6,7},{7,6},{8,9},{9,8},{10,11... | collective-permute-start | bytes 589832 | tf_op jit(solution)/shard_map/ppermute | solution.py:22
  11.8 1.6 %collective-permute-start.2 = (s32[6,3]{1,0:T(8,128)S(1)}, s32[6,3]{1,0:T(8,128)S(1)}, u32[]{:S(2)}, u32[]{:S(2)}) collective-permute-start(s32[6,3]{1,0:T(8,128)S(1)} %pad_add_fusion), channel_id=1, source_target_pairs={{0,1},{1,0},{2,3},{3,2},{4,5},{5,4},{6,7},{7,6},{8,9},{9,8},{10,11... | collective-permute-start | bytes 224 | tf_op jit(solution)/shard_map/ppermute | solution.py:22
  11.9 8.2 %collective-permute-start.7 = (bf16[2,3,128,128]{3,2,1,0:T(8,128)(2,1)}, bf16[2,3,128,128]{3,2,1,0:T(8,128)(2,1)S(1)}, u32[]{:S(2)}, u32[]{:S(2)}) collective-permute-start(bf16[2,3,128,128]{3,2,1,0:T(8,128)(2,1)} %refs_0_.1), channel_id=1, source_target_pairs={{0,3},{1,2},{2,1},{3,0},{4,7},{5,6},{6,5},{7,4},{8,11},{9,10},{10,... | collective-permute-start | bytes 589832 | tf_op jit(solution)/shard_map/ppermute | solution.py:22
  13.5 3.8 %collective-permute-start.4 = (s32[6,3]{1,0:T(8,128)S(1)}, s32[6,3]{1,0:T(8,128)S(1)}, u32[]{:S(2)}, u32[]{:S(2)}) collective-permute-start(s32[6,3]{1,0:T(8,128)S(1)} %pad_add_fusion), channel_id=1, source_target_pairs={{0,8},{1,2},{2,1},{3,11},{4,12},{5,6},{6,5},{7,15},{8,0},{9,10},{1... | collective-permute-start | bytes 224 | tf_op jit(solution)/shard_map/ppermute | solution.py:22
  13.5 6.6 %collective-permute-start.10 = (bf16[2,3,128,128]{3,2,1,0:T(8,128)(2,1)S(1)}, bf16[2,3,128,128]{3,2,1,0:T(8,128)(2,1)S(1)}, u32[]{:S(2)}, u32[]{:S(2)}) collective-permute-start(bf16[2,3,128,128]{3,2,1,0:T(8,128)(2,1)S(1)} %collective-permute-done.8.refs_3_), channel_id=1, source_target_pairs={{0,0},{1,2},{2,1},{3,3},{4,4},{5,6},{6,5},{7,7},{8,8},{9,10},{10,9... | collective-permute-start | bytes 589832 | tf_op jit(solution)/shard_map/ppermute | solution.py:22
  14.2 5.9 %collective-permute-start.11 = (bf16[2,3,128,128]{3,2,1,0:T(8,128)(2,1)S(1)}, bf16[2,3,128,128]{3,2,1,0:T(8,128)(2,1)S(1)}, u32[]{:S(2)}, u32[]{:S(2)}) collective-permute-start(bf16[2,3,128,128]{3,2,1,0:T(8,128)(2,1)S(1)} %collective-permute-done.5.refs_6_), channel_id=1, source_target_pairs={{0,1},{1,0},{2,3},{3,2},{4,5},{5,4},{6,7},{7,6},{8,9},{9,8},{10,11... | collective-permute-start | bytes 589832 | tf_op jit(solution)/shard_map/ppermute | solution.py:22
  17.3 3.0 %collective-permute-start.9 = (bf16[2,3,128,128]{3,2,1,0:T(8,128)(2,1)S(1)}, bf16[2,3,128,128]{3,2,1,0:T(8,128)(2,1)S(1)}, u32[]{:S(2)}, u32[]{:S(2)}) collective-permute-start(bf16[2,3,128,128]{3,2,1,0:T(8,128)(2,1)S(1)} %collective-permute-done.8.refs_3_), channel_id=1, source_target_pairs={{0,1},{1,0},{2,3},{3,2},{4,5},{5,4},{6,7},{7,6},{8,9},{9,8},{10,11... | collective-permute-start | bytes 589832 | tf_op jit(solution)/shard_map/ppermute | solution.py:22
  19.2 7.8 %collective-permute-start.6 = (bf16[2,3,128,128]{3,2,1,0:T(8,128)(2,1)S(1)}, bf16[2,3,128,128]{3,2,1,0:T(8,128)(2,1)S(1)}, u32[]{:S(2)}, u32[]{:S(2)}) collective-permute-start(bf16[2,3,128,128]{3,2,1,0:T(8,128)(2,1)S(1)} %collective-permute-done.5.refs_6_), channel_id=1, source_target_pairs={{0,8},{1,2},{2,1},{3,11},{4,12},{5,6},{6,5},{7,15},{8,0},{9,10},{1... | collective-permute-start | bytes 589832 | tf_op jit(solution)/shard_map/ppermute | solution.py:22
  20.3 1.0 %copy-start = (bf16[2,7,128,128]{3,2,1,0:T(8,128)(2,1)S(1)}, bf16[2,7,128,128]{3,2,1,0:T(8,128)(2,1)}, u32[]{:S(2)}) copy-start(bf16[2,7,128,128]{3,2,1,0:T(8,128)(2,1)} %a_tiles.1) | copy-start | bytes 1376260
  21.3 0.9 %copy-start.1 = (bf16[2,3,128,128]{3,2,1,0:T(8,128)(2,1)S(1)}, bf16[2,3,128,128]{3,2,1,0:T(8,128)(2,1)}, u32[]{:S(2)}) copy-start(bf16[2,3,128,128]{3,2,1,0:T(8,128)(2,1)} %refs_0_.1) | copy-start | bytes 589828
  22.2 0.9 %copy-start.3 = (bf16[4,128,128]{2,1,0:T(8,128)(2,1)S(1)}, bf16[4,128,128]{2,1,0:T(8,128)(2,1)}, u32[]{:S(2)}) copy-start(bf16[4,128,128]{2,1,0:T(8,128)(2,1)} %over_tiles.1) | copy-start | bytes 393220
  23.1 0.7 %copy-start.4 = (s32[2,7]{1,0:T(2,128)S(1)}, s32[2,7]{1,0:T(2,128)}, u32[]{:S(2)}) copy-start(s32[2,7]{1,0:T(2,128)} %a_cols.3) | copy-start | bytes 172
  23.8 0.7 %copy-start.5 = (s32[4]{0:T(128)S(1)}, s32[4]{0:T(128)}, u32[]{:S(2)}) copy-start(s32[4]{0:T(128)} %over_rows.3) | copy-start | bytes 52
  24.5 0.7 %copy-start.6 = (s32[4]{0:T(128)S(1)}, s32[4]{0:T(128)}, u32[]{:S(2)}) copy-start(s32[4]{0:T(128)} %over_cols.3) | copy-start | bytes 52
  27.0 2.8 %copy-start.7 = (s32[2,3]{1,0:T(2,128)S(1)}, s32[2,3]{1,0:T(2,128)}, u32[]{:S(2)}) copy-start(s32[2,3]{1,0:T(2,128)} %param.13) | copy-start | bytes 76
  27.0 2.8 %copy-start.2 = (bf16[2,3,128,128]{3,2,1,0:T(8,128)(2,1)S(1)}, bf16[2,3,128,128]{3,2,1,0:T(8,128)(2,1)}, u32[]{:S(2)}) copy-start(bf16[2,3,128,128]{3,2,1,0:T(8,128)(2,1)} %refs_0_.1) | copy-start | bytes 589828
  27.8 3.7 %collective-permute-start.12 = (bf16[256,1280]{1,0:T(8,128)(2,1)S(1)}, bf16[256,1280]{1,0:T(8,128)(2,1)S(1)}, u32[]{:S(2)}, u32[]{:S(2)}) collective-permute-start(bf16[256,1280]{1,0:T(8,128)(2,1)S(1)} %get-tuple-element.16.own), channel_id=1, source_target_pairs={{0,1},{1,0},{2,3},{3,2},{4,5},{5,4},{6,7},{7,6},{8,9},{9,8},{10,11... | collective-permute-start | bytes 1966088 | tf_op jit(solution)/shard_map/ppermute | solution.py:22
  32.2 7.2 %collective-permute-start.16 = (bf16[64,1280]{1,0:T(8,128)(2,1)S(1)}, bf16[64,1280]{1,0:T(8,128)(2,1)S(1)}, u32[]{:S(2)}, u32[]{:S(2)}) collective-permute-start(bf16[64,1280]{1,0:T(8,128)(2,1)S(1)} %get-tuple-element.22), channel_id=1, source_target_pairs={{0,2},{1,3},{2,0},{3,1},{4,6},{5,7},{6,4},{7,5},{8,10},{9,11},{10,... | collective-permute-start | bytes 491528 | tf_op jit(solution)/shard_map/ppermute | solution.py:22
  34.4 8.6 %collective-permute-start.13 = (bf16[64,1280]{1,0:T(8,128)(2,1)S(1)}, bf16[64,1280]{1,0:T(8,128)(2,1)S(1)}, u32[]{:S(2)}, u32[]{:S(2)}) collective-permute-start(bf16[64,1280]{1,0:T(8,128)(2,1)S(1)} %get-tuple-element.18), channel_id=1, source_target_pairs={{0,2},{1,3},{2,0},{3,1},{4,6},{5,7},{6,4},{7,5},{8,10},{9,11},{10,... | collective-permute-start | bytes 491528 | tf_op jit(solution)/shard_map/ppermute | solution.py:22
  34.5 8.5 %collective-permute-start.14 = (bf16[64,1280]{1,0:T(8,128)(2,1)S(1)}, bf16[64,1280]{1,0:T(8,128)(2,1)S(1)}, u32[]{:S(2)}, u32[]{:S(2)}) collective-permute-start(bf16[64,1280]{1,0:T(8,128)(2,1)S(1)} %get-tuple-element.19), channel_id=1, source_target_pairs={{0,4},{1,5},{2,6},{3,7},{4,0},{5,1},{6,2},{7,3},{8,12},{9,13},{10,... | collective-permute-start | bytes 491528 | tf_op jit(solution)/shard_map/ppermute | solution.py:22
  35.8 13.3 %collective-permute-start.15 = (bf16[64,1280]{1,0:T(8,128)(2,1)S(1)}, bf16[64,1280]{1,0:T(8,128)(2,1)S(1)}, u32[]{:S(2)}, u32[]{:S(2)}) collective-permute-start(bf16[64,1280]{1,0:T(8,128)(2,1)S(1)} %get-tuple-element.20), channel_id=1, source_target_pairs={{0,6},{1,7},{2,4},{3,5},{4,2},{5,3},{6,0},{7,1},{8,14},{9,15},{10,... | collective-permute-start | bytes 491528 | tf_op jit(solution)/shard_map/ppermute | solution.py:22
  39.5 9.6 %collective-permute-start.17 = (bf16[64,1280]{1,0:T(8,128)(2,1)S(1)}, bf16[64,1280]{1,0:T(8,128)(2,1)S(1)}, u32[]{:S(2)}, u32[]{:S(2)}) collective-permute-start(bf16[64,1280]{1,0:T(8,128)(2,1)S(1)} %add_convert_fusion), channel_id=1, source_target_pairs={{0,1},{1,0},{2,3},{3,2},{4,8},{5,9},{6,10},{7,11},{8,4},{9,5},{10,... | collective-permute-start | bytes 491528 | tf_op jit(solution)/shard_map/ppermute | solution.py:22

commit v6 on v4

--- a/solution.py
+++ b/solution.py
@@ -40,6 +40,9 @@
         "odd": odd,
         "pair": lambda s, c: (s, c ^ 1),
         "across": across,
+        "across_self": lambda s, c: (s, across(s, c)[1]),
+        "across_y": lambda s, c: across(s, c) if across(s, c)[0] == s else (s ^ 1, c),
+        "across_x": lambda s, c: across(s, c) if across(s, c)[0] == s else (s, parts - 1 - c),
         "other": lambda s, c: (s, c ^ 2),
     }
 
@@ -152,7 +155,7 @@
 
 
 def last_kernel(slabs, parts, a_cols, over_rows, over_cols, source, a_tiles, over_tiles,
-                acc_in, out_in, acc, out, ext, cols_v, cols_s, sem):
+                acc_in, out_in, acc, out, ext, cols_s):
     blocks, taps, tile = a_tiles.shape[0], a_tiles.shape[1], a_tiles.shape[-1]
     kp = ext.shape[-1] // tile
     place = Place(slabs, parts, blocks)
@@ -160,9 +163,13 @@
 
     @pl.when(place.valid[LAST])
     def _():
-        copy = columns_of([(0, source)], cols_v, cols_s, sem)
         fetch(source, 0, None, ext)
-        copy.wait()
+        lane = lax.broadcasted_iota(jnp.int32, (1, tile), 1)
+        lines = [source[n, source.shape[1] - PAD :].astype(jnp.float32)[:1] for n in range(blocks)]
+        for n in range(blocks):
+            for m in range(kp):
+                value = jnp.sum(jnp.where(lane == m, lines[n], 0.0))
+                cols_s[n, m] = value.astype(jnp.int32)
 
         def visit(n, col, matrix):
             row = col - first
@@ -249,7 +256,7 @@
     own = pack(p_tiles, p_cols)
     even = send(own, "even")
     mate = send(own, "pair")
-    own_x = send(own, "across")
+    own_x = send(own, "across_x")
     left = pl.pallas_call(
         functools.partial(prepare_kernel, kp),
         out_shape=jax.ShapeDtypeStruct((3 * CB, half, 2 * span), jnp.bfloat16),
@@ -261,7 +268,7 @@
         name="prepare",
     )(own, mate)
     odd = send(own, "odd")
-    even_x = send(even, "across")
+    even_x = send(even, "across_self")
     even_p = send(even, "pair")
     odd_x = send(odd, "across")
     odd_p = send(odd, "pair")
@@ -285,7 +292,7 @@
         in_specs=smem(3) + vmem(5),
         out_specs=vmem(2),
         scratch_shapes=[pltpu.VMEM((blocks, tile, kp * tile), jnp.bfloat16)]
-        + column_scratch(1),
+        + [pltpu.SMEM((blocks, kp), jnp.int32)],
         input_output_aliases={6: 0, 7: 1},
         compiler_params=grant(4),
         cost_estimate=cost(1 << 30, 1 << 24),

time: 46.7 us -> 48.2 us (1.032)
  starting transfers between devices: 13.6 us -> 16.6 us
  waiting for transfers between devices: 21.4 us -> 19.9 us
    ppermute x14, starting transfers between devices: 13.6 us -> 16.6 us  [exchange(): return lax.ppermute(value, AXES, pairs)]
    ppermute x14, waiting for transfers between devices: 21.4 us -> 19.9 us  [exchange(): return lax.ppermute(value, AXES, pairs)]
  transfers between devices with their start and end apart: 14 -> 14, of which waited for: 6 -> 7; matrix products, arithmetic and copies ran while one was open for 0% -> 0% of each run, Pallas kernels for 8% -> 8%
where the time goes in v6:
time: 48.2 us; the launch traced here: 47.9 us
  waiting for transfers between devices  19.9 us (41%)
  starting transfers between devices  16.6 us (34%)
  Pallas kernels  5.8 us (12%)
  local copies, waits for them, and re-layouts  3.93 us (8%)
  other arithmetic  1.65 us (3%)
    ppermute x14, waiting for transfers between devices, exchange(): return lax.ppermute(value, AXES, pairs)  19.9 us
    ppermute x14, starting transfers between devices, exchange(): return lax.ppermute(value, AXES, pairs)  16.6 us
    unnamed x10, local copies, waits for them, and re-layouts  3.91 us
    pallas_call x1, Pallas kernels, fast_body(): pl.pallas_call(functools.partial(product_kernel, slabs, parts), out_shape...  2.33 us
    pallas_call x1, Pallas kernels, fast_body(): pl.pallas_call(functools.partial(prepare_kernel, kp), out_shape=jax.Shape...  1.26 us
  transfers between devices with their start and end apart: 14, of which 7 were waited for; matrix products, arithmetic and copies ran while one was open for 0% of the time, Pallas kernels for 8%

profile of v6, /device:TPU:8, one launch (start us, length us, event | category | flops | bytes accessed | tf_op | source)
XLA Modules:
  0.0 47.9 jit_solution(8886305865107843907)
XLA Ops:
  0.0 0.7 %convert.4 = bf16[2,3]{1,0:T(2,128)(2,1)S(1)} convert(s32[2,3]{1,0:T(2,128)} %param.13) | non-fusion elementwise | flops 6 | bytes 36 | tf_op jit(solution)/shard_map/convert
  0.7 0.9 %pad_maximum_fusion.own.refs_0_ = bf16[2,400,128]{2,1,0:T(8,128)(2,1)S(1)} fusion(bf16[2,16,128]{2,1,0:T(8,128)(2,1)S(1)} %broadcast_in_dim.2, bf16[2,384,128]{2,1,0:T(8,128)(2,1)} %bitcast.1), kind=kLoop, calls=%fused_computation.1 | loop fusion | flops 409600 | bytes 409600 | tf_op jit(solution)/shard_map/concatenate | solution.py:54
  1.6 1.6 %collective-permute-start.4 = (bf16[2,400,128]{2,1,0:T(8,128)(2,1)S(1)}, bf16[2,400,128]{2,1,0:T(8,128)(2,1)S(1)}, u32[]{:S(2)}, u32[]{:S(2)}) collective-permute-start(bf16[2,400,128]{2,1,0:T(8,128)(2,1)S(1)} %pad_maximum_fusion.own.refs_0_), channel_id=1, source_target_pairs={{0,4},{1,5},{2,6},{3,7},{4,0},{5,1},{6,2},{7,3},{8,12},{9,13},{10,... | collective-permute-start | bytes 614408 | tf_op jit(solution)/shard_map/ppermute | solution.py:23
  3.2 0.8 %collective-permute-start.3 = (bf16[2,400,128]{2,1,0:T(8,128)(2,1)S(1)}, bf16[2,400,128]{2,1,0:T(8,128)(2,1)S(1)}, u32[]{:S(2)}, u32[]{:S(2)}) collective-permute-start(bf16[2,400,128]{2,1,0:T(8,128)(2,1)S(1)} %pad_maximum_fusion.own.refs_0_), channel_id=1, source_target_pairs={{0,3},{1,2},{2,1},{3,0},{4,7},{5,6},{6,5},{7,4},{8,11},{9,10},{10,... | collective-permute-start | bytes 614408 | tf_op jit(solution)/shard_map/ppermute | solution.py:23
  4.0 1.2 %collective-permute-start = (bf16[2,400,128]{2,1,0:T(8,128)(2,1)S(1)}, bf16[2,400,128]{2,1,0:T(8,128)(2,1)S(1)}, u32[]{:S(2)}, u32[]{:S(2)}) collective-permute-start(bf16[2,400,128]{2,1,0:T(8,128)(2,1)S(1)} %pad_maximum_fusion.own.refs_0_), channel_id=1, source_target_pairs={{0,1},{1,0},{2,3},{3,2},{4,5},{5,4},{6,7},{7,6},{8,9},{9,8},{10,11... | collective-permute-start | bytes 614408 | tf_op jit(solution)/shard_map/ppermute | solution.py:23
  5.2 7.7 %collective-permute-done.4.refs_3_ = bf16[2,400,128]{2,1,0:T(8,128)(2,1)S(1)} collective-permute-done((bf16[2,400,128]{2,1,0:T(8,128)(2,1)S(1)}, bf16[2,400,128]{2,1,0:T(8,128)(2,1)S(1)}, u32[]{:S(2)}, u32[]{:S(2)}) %collective-permute-start.4) | collective-permute-done | bytes 204832 | tf_op jit(solution)/shard_map/ppermute | solution.py:23
  12.9 0.7 %collective-permute-start.6 = (bf16[2,400,128]{2,1,0:T(8,128)(2,1)S(1)}, bf16[2,400,128]{2,1,0:T(8,128)(2,1)S(1)}, u32[]{:S(2)}, u32[]{:S(2)}) collective-permute-start(bf16[2,400,128]{2,1,0:T(8,128)(2,1)S(1)} %collective-permute-done.4.refs_3_), channel_id=1, source_target_pairs={{0,0},{1,2},{2,1},{3,3},{4,4},{5,6},{6,5},{7,7},{8,8},{9,10},{10,9... | collective-permute-start | bytes 614408 | tf_op jit(solution)/shard_map/ppermute | solution.py:23
  13.6 2.9 %collective-permute-start.5 = (bf16[2,400,128]{2,1,0:T(8,128)(2,1)S(1)}, bf16[2,400,128]{2,1,0:T(8,128)(2,1)S(1)}, u32[]{:S(2)}, u32[]{:S(2)}) collective-permute-start(bf16[2,400,128]{2,1,0:T(8,128)(2,1)S(1)} %collective-permute-done.4.refs_3_), channel_id=1, source_target_pairs={{0,1},{1,0},{2,3},{3,2},{4,5},{5,4},{6,7},{7,6},{8,9},{9,8},{10,11... | collective-permute-start | bytes 614408 | tf_op jit(solution)/shard_map/ppermute | solution.py:23
  16.5 0.1 collective-permute-start.7
  16.6 0.0 collective-permute-done.3.refs_2_
  16.6 1.0 %collective-permute-done.5.refs_4_ = bf16[2,400,128]{2,1,0:T(8,128)(2,1)S(1)} collective-permute-done((bf16[2,400,128]{2,1,0:T(8,128)(2,1)S(1)}, bf16[2,400,128]{2,1,0:T(8,128)(2,1)S(1)}, u32[]{:S(2)}, u32[]{:S(2)}) %collective-permute-start.5) | collective-permute-done | bytes 204832 | tf_op jit(solution)/shard_map/ppermute | solution.py:23
  17.6 0.4 collective-permute-done.7.refs_7_
  18.0 1.0 %copy-done = bf16[2,7,128,128]{3,2,1,0:T(8,128)(2,1)S(1)} copy-done((bf16[2,7,128,128]{3,2,1,0:T(8,128)(2,1)S(1)}, bf16[2,7,128,128]{3,2,1,0:T(8,128)(2,1)}, u32[]{:S(2)}) %copy-start) | copy-done | bytes 458776
  19.0 0.9 %copy-done.1 = bf16[4,128,128]{2,1,0:T(8,128)(2,1)S(1)} copy-done((bf16[4,128,128]{2,1,0:T(8,128)(2,1)S(1)}, bf16[4,128,128]{2,1,0:T(8,128)(2,1)}, u32[]{:S(2)}) %copy-start.1) | copy-done | bytes 131096
  19.9 0.7 %copy-done.2 = s32[2,7]{1,0:T(2,128)S(1)} copy-done((s32[2,7]{1,0:T(2,128)S(1)}, s32[2,7]{1,0:T(2,128)}, u32[]{:S(2)}) %copy-start.2) | copy-done | bytes 80
  20.6 0.7 %copy-done.3 = s32[4]{0:T(128)S(1)} copy-done((s32[4]{0:T(128)S(1)}, s32[4]{0:T(128)}, u32[]{:S(2)}) %copy-start.3) | copy-done | bytes 40
  21.2 0.7 %copy-done.4 = s32[4]{0:T(128)S(1)} copy-done((s32[4]{0:T(128)S(1)}, s32[4]{0:T(128)}, u32[]{:S(2)}) %copy-start.4) | copy-done | bytes 40
  21.9 2.3 %product.1 = (bf16[256,1280]{1,0:T(8,128)(2,1)S(1)}, f32[2,10,128,128]{3,2,1,0:T(8,128)S(1)}) custom-call(s32[2,7]{1,0:T(2,128)S(1)} %copy-done.2, s32[4]{0:T(128)S(1)} %copy-done.3, s32[4]{0:T(128)S(1)} %copy-done.4, bf16[2,400,128]{2,1,0:T(8,128)(2,1)S(1)} %pad_maximum_fusion.own.refs_0_, bf16[2,400,128]{2,1,0:T(8,128)(2,1)S(1)} %collective-permute-done.mate.refs_1_, ...), custom_call_target="tpu_custom_call" | custom-call | flops 1073741824 | bytes 16777216 | tf_op jit(solution)/shard_map/product/pallas_call | solution.py:278
  24.2 0.6 %last.1 = (f32[2,10,128,128]{3,2,1,0:T(8,128)S(1)}, bf16[256,1280]{1,0:T(8,128)(2,1)S(1)}) custom-call(s32[2,7]{1,0:T(2,128)S(1)} %copy-done.2, s32[4]{0:T(128)S(1)} %copy-done.3, s32[4]{0:T(128)S(1)} %copy-done.4, bf16[2,400,128]{2,1,0:T(8,128)(2,1)S(1)} %collective-permute-done.2.source, ...), custom_call_target="tpu_custom_call", output_to_operand_aliasing={{0}: (6, {}), {1}: (7, {})} | custom-call | flops 1073741824 | bytes 16777216 | tf_op jit(solution)/shard_map/last/pallas_call | solution.py:289
  24.8 2.6 %collective-permute-start.8 = (bf16[256,1280]{1,0:T(8,128)(2,1)S(1)}, bf16[256,1280]{1,0:T(8,128)(2,1)S(1)}, u32[]{:S(2)}, u32[]{:S(2)}) collective-permute-start(bf16[256,1280]{1,0:T(8,128)(2,1)S(1)} %get-tuple-element.16.own), channel_id=1, source_target_pairs={{0,1},{1,0},{2,3},{3,2},{4,5},{5,4},{6,7},{7,6},{8,9},{9,8},{10,11... | collective-permute-start | bytes 1966088 | tf_op jit(solution)/shard_map/ppermute | solution.py:23
  27.5 1.3 %prepare.1.left = bf16[6,64,512]{2,1,0:T(8,128)(2,1)S(1)} custom-call(bf16[2,400,128]{2,1,0:T(8,128)(2,1)S(1)} %pad_maximum_fusion.own.refs_0_, bf16[2,400,128]{2,1,0:T(8,128)(2,1)S(1)} %collective-permute-done.mate.refs_1_), custom_call_target="tpu_custom_call" | custom-call | flops 1073741824 | bytes 16777216 | tf_op jit(solution)/shard_map/prepare/pallas_call | solution.py:260
  28.7 0.5 collective-permute-done.8.mate
  29.2 0.7 %partial.1 = (bf16[64,1280]{1,0:T(8,128)(2,1)S(1)}, bf16[64,1280]{1,0:T(8,128)(2,1)S(1)}, bf16[64,1280]{1,0:T(8,128)(2,1)S(1)}, f32[64,1280]{1,0:T(8,128)S(1)}, ...) custom-call(bf16[6,64,512]{2,1,0:T(8,128)(2,1)S(1)} %prepare.1.left, bf16[256,1280]{1,0:T(8,128)(2,1)S(1)} %get-tuple-element.16.own, ...), custom_call_target="tpu_custom_call" | custom-call | flops 536870912 | bytes 4194304 | tf_op jit(solution)/shard_map/partial/pallas_call | solution.py:304
  29.9 2.4 %collective-permute-start.12 = (bf16[64,1280]{1,0:T(8,128)(2,1)S(1)}, bf16[64,1280]{1,0:T(8,128)(2,1)S(1)}, u32[]{:S(2)}, u32[]{:S(2)}) collective-permute-start(bf16[64,1280]{1,0:T(8,128)(2,1)S(1)} %get-tuple-element.22), channel_id=1, source_target_pairs={{0,2},{1,3},{2,0},{3,1},{4,6},{5,7},{6,4},{7,5},{8,10},{9,11},{10,... | collective-permute-start | bytes 491528 | tf_op jit(solution)/shard_map/ppermute | solution.py:23
  32.3 0.1 collective-permute-start.9
  32.4 1.3 %collective-permute-start.10 = (bf16[64,1280]{1,0:T(8,128)(2,1)S(1)}, bf16[64,1280]{1,0:T(8,128)(2,1)S(1)}, u32[]{:S(2)}, u32[]{:S(2)}) collective-permute-start(bf16[64,1280]{1,0:T(8,128)(2,1)S(1)} %get-tuple-element.19), channel_id=1, source_target_pairs={{0,4},{1,5},{2,6},{3,7},{4,0},{5,1},{6,2},{7,3},{8,12},{9,13},{10,... | collective-permute-start | bytes 491528 | tf_op jit(solution)/shard_map/ppermute | solution.py:23
  33.7 2.1 %collective-permute-start.11 = (bf16[64,1280]{1,0:T(8,128)(2,1)S(1)}, bf16[64,1280]{1,0:T(8,128)(2,1)S(1)}, u32[]{:S(2)}, u32[]{:S(2)}) collective-permute-start(bf16[64,1280]{1,0:T(8,128)(2,1)S(1)} %get-tuple-element.20), channel_id=1, source_target_pairs={{0,6},{1,7},{2,4},{3,5},{4,2},{5,3},{6,0},{7,1},{8,14},{9,15},{10,... | collective-permute-start | bytes 491528 | tf_op jit(solution)/shard_map/ppermute | solution.py:23
  35.8 1.6 %collective-permute-done.12 = bf16[64,1280]{1,0:T(8,128)(2,1)S(1)} collective-permute-done((bf16[64,1280]{1,0:T(8,128)(2,1)S(1)}, bf16[64,1280]{1,0:T(8,128)(2,1)S(1)}, u32[]{:S(2)}, u32[]{:S(2)}) %collective-permute-start.12) | collective-permute-done | bytes 163872 | tf_op jit(solution)/shard_map/ppermute | solution.py:23
  37.4 0.7 %collective-permute-start.13 = (bf16[64,1280]{1,0:T(8,128)(2,1)S(1)}, bf16[64,1280]{1,0:T(8,128)(2,1)S(1)}, u32[]{:S(2)}, u32[]{:S(2)}) collective-permute-start(bf16[64,1280]{1,0:T(8,128)(2,1)S(1)} %add_convert_fusion), channel_id=1, source_target_pairs={{0,1},{1,0},{2,3},{3,2},{4,8},{5,9},{6,10},{7,11},{8,4},{9,5},{10,... | collective-permute-start | bytes 491528 | tf_op jit(solution)/shard_map/ppermute | solution.py:23
  38.1 2.7 %collective-permute-done.9.across = bf16[64,1280]{1,0:T(8,128)(2,1)S(1)} collective-permute-done((bf16[64,1280]{1,0:T(8,128)(2,1)S(1)}, bf16[64,1280]{1,0:T(8,128)(2,1)S(1)}, u32[]{:S(2)}, u32[]{:S(2)}) %collective-permute-start.9) | collective-permute-done | bytes 163872 | tf_op jit(solution)/shard_map/ppermute | solution.py:23
  40.9 6.1 %collective-permute-done.11.even_x = bf16[64,1280]{1,0:T(8,128)(2,1)S(1)} collective-permute-done((bf16[64,1280]{1,0:T(8,128)(2,1)S(1)}, bf16[64,1280]{1,0:T(8,128)(2,1)S(1)}, u32[]{:S(2)}, u32[]{:S(2)}) %collective-permute-start.11) | collective-permute-done | bytes 163872 | tf_op jit(solution)/shard_map/ppermute | solution.py:23
  47.0 1.0 %final.1 = f32[64,1792]{1,0:T(8,128)} custom-call(f32[64,1280]{1,0:T(8,128)S(1)} %get-tuple-element.17.own, bf16[64,1280]{1,0:T(8,128)(2,1)S(1)} %collective-permute-done.9.across, bf16[64,1280]{1,0:T(8,128)(2,1)S(1)} %collective-permute-done.10.even, bf16[64,1280]{1,0:T(8,128)(2,1)S(1)} %collective-permute-done.11.even_x, ...), custom_call_target="tpu_custom_call" | custom-call | tf_op jit(solution)/shard_map/final/pallas_call | solution.py:318
  (16 shorter events, 0.1 us)
Async XLA Ops:
  1.6 11.3 %collective-permute-start.4 = (bf16[2,400,128]{2,1,0:T(8,128)(2,1)S(1)}, bf16[2,400,128]{2,1,0:T(8,128)(2,1)S(1)}, u32[]{:S(2)}, u32[]{:S(2)}) collective-permute-start(bf16[2,400,128]{2,1,0:T(8,128)(2,1)S(1)} %pad_maximum_fusion.own.refs_0_), channel_id=1, source_target_pairs={{0,4},{1,5},{2,6},{3,7},{4,0},{5,1},{6,2},{7,3},{8,12},{9,13},{10,... | collective-permute-start | bytes 614408 | tf_op jit(solution)/shard_map/ppermute | solution.py:23
  3.2 13.3 %collective-permute-start.1 = (bf16[2,400,128]{2,1,0:T(8,128)(2,1)S(1)}, bf16[2,400,128]{2,1,0:T(8,128)(2,1)S(1)}, u32[]{:S(2)}, u32[]{:S(2)}) collective-permute-start(bf16[2,400,128]{2,1,0:T(8,128)(2,1)S(1)} %pad_maximum_fusion.own.refs_0_), channel_id=1, source_target_pairs={{0,1},{1,0},{2,3},{3,2},{4,8},{5,9},{6,10},{7,11},{8,4},{9,5},{10,... | collective-permute-start | bytes 614408 | tf_op jit(solution)/shard_map/ppermute | solution.py:23
  3.2 13.4 %collective-permute-start.3 = (bf16[2,400,128]{2,1,0:T(8,128)(2,1)S(1)}, bf16[2,400,128]{2,1,0:T(8,128)(2,1)S(1)}, u32[]{:S(2)}, u32[]{:S(2)}) collective-permute-start(bf16[2,400,128]{2,1,0:T(8,128)(2,1)S(1)} %pad_maximum_fusion.own.refs_0_), channel_id=1, source_target_pairs={{0,3},{1,2},{2,1},{3,0},{4,7},{5,6},{6,5},{7,4},{8,11},{9,10},{10,... | collective-permute-start | bytes 614408 | tf_op jit(solution)/shard_map/ppermute | solution.py:23
  4.0 12.6 %collective-permute-start = (bf16[2,400,128]{2,1,0:T(8,128)(2,1)S(1)}, bf16[2,400,128]{2,1,0:T(8,128)(2,1)S(1)}, u32[]{:S(2)}, u32[]{:S(2)}) collective-permute-start(bf16[2,400,128]{2,1,0:T(8,128)(2,1)S(1)} %pad_maximum_fusion.own.refs_0_), channel_id=1, source_target_pairs={{0,1},{1,0},{2,3},{3,2},{4,5},{5,4},{6,7},{7,6},{8,9},{9,8},{10,11... | collective-permute-start | bytes 614408 | tf_op jit(solution)/shard_map/ppermute | solution.py:23
  12.9 3.7 %collective-permute-start.6 = (bf16[2,400,128]{2,1,0:T(8,128)(2,1)S(1)}, bf16[2,400,128]{2,1,0:T(8,128)(2,1)S(1)}, u32[]{:S(2)}, u32[]{:S(2)}) collective-permute-start(bf16[2,400,128]{2,1,0:T(8,128)(2,1)S(1)} %collective-permute-done.4.refs_3_), channel_id=1, source_target_pairs={{0,0},{1,2},{2,1},{3,3},{4,4},{5,6},{6,5},{7,7},{8,8},{9,10},{10,9... | collective-permute-start | bytes 614408 | tf_op jit(solution)/shard_map/ppermute | solution.py:23
  13.6 4.0 %collective-permute-start.5 = (bf16[2,400,128]{2,1,0:T(8,128)(2,1)S(1)}, bf16[2,400,128]{2,1,0:T(8,128)(2,1)S(1)}, u32[]{:S(2)}, u32[]{:S(2)}) collective-permute-start(bf16[2,400,128]{2,1,0:T(8,128)(2,1)S(1)} %collective-permute-done.4.refs_3_), channel_id=1, source_target_pairs={{0,1},{1,0},{2,3},{3,2},{4,5},{5,4},{6,7},{7,6},{8,9},{9,8},{10,11... | collective-permute-start | bytes 614408 | tf_op jit(solution)/shard_map/ppermute | solution.py:23
  16.5 1.5 %collective-permute-start.7 = (bf16[2,400,128]{2,1,0:T(8,128)(2,1)S(1)}, bf16[2,400,128]{2,1,0:T(8,128)(2,1)S(1)}, u32[]{:S(2)}, u32[]{:S(2)}) collective-permute-start(bf16[2,400,128]{2,1,0:T(8,128)(2,1)S(1)} %collective-permute-done.1.refs_6_), channel_id=1, source_target_pairs={{0,1},{1,0},{2,3},{3,2},{4,5},{5,4},{6,7},{7,6},{8,9},{9,8},{10,11... | collective-permute-start | bytes 614408 | tf_op jit(solution)/shard_map/ppermute | solution.py:23
  16.6 7.6 %collective-permute-start.2 = (bf16[2,400,128]{2,1,0:T(8,128)(2,1)S(1)}, bf16[2,400,128]{2,1,0:T(8,128)(2,1)S(1)}, u32[]{:S(2)}, u32[]{:S(2)}) collective-permute-start(bf16[2,400,128]{2,1,0:T(8,128)(2,1)S(1)} %collective-permute-done.1.refs_6_), channel_id=1, source_target_pairs={{0,8},{1,2},{2,1},{3,11},{4,12},{5,6},{6,5},{7,15},{8,0},{9,10},{1... | collective-permute-start | bytes 614408 | tf_op jit(solution)/shard_map/ppermute | solution.py:23
  17.9 1.0 %copy-start = (bf16[2,7,128,128]{3,2,1,0:T(8,128)(2,1)S(1)}, bf16[2,7,128,128]{3,2,1,0:T(8,128)(2,1)}, u32[]{:S(2)}) copy-start(bf16[2,7,128,128]{3,2,1,0:T(8,128)(2,1)} %a_tiles.1) | copy-start | bytes 1376260
  19.0 0.9 %copy-start.1 = (bf16[4,128,128]{2,1,0:T(8,128)(2,1)S(1)}, bf16[4,128,128]{2,1,0:T(8,128)(2,1)}, u32[]{:S(2)}) copy-start(bf16[4,128,128]{2,1,0:T(8,128)(2,1)} %over_tiles.1) | copy-start | bytes 393220
  19.9 0.7 %copy-start.2 = (s32[2,7]{1,0:T(2,128)S(1)}, s32[2,7]{1,0:T(2,128)}, u32[]{:S(2)}) copy-start(s32[2,7]{1,0:T(2,128)} %a_cols.3) | copy-start | bytes 172
  20.6 0.7 %copy-start.3 = (s32[4]{0:T(128)S(1)}, s32[4]{0:T(128)}, u32[]{:S(2)}) copy-start(s32[4]{0:T(128)} %over_rows.3) | copy-start | bytes 52
  21.2 0.7 %copy-start.4 = (s32[4]{0:T(128)S(1)}, s32[4]{0:T(128)}, u32[]{:S(2)}) copy-start(s32[4]{0:T(128)} %over_cols.3) | copy-start | bytes 52
  24.8 4.4 %collective-permute-start.8 = (bf16[256,1280]{1,0:T(8,128)(2,1)S(1)}, bf16[256,1280]{1,0:T(8,128)(2,1)S(1)}, u32[]{:S(2)}, u32[]{:S(2)}) collective-permute-start(bf16[256,1280]{1,0:T(8,128)(2,1)S(1)} %get-tuple-element.16.own), channel_id=1, source_target_pairs={{0,1},{1,0},{2,3},{3,2},{4,5},{5,4},{6,7},{7,6},{8,9},{9,8},{10,11... | collective-permute-start | bytes 1966088 | tf_op jit(solution)/shard_map/ppermute | solution.py:23
  29.9 7.5 %collective-permute-start.12 = (bf16[64,1280]{1,0:T(8,128)(2,1)S(1)}, bf16[64,1280]{1,0:T(8,128)(2,1)S(1)}, u32[]{:S(2)}, u32[]{:S(2)}) collective-permute-start(bf16[64,1280]{1,0:T(8,128)(2,1)S(1)} %get-tuple-element.22), channel_id=1, source_target_pairs={{0,2},{1,3},{2,0},{3,1},{4,6},{5,7},{6,4},{7,5},{8,10},{9,11},{10,... | collective-permute-start | bytes 491528 | tf_op jit(solution)/shard_map/ppermute | solution.py:23
  32.3 8.6 %collective-permute-start.9 = (bf16[64,1280]{1,0:T(8,128)(2,1)S(1)}, bf16[64,1280]{1,0:T(8,128)(2,1)S(1)}, u32[]{:S(2)}, u32[]{:S(2)}) collective-permute-start(bf16[64,1280]{1,0:T(8,128)(2,1)S(1)} %get-tuple-element.18), channel_id=1, source_target_pairs={{0,2},{1,3},{2,0},{3,1},{4,6},{5,7},{6,4},{7,5},{8,10},{9,11},{10,... | collective-permute-start | bytes 491528 | tf_op jit(solution)/shard_map/ppermute | solution.py:23
  32.4 8.5 %collective-permute-start.10 = (bf16[64,1280]{1,0:T(8,128)(2,1)S(1)}, bf16[64,1280]{1,0:T(8,128)(2,1)S(1)}, u32[]{:S(2)}, u32[]{:S(2)}) collective-permute-start(bf16[64,1280]{1,0:T(8,128)(2,1)S(1)} %get-tuple-element.19), channel_id=1, source_target_pairs={{0,4},{1,5},{2,6},{3,7},{4,0},{5,1},{6,2},{7,3},{8,12},{9,13},{10,... | collective-permute-start | bytes 491528 | tf_op jit(solution)/shard_map/ppermute | solution.py:23
  33.7 13.3 %collective-permute-start.11 = (bf16[64,1280]{1,0:T(8,128)(2,1)S(1)}, bf16[64,1280]{1,0:T(8,128)(2,1)S(1)}, u32[]{:S(2)}, u32[]{:S(2)}) collective-permute-start(bf16[64,1280]{1,0:T(8,128)(2,1)S(1)} %get-tuple-element.20), channel_id=1, source_target_pairs={{0,6},{1,7},{2,4},{3,5},{4,2},{5,3},{6,0},{7,1},{8,14},{9,15},{10,... | collective-permute-start | bytes 491528 | tf_op jit(solution)/shard_map/ppermute | solution.py:23
  37.4 9.6 %collective-permute-start.13 = (bf16[64,1280]{1,0:T(8,128)(2,1)S(1)}, bf16[64,1280]{1,0:T(8,128)(2,1)S(1)}, u32[]{:S(2)}, u32[]{:S(2)}) collective-permute-start(bf16[64,1280]{1,0:T(8,128)(2,1)S(1)} %add_convert_fusion), channel_id=1, source_target_pairs={{0,1},{1,0},{2,3},{3,2},{4,8},{5,9},{6,10},{7,11},{8,4},{9,5},{10,... | collective-permute-start | bytes 491528 | tf_op jit(solution)/shard_map/ppermute | solution.py:23

commit v7 on v6

--- a/solution.py
+++ b/solution.py
@@ -49,9 +49,11 @@
 
 def pack(p_tiles, p_cols):
     blocks, kp, tile = p_tiles.shape[0], p_tiles.shape[1], p_tiles.shape[-1]
+    tiles = jnp.pad(p_tiles.reshape(blocks, kp * tile, tile), ((0, 0), (0, PAD), (0, 0)))
+    tiles, p_cols = lax.optimization_barrier((tiles, p_cols))
     cols = jnp.pad(p_cols, ((0, 0), (0, tile - kp)))[:, None, :]
     cols = jnp.broadcast_to(cols, (blocks, PAD, tile)).astype(jnp.bfloat16)
-    return jnp.concatenate([p_tiles.reshape(blocks, kp * tile, tile), cols], axis=1)
+    return tiles.at[:, kp * tile :].set(cols)
 
 
 def columns_of(sources, cols_v, cols_s, sem):
@@ -192,12 +194,17 @@
             visit(over_rows[o], over_cols[o], over_tiles.at[o])
 
 
-def partial_kernel(left, own, mate, *outs):
+def own_part_kernel(left, own, total):
+    stack = left[...].reshape(total.shape[0], left.shape[2])
+    total[...] = jnp.dot(stack[:, : own.shape[0]], own[...], preferred_element_type=jnp.float32)
+
+
+def partial_kernel(left, share, mate, *outs):
     count, half = left.shape[0], left.shape[1]
-    rows = own.shape[0]
-    stack = left[...].reshape(count * half, 2 * rows)
-    total = jnp.dot(stack[:, :rows], own[...], preferred_element_type=jnp.float32)
-    total += jnp.dot(stack[:, rows:], mate[...], preferred_element_type=jnp.float32)
+    stack = left[...].reshape(count * half, left.shape[2])
+    total = share[...] + jnp.dot(
+        stack[:, mate.shape[0] :], mate[...], preferred_element_type=jnp.float32
+    )
     for i in range(count):
         outs[i][...] = total[i * half : (i + 1) * half].astype(outs[i].dtype)
 
@@ -299,6 +306,15 @@
         name="last",
     )(a_cols, over_rows, over_cols, sources[LAST], a_tiles, over_tiles, acc, product)
     product_mate = send(product, "pair")
+    share = pl.pallas_call(
+        own_part_kernel,
+        out_shape=jax.ShapeDtypeStruct((3 * CB * half, 5 * width), jnp.float32),
+        in_specs=vmem(2),
+        out_specs=vmem(1)[0],
+        compiler_params=grant(6),
+        cost_estimate=cost(1 << 28, 1 << 21),
+        name="own_part",
+    )(left, product)
 
     kinds = [jnp.bfloat16] * 3 + [jnp.float32, jnp.bfloat16, jnp.float32]
     x_odd, x_even, x_own, b_odd, b_even, b_own = pl.pallas_call(
@@ -309,7 +325,7 @@
         compiler_params=grant(8),
         cost_estimate=cost(1 << 29, 1 << 22),
         name="partial",
-    )(left, product, product_mate)
+    )(left, share, product_mate)
     g_odd = send(x_odd, "other")
     g_even_x = send(x_even, "even_other")
     g_even = send(b_even, "even")

time: 48.2 us -> 47.9 us (level)
  other arithmetic: 1.65 us -> 0.71 us
  local copies, waits for them, and re-layouts: 3.93 us -> 4.87 us
    concatenate x1 -> x0, other arithmetic: 0.94 us -> none  [pack(): jnp.concatenate([p_tiles.reshape(blocks, kp * tile, tile), cols], axis=1)]
    pad x0 -> x1, local copies, waits for them, and re-layouts: none -> 0.94 us  [pack(): jnp.pad(p_tiles.reshape(blocks, kp * tile, tile), ((0, 0), (0, PAD), (0,...]
  transfers between devices with their start and end apart: 14 -> 14, of which waited for: 7 -> 6; matrix products, arithmetic and copies ran while one was open for 0% -> 0% of each run, Pallas kernels for 8% -> 8%
where the time goes in v7:
time: 47.9 us; the launch traced here: 47.7 us
  waiting for transfers between devices  19.5 us (41%)
  starting transfers between devices  16.6 us (35%)
  Pallas kernels  5.98 us (12%)
  local copies, waits for them, and re-layouts  4.87 us (10%)
  other arithmetic  0.71 us (1%)
    ppermute x14, waiting for transfers between devices, exchange(): return lax.ppermute(value, AXES, pairs)  19.5 us
    ppermute x14, starting transfers between devices, exchange(): return lax.ppermute(value, AXES, pairs)  16.6 us
    unnamed x10, local copies, waits for them, and re-layouts  3.91 us
    pallas_call x1, Pallas kernels, fast_body(): pl.pallas_call(functools.partial(product_kernel, slabs, parts), out_shape...  2.33 us
    pallas_call x1, Pallas kernels, fast_body(): pl.pallas_call(functools.partial(prepare_kernel, kp), out_shape=jax.Shape...  1.26 us
  transfers between devices with their start and end apart: 14, of which 6 were waited for; matrix products, arithmetic and copies ran while one was open for 0% of the time, Pallas kernels for 8%

profile of v7, /device:TPU:8, one launch (start us, length us, event | category | flops | bytes accessed | tf_op | source)
XLA Modules:
  0.0 47.7 jit_solution(2966660920958025417)
XLA Ops:
  0.0 0.9 %pad.11 = bf16[2,400,128]{2,1,0:T(8,128)(2,1)S(1)} pad(bf16[2,384,128]{2,1,0:T(8,128)(2,1)} %bitcast.1, bf16[]{:T(256)} %constant.30.clone.1), padding=0_0x0_16x0_0 | pad | bytes 401410 | tf_op jit(solution)/shard_map/jit(_pad)/pad | solution.py:52
  0.9 0.7 %convert.4 = bf16[2,3]{1,0:T(2,128)(2,1)S(1)} convert(s32[2,3]{1,0:T(2,128)} %param.15) | non-fusion elementwise | flops 6 | bytes 36 | tf_op jit(solution)/shard_map/convert
  1.7 1.6 %collective-permute-start.4 = (bf16[2,400,128]{2,1,0:T(8,128)(2,1)S(1)}, bf16[2,400,128]{2,1,0:T(8,128)(2,1)S(1)}, u32[]{:S(2)}, u32[]{:S(2)}) collective-permute-start(bf16[2,400,128]{2,1,0:T(8,128)(2,1)S(1)} %broadcast_dynamic-update-slice_fusion.own.refs_0_), channel_id=1, source_target_pairs={{0,4},{1,5},{2,6},{3,7},{4,0},{5,1},{6,2},{7,3},{8,12},{9,13},{10,... | collective-permute-start | bytes 614408 | tf_op jit(solution)/shard_map/ppermute | solution.py:23
  3.2 0.8 %collective-permute-start.3 = (bf16[2,400,128]{2,1,0:T(8,128)(2,1)S(1)}, bf16[2,400,128]{2,1,0:T(8,128)(2,1)S(1)}, u32[]{:S(2)}, u32[]{:S(2)}) collective-permute-start(bf16[2,400,128]{2,1,0:T(8,128)(2,1)S(1)} %broadcast_dynamic-update-slice_fusion.own.refs_0_), channel_id=1, source_target_pairs={{0,3},{1,2},{2,1},{3,0},{4,7},{5,6},{6,5},{7,4},{8,11},{9,10},{10,... | collective-permute-start | bytes 614408 | tf_op jit(solution)/shard_map/ppermute | solution.py:23
  4.0 1.2 %collective-permute-start = (bf16[2,400,128]{2,1,0:T(8,128)(2,1)S(1)}, bf16[2,400,128]{2,1,0:T(8,128)(2,1)S(1)}, u32[]{:S(2)}, u32[]{:S(2)}) collective-permute-start(bf16[2,400,128]{2,1,0:T(8,128)(2,1)S(1)} %broadcast_dynamic-update-slice_fusion.own.refs_0_), channel_id=1, source_target_pairs={{0,1},{1,0},{2,3},{3,2},{4,5},{5,4},{6,7},{7,6},{8,9},{9,8},{10,11... | collective-permute-start | bytes 614408 | tf_op jit(solution)/shard_map/ppermute | solution.py:23
  5.2 7.7 %collective-permute-done.4.refs_3_ = bf16[2,400,128]{2,1,0:T(8,128)(2,1)S(1)} collective-permute-done((bf16[2,400,128]{2,1,0:T(8,128)(2,1)S(1)}, bf16[2,400,128]{2,1,0:T(8,128)(2,1)S(1)}, u32[]{:S(2)}, u32[]{:S(2)}) %collective-permute-start.4) | collective-permute-done | bytes 204832 | tf_op jit(solution)/shard_map/ppermute | solution.py:23
  12.9 0.7 %collective-permute-start.6 = (bf16[2,400,128]{2,1,0:T(8,128)(2,1)S(1)}, bf16[2,400,128]{2,1,0:T(8,128)(2,1)S(1)}, u32[]{:S(2)}, u32[]{:S(2)}) collective-permute-start(bf16[2,400,128]{2,1,0:T(8,128)(2,1)S(1)} %collective-permute-done.4.refs_3_), channel_id=1, source_target_pairs={{0,0},{1,2},{2,1},{3,3},{4,4},{5,6},{6,5},{7,7},{8,8},{9,10},{10,9... | collective-permute-start | bytes 614408 | tf_op jit(solution)/shard_map/ppermute | solution.py:23
  13.6 2.9 %collective-permute-start.5 = (bf16[2,400,128]{2,1,0:T(8,128)(2,1)S(1)}, bf16[2,400,128]{2,1,0:T(8,128)(2,1)S(1)}, u32[]{:S(2)}, u32[]{:S(2)}) collective-permute-start(bf16[2,400,128]{2,1,0:T(8,128)(2,1)S(1)} %collective-permute-done.4.refs_3_), channel_id=1, source_target_pairs={{0,1},{1,0},{2,3},{3,2},{4,5},{5,4},{6,7},{7,6},{8,9},{9,8},{10,11... | collective-permute-start | bytes 614408 | tf_op jit(solution)/shard_map/ppermute | solution.py:23
  16.5 0.1 collective-permute-start.7
  16.6 1.0 %collective-permute-done.5.refs_4_ = bf16[2,400,128]{2,1,0:T(8,128)(2,1)S(1)} collective-permute-done((bf16[2,400,128]{2,1,0:T(8,128)(2,1)S(1)}, bf16[2,400,128]{2,1,0:T(8,128)(2,1)S(1)}, u32[]{:S(2)}, u32[]{:S(2)}) %collective-permute-start.5) | collective-permute-done | bytes 204832 | tf_op jit(solution)/shard_map/ppermute | solution.py:23
  17.6 0.4 collective-permute-done.7.refs_7_
  18.0 1.0 %copy-done = bf16[2,7,128,128]{3,2,1,0:T(8,128)(2,1)S(1)} copy-done((bf16[2,7,128,128]{3,2,1,0:T(8,128)(2,1)S(1)}, bf16[2,7,128,128]{3,2,1,0:T(8,128)(2,1)}, u32[]{:S(2)}) %copy-start) | copy-done | bytes 458776
  19.0 0.9 %copy-done.1 = bf16[4,128,128]{2,1,0:T(8,128)(2,1)S(1)} copy-done((bf16[4,128,128]{2,1,0:T(8,128)(2,1)S(1)}, bf16[4,128,128]{2,1,0:T(8,128)(2,1)}, u32[]{:S(2)}) %copy-start.1) | copy-done | bytes 131096
  19.9 0.7 %copy-done.2 = s32[2,7]{1,0:T(2,128)S(1)} copy-done((s32[2,7]{1,0:T(2,128)S(1)}, s32[2,7]{1,0:T(2,128)}, u32[]{:S(2)}) %copy-start.2) | copy-done | bytes 80
  20.6 0.7 %copy-done.3 = s32[4]{0:T(128)S(1)} copy-done((s32[4]{0:T(128)S(1)}, s32[4]{0:T(128)}, u32[]{:S(2)}) %copy-start.3) | copy-done | bytes 40
  21.2 0.7 %copy-done.4 = s32[4]{0:T(128)S(1)} copy-done((s32[4]{0:T(128)S(1)}, s32[4]{0:T(128)}, u32[]{:S(2)}) %copy-start.4) | copy-done | bytes 40
  21.9 2.3 %product.1 = (bf16[256,1280]{1,0:T(8,128)(2,1)S(1)}, f32[2,10,128,128]{3,2,1,0:T(8,128)S(1)}) custom-call(s32[2,7]{1,0:T(2,128)S(1)} %copy-done.2, s32[4]{0:T(128)S(1)} %copy-done.3, s32[4]{0:T(128)S(1)} %copy-done.4, bf16[2,400,128]{2,1,0:T(8,128)(2,1)S(1)} %broadcast_dynamic-update-slice_fusion.own.refs_0_, ...), custom_call_target="tpu_custom_call" | custom-call | flops 1073741824 | bytes 16777216 | tf_op jit(solution)/shard_map/product/pallas_call | solution.py:285
  24.2 0.6 %last.1 = (f32[2,10,128,128]{3,2,1,0:T(8,128)S(1)}, bf16[256,1280]{1,0:T(8,128)(2,1)S(1)}) custom-call(s32[2,7]{1,0:T(2,128)S(1)} %copy-done.2, s32[4]{0:T(128)S(1)} %copy-done.3, s32[4]{0:T(128)S(1)} %copy-done.4, bf16[2,400,128]{2,1,0:T(8,128)(2,1)S(1)} %collective-permute-done.2.source, ...), custom_call_target="tpu_custom_call", output_to_operand_aliasing={{0}: (6, {}), {1}: (7, {})} | custom-call | flops 1073741824 | bytes 16777216 | tf_op jit(solution)/shard_map/last/pallas_call | solution.py:296
  24.8 2.6 %collective-permute-start.8 = (bf16[256,1280]{1,0:T(8,128)(2,1)S(1)}, bf16[256,1280]{1,0:T(8,128)(2,1)S(1)}, u32[]{:S(2)}, u32[]{:S(2)}) collective-permute-start(bf16[256,1280]{1,0:T(8,128)(2,1)S(1)} %get-tuple-element.32.own), channel_id=1, source_target_pairs={{0,1},{1,0},{2,3},{3,2},{4,5},{5,4},{6,7},{7,6},{8,9},{9,8},{10,11... | collective-permute-start | bytes 1966088 | tf_op jit(solution)/shard_map/ppermute | solution.py:23
  27.5 1.3 %prepare.1.left = bf16[6,64,512]{2,1,0:T(8,128)(2,1)S(1)} custom-call(bf16[2,400,128]{2,1,0:T(8,128)(2,1)S(1)} %broadcast_dynamic-update-slice_fusion.own.refs_0_, bf16[2,400,128]{2,1,0:T(8,128)(2,1)S(1)} %collective-permute-done.mate.refs_1_), custom_call_target="tpu_custom_call" | custom-call | flops 1073741824 | bytes 16777216 | tf_op jit(solution)/shard_map/prepare/pallas_call | solution.py:267
  28.7 0.4 own_part.1.share
  29.1 0.0 collective-permute-done.8.mate
  29.2 0.4 partial.1
  29.6 2.4 %collective-permute-start.12 = (bf16[64,1280]{1,0:T(8,128)(2,1)S(1)}, bf16[64,1280]{1,0:T(8,128)(2,1)S(1)}, u32[]{:S(2)}, u32[]{:S(2)}) collective-permute-start(bf16[64,1280]{1,0:T(8,128)(2,1)S(1)} %get-tuple-element.38), channel_id=1, source_target_pairs={{0,2},{1,3},{2,0},{3,1},{4,6},{5,7},{6,4},{7,5},{8,10},{9,11},{10,... | collective-permute-start | bytes 491528 | tf_op jit(solution)/shard_map/ppermute | solution.py:23
  32.1 0.1 collective-permute-start.9
  32.1 1.3 %collective-permute-start.10 = (bf16[64,1280]{1,0:T(8,128)(2,1)S(1)}, bf16[64,1280]{1,0:T(8,128)(2,1)S(1)}, u32[]{:S(2)}, u32[]{:S(2)}) collective-permute-start(bf16[64,1280]{1,0:T(8,128)(2,1)S(1)} %get-tuple-element.35), channel_id=1, source_target_pairs={{0,4},{1,5},{2,6},{3,7},{4,0},{5,1},{6,2},{7,3},{8,12},{9,13},{10,... | collective-permute-start | bytes 491528 | tf_op jit(solution)/shard_map/ppermute | solution.py:23
  33.5 2.1 %collective-permute-start.11 = (bf16[64,1280]{1,0:T(8,128)(2,1)S(1)}, bf16[64,1280]{1,0:T(8,128)(2,1)S(1)}, u32[]{:S(2)}, u32[]{:S(2)}) collective-permute-start(bf16[64,1280]{1,0:T(8,128)(2,1)S(1)} %get-tuple-element.36), channel_id=1, source_target_pairs={{0,6},{1,7},{2,4},{3,5},{4,2},{5,3},{6,0},{7,1},{8,14},{9,15},{10,... | collective-permute-start | bytes 491528 | tf_op jit(solution)/shard_map/ppermute | solution.py:23
  35.6 1.6 %collective-permute-done.12 = bf16[64,1280]{1,0:T(8,128)(2,1)S(1)} collective-permute-done((bf16[64,1280]{1,0:T(8,128)(2,1)S(1)}, bf16[64,1280]{1,0:T(8,128)(2,1)S(1)}, u32[]{:S(2)}, u32[]{:S(2)}) %collective-permute-start.12) | collective-permute-done | bytes 163872 | tf_op jit(solution)/shard_map/ppermute | solution.py:23
  37.1 0.7 %collective-permute-start.13 = (bf16[64,1280]{1,0:T(8,128)(2,1)S(1)}, bf16[64,1280]{1,0:T(8,128)(2,1)S(1)}, u32[]{:S(2)}, u32[]{:S(2)}) collective-permute-start(bf16[64,1280]{1,0:T(8,128)(2,1)S(1)} %add_convert_fusion), channel_id=1, source_target_pairs={{0,1},{1,0},{2,3},{3,2},{4,8},{5,9},{6,10},{7,11},{8,4},{9,5},{10,... | collective-permute-start | bytes 491528 | tf_op jit(solution)/shard_map/ppermute | solution.py:23
  37.9 2.7 %collective-permute-done.9.across = bf16[64,1280]{1,0:T(8,128)(2,1)S(1)} collective-permute-done((bf16[64,1280]{1,0:T(8,128)(2,1)S(1)}, bf16[64,1280]{1,0:T(8,128)(2,1)S(1)}, u32[]{:S(2)}, u32[]{:S(2)}) %collective-permute-start.9) | collective-permute-done | bytes 163872 | tf_op jit(solution)/shard_map/ppermute | solution.py:23
  40.6 6.1 %collective-permute-done.11.even_x = bf16[64,1280]{1,0:T(8,128)(2,1)S(1)} collective-permute-done((bf16[64,1280]{1,0:T(8,128)(2,1)S(1)}, bf16[64,1280]{1,0:T(8,128)(2,1)S(1)}, u32[]{:S(2)}, u32[]{:S(2)}) %collective-permute-start.11) | collective-permute-done | bytes 163872 | tf_op jit(solution)/shard_map/ppermute | solution.py:23
  46.7 1.0 %final.1 = f32[64,1792]{1,0:T(8,128)} custom-call(f32[64,1280]{1,0:T(8,128)S(1)} %get-tuple-element.33.own, bf16[64,1280]{1,0:T(8,128)(2,1)S(1)} %collective-permute-done.9.across, bf16[64,1280]{1,0:T(8,128)(2,1)S(1)} %collective-permute-done.10.even, bf16[64,1280]{1,0:T(8,128)(2,1)S(1)} %collective-permute-done.11.even_x, ...), custom_call_target="tpu_custom_call" | custom-call | tf_op jit(solution)/shard_map/final/pallas_call | solution.py:334
  (17 shorter events, 0.1 us)
Async XLA Ops:
  1.7 11.3 %collective-permute-start.4 = (bf16[2,400,128]{2,1,0:T(8,128)(2,1)S(1)}, bf16[2,400,128]{2,1,0:T(8,128)(2,1)S(1)}, u32[]{:S(2)}, u32[]{:S(2)}) collective-permute-start(bf16[2,400,128]{2,1,0:T(8,128)(2,1)S(1)} %broadcast_dynamic-update-slice_fusion.own.refs_0_), channel_id=1, source_target_pairs={{0,4},{1,5},{2,6},{3,7},{4,0},{5,1},{6,2},{7,3},{8,12},{9,13},{10,... | collective-permute-start | bytes 614408 | tf_op jit(solution)/shard_map/ppermute | solution.py:23
  3.2 13.3 %collective-permute-start.1 = (bf16[2,400,128]{2,1,0:T(8,128)(2,1)S(1)}, bf16[2,400,128]{2,1,0:T(8,128)(2,1)S(1)}, u32[]{:S(2)}, u32[]{:S(2)}) collective-permute-start(bf16[2,400,128]{2,1,0:T(8,128)(2,1)S(1)} %broadcast_dynamic-update-slice_fusion.own.refs_0_), channel_id=1, source_target_pairs={{0,1},{1,0},{2,3},{3,2},{4,8},{5,9},{6,10},{7,11},{8,4},{9,5},{10,... | collective-permute-start | bytes 614408 | tf_op jit(solution)/shard_map/ppermute | solution.py:23
  3.2 13.4 %collective-permute-start.3 = (bf16[2,400,128]{2,1,0:T(8,128)(2,1)S(1)}, bf16[2,400,128]{2,1,0:T(8,128)(2,1)S(1)}, u32[]{:S(2)}, u32[]{:S(2)}) collective-permute-start(bf16[2,400,128]{2,1,0:T(8,128)(2,1)S(1)} %broadcast_dynamic-update-slice_fusion.own.refs_0_), channel_id=1, source_target_pairs={{0,3},{1,2},{2,1},{3,0},{4,7},{5,6},{6,5},{7,4},{8,11},{9,10},{10,... | collective-permute-start | bytes 614408 | tf_op jit(solution)/shard_map/ppermute | solution.py:23
  4.0 12.6 %collective-permute-start = (bf16[2,400,128]{2,1,0:T(8,128)(2,1)S(1)}, bf16[2,400,128]{2,1,0:T(8,128)(2,1)S(1)}, u32[]{:S(2)}, u32[]{:S(2)}) collective-permute-start(bf16[2,400,128]{2,1,0:T(8,128)(2,1)S(1)} %broadcast_dynamic-update-slice_fusion.own.refs_0_), channel_id=1, source_target_pairs={{0,1},{1,0},{2,3},{3,2},{4,5},{5,4},{6,7},{7,6},{8,9},{9,8},{10,11... | collective-permute-start | bytes 614408 | tf_op jit(solution)/shard_map/ppermute | solution.py:23
  12.9 3.7 %collective-permute-start.6 = (bf16[2,400,128]{2,1,0:T(8,128)(2,1)S(1)}, bf16[2,400,128]{2,1,0:T(8,128)(2,1)S(1)}, u32[]{:S(2)}, u32[]{:S(2)}) collective-permute-start(bf16[2,400,128]{2,1,0:T(8,128)(2,1)S(1)} %collective-permute-done.4.refs_3_), channel_id=1, source_target_pairs={{0,0},{1,2},{2,1},{3,3},{4,4},{5,6},{6,5},{7,7},{8,8},{9,10},{10,9... | collective-permute-start | bytes 614408 | tf_op jit(solution)/shard_map/ppermute | solution.py:23
  13.6 4.0 %collective-permute-start.5 = (bf16[2,400,128]{2,1,0:T(8,128)(2,1)S(1)}, bf16[2,400,128]{2,1,0:T(8,128)(2,1)S(1)}, u32[]{:S(2)}, u32[]{:S(2)}) collective-permute-start(bf16[2,400,128]{2,1,0:T(8,128)(2,1)S(1)} %collective-permute-done.4.refs_3_), channel_id=1, source_target_pairs={{0,1},{1,0},{2,3},{3,2},{4,5},{5,4},{6,7},{7,6},{8,9},{9,8},{10,11... | collective-permute-start | bytes 614408 | tf_op jit(solution)/shard_map/ppermute | solution.py:23
  16.5 1.5 %collective-permute-start.7 = (bf16[2,400,128]{2,1,0:T(8,128)(2,1)S(1)}, bf16[2,400,128]{2,1,0:T(8,128)(2,1)S(1)}, u32[]{:S(2)}, u32[]{:S(2)}) collective-permute-start(bf16[2,400,128]{2,1,0:T(8,128)(2,1)S(1)} %collective-permute-done.1.refs_6_), channel_id=1, source_target_pairs={{0,1},{1,0},{2,3},{3,2},{4,5},{5,4},{6,7},{7,6},{8,9},{9,8},{10,11... | collective-permute-start | bytes 614408 | tf_op jit(solution)/shard_map/ppermute | solution.py:23
  16.6 7.6 %collective-permute-start.2 = (bf16[2,400,128]{2,1,0:T(8,128)(2,1)S(1)}, bf16[2,400,128]{2,1,0:T(8,128)(2,1)S(1)}, u32[]{:S(2)}, u32[]{:S(2)}) collective-permute-start(bf16[2,400,128]{2,1,0:T(8,128)(2,1)S(1)} %collective-permute-done.1.refs_6_), channel_id=1, source_target_pairs={{0,8},{1,2},{2,1},{3,11},{4,12},{5,6},{6,5},{7,15},{8,0},{9,10},{1... | collective-permute-start | bytes 614408 | tf_op jit(solution)/shard_map/ppermute | solution.py:23
  17.9 1.0 %copy-start = (bf16[2,7,128,128]{3,2,1,0:T(8,128)(2,1)S(1)}, bf16[2,7,128,128]{3,2,1,0:T(8,128)(2,1)}, u32[]{:S(2)}) copy-start(bf16[2,7,128,128]{3,2,1,0:T(8,128)(2,1)} %a_tiles.1) | copy-start | bytes 1376260
  19.0 0.9 %copy-start.1 = (bf16[4,128,128]{2,1,0:T(8,128)(2,1)S(1)}, bf16[4,128,128]{2,1,0:T(8,128)(2,1)}, u32[]{:S(2)}) copy-start(bf16[4,128,128]{2,1,0:T(8,128)(2,1)} %over_tiles.1) | copy-start | bytes 393220
  19.9 0.7 %copy-start.2 = (s32[2,7]{1,0:T(2,128)S(1)}, s32[2,7]{1,0:T(2,128)}, u32[]{:S(2)}) copy-start(s32[2,7]{1,0:T(2,128)} %a_cols.3) | copy-start | bytes 172
  20.6 0.7 %copy-start.3 = (s32[4]{0:T(128)S(1)}, s32[4]{0:T(128)}, u32[]{:S(2)}) copy-start(s32[4]{0:T(128)} %over_rows.3) | copy-start | bytes 52
  21.2 0.7 %copy-start.4 = (s32[4]{0:T(128)S(1)}, s32[4]{0:T(128)}, u32[]{:S(2)}) copy-start(s32[4]{0:T(128)} %over_cols.3) | copy-start | bytes 52
  24.8 4.4 %collective-permute-start.8 = (bf16[256,1280]{1,0:T(8,128)(2,1)S(1)}, bf16[256,1280]{1,0:T(8,128)(2,1)S(1)}, u32[]{:S(2)}, u32[]{:S(2)}) collective-permute-start(bf16[256,1280]{1,0:T(8,128)(2,1)S(1)} %get-tuple-element.32.own), channel_id=1, source_target_pairs={{0,1},{1,0},{2,3},{3,2},{4,5},{5,4},{6,7},{7,6},{8,9},{9,8},{10,11... | collective-permute-start | bytes 1966088 | tf_op jit(solution)/shard_map/ppermute | solution.py:23
  29.6 7.5 %collective-permute-start.12 = (bf16[64,1280]{1,0:T(8,128)(2,1)S(1)}, bf16[64,1280]{1,0:T(8,128)(2,1)S(1)}, u32[]{:S(2)}, u32[]{:S(2)}) collective-permute-start(bf16[64,1280]{1,0:T(8,128)(2,1)S(1)} %get-tuple-element.38), channel_id=1, source_target_pairs={{0,2},{1,3},{2,0},{3,1},{4,6},{5,7},{6,4},{7,5},{8,10},{9,11},{10,... | collective-permute-start | bytes 491528 | tf_op jit(solution)/shard_map/ppermute | solution.py:23
  32.1 8.6 %collective-permute-start.9 = (bf16[64,1280]{1,0:T(8,128)(2,1)S(1)}, bf16[64,1280]{1,0:T(8,128)(2,1)S(1)}, u32[]{:S(2)}, u32[]{:S(2)}) collective-permute-start(bf16[64,1280]{1,0:T(8,128)(2,1)S(1)} %get-tuple-element.34), channel_id=1, source_target_pairs={{0,2},{1,3},{2,0},{3,1},{4,6},{5,7},{6,4},{7,5},{8,10},{9,11},{10,... | collective-permute-start | bytes 491528 | tf_op jit(solution)/shard_map/ppermute | solution.py:23
  32.1 8.5 %collective-permute-start.10 = (bf16[64,1280]{1,0:T(8,128)(2,1)S(1)}, bf16[64,1280]{1,0:T(8,128)(2,1)S(1)}, u32[]{:S(2)}, u32[]{:S(2)}) collective-permute-start(bf16[64,1280]{1,0:T(8,128)(2,1)S(1)} %get-tuple-element.35), channel_id=1, source_target_pairs={{0,4},{1,5},{2,6},{3,7},{4,0},{5,1},{6,2},{7,3},{8,12},{9,13},{10,... | collective-permute-start | bytes 491528 | tf_op jit(solution)/shard_map/ppermute | solution.py:23
  33.5 13.3 %collective-permute-start.11 = (bf16[64,1280]{1,0:T(8,128)(2,1)S(1)}, bf16[64,1280]{1,0:T(8,128)(2,1)S(1)}, u32[]{:S(2)}, u32[]{:S(2)}) collective-permute-start(bf16[64,1280]{1,0:T(8,128)(2,1)S(1)} %get-tuple-element.36), channel_id=1, source_target_pairs={{0,6},{1,7},{2,4},{3,5},{4,2},{5,3},{6,0},{7,1},{8,14},{9,15},{10,... | collective-permute-start | bytes 491528 | tf_op jit(solution)/shard_map/ppermute | solution.py:23
  37.1 9.6 %collective-permute-start.13 = (bf16[64,1280]{1,0:T(8,128)(2,1)S(1)}, bf16[64,1280]{1,0:T(8,128)(2,1)S(1)}, u32[]{:S(2)}, u32[]{:S(2)}) collective-permute-start(bf16[64,1280]{1,0:T(8,128)(2,1)S(1)} %add_convert_fusion), channel_id=1, source_target_pairs={{0,1},{1,0},{2,3},{3,2},{4,8},{5,9},{6,10},{7,11},{8,4},{9,5},{10,... | collective-permute-start | bytes 491528 | tf_op jit(solution)/shard_map/ppermute | solution.py:23
